TPU v7x, 32 devices: a whole 2x2x4 slice. The times are simulated.
32 devices in a mesh: head: 4 (over y, x), seq: 8 (over z, core).
Axes of the slice: x: 2, y: 2, z: 4, core: 2. Of those that a mesh axis runs over, the one named last changes fastest.
Arguments:
- frames: bfloat16 [2, 8, 1024, 512], P(None, 'seq', 'head'), may hold values from -6 to 6
- cotangent: bfloat16 [2, 8, 1024, 512], P(None, 'seq', 'head'), may hold values from -6 to 6
- lengths: int32 [2, 8, 4], P(None, 'seq'), may hold values from 1 to 512, 1024 in all within a row
- gain_first: bfloat16 [512], P(('head', 'seq')), may hold values from 0.3984375 to 1.59375
- first_in: bfloat16 [512, 2048], P(('head', 'seq')), may hold values from -0.25 to 0.25
- first_out: bfloat16 [2048, 512], P(('head', 'seq')), may hold values from -0.125 to 0.125
- gain_attend: bfloat16 [512], P(('head', 'seq')), may hold values from 0.3984375 to 1.59375
- head_projection: bfloat16 [512, 1536], P(('head', 'seq')), may hold values from -0.25 to 0.25
- output_projection: bfloat16 [512, 512], P(('head', 'seq')), may hold values from -2 to 2
- gain_gated: bfloat16 [512], P(('head', 'seq')), may hold values from 0.3984375 to 1.59375
- gated_up: bfloat16 [512, 3072], P(('head', 'seq')), may hold values from -0.25 to 0.25
- gain_gate: bfloat16 [1536], P(('head', 'seq')), may hold values from 0.3984375 to 1.59375
- kernel_gate: bfloat16 [31, 1536], P(None, ('head', 'seq')), may hold values from -1 to 1
- gated_down: bfloat16 [1536, 512], P(('head', 'seq')), may hold values from -0.15625 to 0.15625
- kernel_merge: bfloat16 [31, 1024], P(None, ('head', 'seq')), may hold values from -1 to 1
- merge_weight: bfloat16 [1024, 512], P(('head', 'seq')), may hold values from -0.1875 to 0.1875
- gain_second: bfloat16 [512], P(('head', 'seq')), may hold values from 0.3984375 to 1.59375
- second_in: bfloat16 [512, 2048], P(('head', 'seq')), may hold values from -0.25 to 0.25
- second_out: bfloat16 [2048, 512], P(('head', 'seq')), may hold values from -0.125 to 0.125
- gain_final: bfloat16 [512], P(('head', 'seq')), may hold values from 0.3984375 to 1.59375
Outputs:
- output_frames: bfloat16 [2, 8, 1024, 512], P(None, 'seq', 'head')
- grad_frames: float32 [2, 8, 1024, 512], P(None, 'seq', 'head')
- grad_gain_first: float32 [512], P(('head', 'seq'))
- grad_first_in: float32 [512, 2048], P(('head', 'seq'))
- grad_first_out: float32 [2048, 512], P(('head', 'seq'))
- grad_gain_attend: float32 [512], P(('head', 'seq'))
- grad_head_projection: float32 [512, 1536], P(('head', 'seq'))
- grad_output_projection: float32 [512, 512], P(('head', 'seq'))
- grad_gain_gated: float32 [512], P(('head', 'seq'))
- grad_gated_up: float32 [512, 3072], P(('head', 'seq'))
- grad_gain_gate: float32 [1536], P(('head', 'seq'))
- grad_kernel_gate: float32 [31, 1536], P(None, ('head', 'seq'))
- grad_gated_down: float32 [1536, 512], P(('head', 'seq'))
- grad_kernel_merge: float32 [31, 1024], P(None, ('head', 'seq'))
- grad_merge_weight: float32 [1024, 512], P(('head', 'seq'))
- grad_gain_second: float32 [512], P(('head', 'seq'))
- grad_second_in: float32 [512, 2048], P(('head', 'seq'))
- grad_second_out: float32 [2048, 512], P(('head', 'seq'))
- grad_gain_final: float32 [512], P(('head', 'seq'))
Inputs may be any that keep to these rules, and one draw needn't show every extreme that they name: The 4 lengths of a stream sum to 1024, and every stream has one utterance of exactly 512 frames.
All inputs are finite; a program needn't handle non-finite values.
Results may differ from a plain program's by a relative error of at most 0.018.
Values may be sent and summed in bfloat16 or wider, within the bound.
No kernel may reach another device: no remote copies, remote signals or barrier semaphores. Data moves between devices by JAX's collectives and lax.ppermute only.
A program may use at most 120 MiB of HBM per device.

v0:
```python
import math

import jax
import jax.numpy as jnp
from jax import lax
from jax.sharding import PartitionSpec as P

D = 512
HD = 64
KER = 31


EPSILON = 1e-05


def extended(shard, sides, width):
    for axis, dim in sides:
        size, length = (lax.axis_size(axis), shard.shape[dim])
        up = [(i, (i + 1) % size) for i in range(size - 1)]
        down = [(j, i) for i, j in up]
        last = lax.slice_in_dim(shard, length - width, length, axis=dim)
        leading = lax.slice_in_dim(shard, 0, width, axis=dim)
        before = lax.ppermute(last, axis, up)
        after = lax.ppermute(leading, axis, down)
        shard = jnp.concatenate([before, shard, after], axis=dim)
    return shard


def layer_norm(values, gain_vector):
    centre = values - jnp.mean(values, axis=-1, keepdims=True)
    scaling = lax.rsqrt(jnp.mean(centre * centre, axis=-1, keepdims=True) + EPSILON)
    return centre * scaling * gain_vector


def exact_gelu(values):
    return jax.nn.gelu(values, approximate=False)


def segment_index(positions, lengths):
    boundary = jnp.cumsum(lengths)
    return jnp.sum((positions[:, None] >= boundary[None, :]).astype(jnp.int32), axis=1)


def rotary_tables(frame_count, head_width):
    half_width = head_width // 2
    frequency = jnp.exp(
        jnp.arange(half_width, dtype=jnp.float32) * (-math.log(10000.0) / half_width)
    )
    angles = jnp.arange(frame_count, dtype=jnp.float32)[:, None] * frequency[None, :]
    return (jnp.cos(angles), jnp.sin(angles))


def rotate(values, cos_table, sin_table, sign):
    half_width = values.shape[1] // 2
    first_half = values[:, :half_width]
    second_half = values[:, half_width:]
    return jnp.concatenate(
        [
            first_half * cos_table - sign * second_half * sin_table,
            sign * first_half * sin_table + second_half * cos_table,
        ],
        axis=1,
    )


def block_length(frame_count):
    return min(512, frame_count)


def product(left, right):
    return jnp.dot(left, right, preferred_element_type=jnp.float32)


def times_transposed(left, right):
    return lax.dot_general(
        left, right, (((1,), (1,)), ((), ())), preferred_element_type=jnp.float32
    )


def transposed_times(left, right):
    return lax.dot_general(
        left, right, (((0,), (0,)), ((), ())), preferred_element_type=jnp.float32
    )


def depthwise(padded, kernel, seg_pad, frame_count):
    reach = (KER - 1) // 2
    centre = seg_pad[reach : reach + frame_count]
    summed = jnp.zeros((frame_count, padded.shape[1]), jnp.float32)
    for shift in range(KER):
        same_part = (seg_pad[shift : shift + frame_count] == centre).astype(jnp.float32)[:, None]
        summed = (
            summed
            + kernel[shift].astype(jnp.float32)[None, :]
            * same_part
            * padded[shift : shift + frame_count]
        )
    return summed


def kernel_grad(padded, gradient, seg_pad, frame_count):
    reach = (KER - 1) // 2
    centre = seg_pad[reach : reach + frame_count]
    tap_rows = []
    for shift in range(KER):
        same_part = (seg_pad[shift : shift + frame_count] == centre).astype(jnp.float32)[:, None]
        tap_rows.append(
            jnp.sum(
                same_part * gradient.astype(jnp.float32) * padded[shift : shift + frame_count],
                axis=0,
            )
        )
    return jnp.stack(tap_rows)


def feed_forward(values, gain_vector, weight_in, weight_out):
    normed, norm_back = jax.vjp(layer_norm, values, gain_vector.astype(jnp.float32))
    normed_low = normed.astype(jnp.bfloat16)
    pre_act = product(normed_low, weight_in)
    activation, act_back = jax.vjp(jax.nn.silu, pre_act)
    act_low = activation.astype(jnp.bfloat16)
    return (0.5 * product(act_low, weight_out), (norm_back, normed_low, act_back, act_low))


def feed_back(gradient, stored, weight_in, weight_out):
    norm_back, normed_low, act_back, act_low = stored
    grad_result = (0.5 * gradient).astype(jnp.bfloat16)
    grad_weight_out = transposed_times(act_low, grad_result)
    grad_act = times_transposed(grad_result, weight_out)
    grad_pre = act_back(grad_act)[0].astype(jnp.bfloat16)
    grad_weight_in = transposed_times(normed_low, grad_pre)
    grad_values, grad_gain = norm_back(times_transposed(grad_pre, weight_in))
    return (gradient + grad_values, grad_gain, grad_weight_in, grad_weight_out)


def attend(queries, key_rows, value_rows, segments, scaling):
    frame_count = queries.shape[0]
    block_rows = block_length(frame_count)

    def one_block(block_index):
        offset = block_index * block_rows
        query_rows = lax.dynamic_slice_in_dim(queries, offset, block_rows, 0)
        segment_rows = lax.dynamic_slice_in_dim(segments, offset, block_rows, 0)
        scores = jnp.where(
            segment_rows[:, None] == segments[None, :],
            times_transposed(query_rows, key_rows) * scaling,
            -1e30,
        )
        row_peak = jnp.max(scores, axis=1, keepdims=True)
        weights = jnp.exp(scores - row_peak)
        row_total = jnp.sum(weights, axis=1, keepdims=True)
        probability = (weights / row_total).astype(jnp.bfloat16)
        return (product(probability, value_rows), (row_peak + jnp.log(row_total))[:, 0])

    outputs, log_total = lax.map(one_block, jnp.arange(frame_count // block_rows))
    return (outputs.reshape(frame_count, -1), log_total.reshape(frame_count))


def attend_back(queries, key_rows, value_rows, segments, log_total, grad_out, scaling):
    frame_count = queries.shape[0]
    block_rows = block_length(frame_count)

    def one_block(carried, block_index):
        grad_keys, grad_values = carried
        offset = block_index * block_rows
        query_rows = lax.dynamic_slice_in_dim(queries, offset, block_rows, 0)
        segment_rows = lax.dynamic_slice_in_dim(segments, offset, block_rows, 0)
        total_rows = lax.dynamic_slice_in_dim(log_total, offset, block_rows, 0)
        grad_rows = lax.dynamic_slice_in_dim(grad_out, offset, block_rows, 0)
        same_part = segment_rows[:, None] == segments[None, :]
        scores = times_transposed(query_rows, key_rows) * scaling
        probability = jnp.where(same_part, jnp.exp(scores - total_rows[:, None]), 0.0)
        grad_prob = times_transposed(grad_rows, value_rows)
        grad_values = grad_values + transposed_times(probability.astype(jnp.bfloat16), grad_rows)
        row_delta = jnp.sum(probability * grad_prob, axis=1, keepdims=True)
        grad_scores = (probability * (grad_prob - row_delta)).astype(jnp.bfloat16)
        grad_queries = product(grad_scores, key_rows) * scaling
        grad_keys = grad_keys + transposed_times(grad_scores, query_rows) * scaling
        return ((grad_keys, grad_values), grad_queries)

    initial = (
        jnp.zeros((frame_count, key_rows.shape[1]), jnp.float32),
        jnp.zeros((frame_count, value_rows.shape[1]), jnp.float32),
    )
    (grad_keys, grad_values), grad_queries = lax.scan(
        one_block, initial, jnp.arange(frame_count // block_rows)
    )
    return (grad_queries.reshape(frame_count, -1), grad_keys, grad_values)


def one_batch(gathered, rows_in, rows_grad, stream_lengths):
    (
        full_gain_first,
        full_first_in,
        full_first_out,
        full_gain_attend,
        full_head_projection,
        full_output_projection,
        full_gain_gated,
        full_gated_up,
        full_gain_gate,
        full_kernel_gate,
        full_gated_down,
        full_kernel_merge,
        full_merge_weight,
        full_gain_second,
        full_second_in,
        full_second_out,
        full_gain_final,
    ) = gathered
    frame_count = rows_in.shape[0]
    reach = (KER - 1) // 2
    scaling = 1.0 / math.sqrt(HD)
    positions = (
        lax.axis_index("head") * frame_count
        - reach
        + jnp.arange(frame_count + 2 * reach, dtype=jnp.int32)
    )
    seg_pad = segment_index(positions, stream_lengths)
    start_rows = rows_in.astype(jnp.float32)
    half_first, stored_first = feed_forward(
        start_rows, full_gain_first, full_first_in, full_first_out
    )
    first_mid = start_rows + half_first
    normed_att, norm_att_back = jax.vjp(layer_norm, first_mid, full_gain_attend.astype(jnp.float32))
    normed_att_low = normed_att.astype(jnp.bfloat16)
    projected = product(normed_att_low, full_head_projection).astype(jnp.bfloat16)
    by_head = lax.all_to_all(projected, "head", split_axis=1, concat_axis=0, tiled=True)
    stream_len = by_head.shape[0]
    local_heads = by_head.shape[1] // (3 * HD)
    segments = segment_index(jnp.arange(stream_len, dtype=jnp.int32), stream_lengths)
    cos_table, sin_table = rotary_tables(stream_len, HD)
    stored_heads = []
    attended_list = []
    for head_index in range(local_heads):
        column_base = head_index * 3 * HD
        queries = rotate(
            by_head[:, column_base : column_base + HD].astype(jnp.float32),
            cos_table,
            sin_table,
            1.0,
        ).astype(jnp.bfloat16)
        key_rows = rotate(
            by_head[:, column_base + HD : column_base + 2 * HD].astype(jnp.float32),
            cos_table,
            sin_table,
            1.0,
        ).astype(jnp.bfloat16)
        value_rows = by_head[:, column_base + 2 * HD : column_base + 3 * HD]
        head_result, log_total = attend(queries, key_rows, value_rows, segments, scaling)
        stored_heads.append((queries, key_rows, value_rows, log_total))
        attended_list.append(head_result.astype(jnp.bfloat16))
    attended = lax.all_to_all(
        jnp.concatenate(attended_list, axis=1), "head", split_axis=0, concat_axis=1, tiled=True
    )
    branch_global = product(attended, full_output_projection)
    normed_cg, norm_cg_back = jax.vjp(layer_norm, first_mid, full_gain_gated.astype(jnp.float32))
    normed_cg_low = normed_cg.astype(jnp.bfloat16)
    lifted = product(normed_cg_low, full_gated_up)
    hidden, gelu_back = jax.vjp(exact_gelu, lifted)
    half_width = hidden.shape[1] // 2
    left_half = hidden[:, :half_width]
    gate_norm, gate_norm_back = jax.vjp(
        layer_norm, hidden[:, half_width:], full_gain_gate.astype(jnp.float32)
    )
    gate_low = gate_norm.astype(jnp.bfloat16)
    gate_pad = extended(gate_low, (("head", 0),), reach)
    gate_values = depthwise(gate_pad, full_kernel_gate, seg_pad, frame_count)
    gated_low = (left_half * gate_values).astype(jnp.bfloat16)
    branch_local = product(gated_low, full_gated_down)
    joined_low = jnp.concatenate([branch_global, branch_local], axis=1).astype(jnp.bfloat16)
    joined_pad = extended(joined_low, (("head", 0),), reach)
    merged_low = (
        joined_low.astype(jnp.float32)
        + depthwise(joined_pad, full_kernel_merge, seg_pad, frame_count)
    ).astype(jnp.bfloat16)
    second_mid = first_mid + product(merged_low, full_merge_weight)
    half_second, stored_second = feed_forward(
        second_mid, full_gain_second, full_second_in, full_second_out
    )
    third_mid = second_mid + half_second
    normed_out, final_back = jax.vjp(layer_norm, third_mid, full_gain_final.astype(jnp.float32))
    grad_third, grad_gain_final = final_back(rows_grad.astype(jnp.float32))
    grad_second_mid, grad_gain_second, grad_second_in, grad_second_out = feed_back(
        grad_third, stored_second, full_second_in, full_second_out
    )
    grad_merged = grad_second_mid.astype(jnp.bfloat16)
    grad_merge_weight = transposed_times(merged_low, grad_merged)
    grad_mix_low = times_transposed(grad_merged, full_merge_weight).astype(jnp.bfloat16)
    grad_mix_pad = extended(grad_mix_low, (("head", 0),), reach)
    grad_joined = grad_mix_low.astype(jnp.float32) + depthwise(
        grad_mix_pad, full_kernel_merge[::-1], seg_pad, frame_count
    )
    grad_kernel_merge = kernel_grad(joined_pad, grad_mix_low, seg_pad, frame_count)
    grad_global = grad_joined[:, :D].astype(jnp.bfloat16)
    grad_local = grad_joined[:, D:].astype(jnp.bfloat16)
    grad_gated_down = transposed_times(gated_low, grad_local)
    grad_gated = times_transposed(grad_local, full_gated_down)
    grad_left = grad_gated * gate_values
    grad_gate_low = (grad_gated * left_half).astype(jnp.bfloat16)
    grad_gate_pad = extended(grad_gate_low, (("head", 0),), reach)
    grad_gate_norm = depthwise(grad_gate_pad, full_kernel_gate[::-1], seg_pad, frame_count)
    grad_kernel_gate = kernel_grad(gate_pad, grad_gate_low, seg_pad, frame_count)
    grad_right, grad_gain_gate = gate_norm_back(grad_gate_norm)
    grad_lifted = gelu_back(jnp.concatenate([grad_left, grad_right], axis=1))[0].astype(
        jnp.bfloat16
    )
    grad_gated_up = transposed_times(normed_cg_low, grad_lifted)
    grad_mid_local, grad_gain_gated = norm_cg_back(times_transposed(grad_lifted, full_gated_up))
    grad_output_projection = transposed_times(attended, grad_global)
    grad_attended = times_transposed(grad_global, full_output_projection).astype(jnp.bfloat16)
    grad_by_head = lax.all_to_all(grad_attended, "head", split_axis=1, concat_axis=0, tiled=True)
    grad_pieces = []
    for head_index in range(local_heads):
        queries, key_rows, value_rows, log_total = stored_heads[head_index]
        grad_head = grad_by_head[:, head_index * HD : (head_index + 1) * HD]
        grad_queries, grad_keys, grad_values = attend_back(
            queries, key_rows, value_rows, segments, log_total, grad_head, scaling
        )
        grad_pieces.append(rotate(grad_queries, cos_table, sin_table, -1.0))
        grad_pieces.append(rotate(grad_keys, cos_table, sin_table, -1.0))
        grad_pieces.append(grad_values)
    grad_by_frame = lax.all_to_all(
        jnp.concatenate(grad_pieces, axis=1).astype(jnp.bfloat16),
        "head",
        split_axis=0,
        concat_axis=1,
        tiled=True,
    )
    grad_head_projection = transposed_times(normed_att_low, grad_by_frame)
    grad_mid_global, grad_gain_attend = norm_att_back(
        times_transposed(grad_by_frame, full_head_projection)
    )
    grad_first_mid = grad_second_mid + grad_mid_local + grad_mid_global
    grad_start, grad_gain_first, grad_first_in, grad_first_out = feed_back(
        grad_first_mid, stored_first, full_first_in, full_first_out
    )
    gradients = (
        grad_gain_first,
        grad_first_in,
        grad_first_out,
        grad_gain_attend,
        grad_head_projection,
        grad_output_projection,
        grad_gain_gated,
        grad_gated_up,
        grad_gain_gate,
        grad_kernel_gate,
        grad_gated_down,
        grad_kernel_merge,
        grad_merge_weight,
        grad_gain_second,
        grad_second_in,
        grad_second_out,
        grad_gain_final,
    )
    return (normed_out.astype(jnp.bfloat16), grad_start, gradients)


def on_device(
    frames,
    cotangent,
    lengths,
    gain_first,
    first_in,
    first_out,
    gain_attend,
    head_projection,
    output_projection,
    gain_gated,
    gated_up,
    gain_gate,
    kernel_gate,
    gated_down,
    kernel_merge,
    merge_weight,
    gain_second,
    second_in,
    second_out,
    gain_final,
):
    shares = None
    summed = None
    outputs_list = []
    grad_list = []
    for batch_index in range(frames.shape[0]):
        gathered = (
            lax.all_gather(gain_first, ("head", "seq"), axis=0, tiled=True),
            lax.all_gather(first_in, ("head", "seq"), axis=0, tiled=True),
            lax.all_gather(first_out, ("head", "seq"), axis=0, tiled=True),
            lax.all_gather(gain_attend, ("head", "seq"), axis=0, tiled=True),
            lax.all_gather(head_projection, ("head", "seq"), axis=0, tiled=True),
            lax.all_gather(output_projection, ("head", "seq"), axis=0, tiled=True),
            lax.all_gather(gain_gated, ("head", "seq"), axis=0, tiled=True),
            lax.all_gather(gated_up, ("head", "seq"), axis=0, tiled=True),
            lax.all_gather(gain_gate, ("head", "seq"), axis=0, tiled=True),
            lax.all_gather(kernel_gate, ("head", "seq"), axis=1, tiled=True),
            lax.all_gather(gated_down, ("head", "seq"), axis=0, tiled=True),
            lax.all_gather(kernel_merge, ("head", "seq"), axis=1, tiled=True),
            lax.all_gather(merge_weight, ("head", "seq"), axis=0, tiled=True),
            lax.all_gather(gain_second, ("head", "seq"), axis=0, tiled=True),
            lax.all_gather(second_in, ("head", "seq"), axis=0, tiled=True),
            lax.all_gather(second_out, ("head", "seq"), axis=0, tiled=True),
            lax.all_gather(gain_final, ("head", "seq"), axis=0, tiled=True),
        )
        result, grad_rows, gradients = one_batch(
            gathered, frames[batch_index, 0], cotangent[batch_index, 0], lengths[batch_index, 0]
        )
        outputs_list.append(result)
        grad_list.append(grad_rows)
        summed = gradients if summed is None else jax.tree.map(jnp.add, summed, gradients)
    shares = (
        lax.psum_scatter(summed[0], ("head", "seq"), scatter_dimension=0, tiled=True),
        lax.psum_scatter(summed[1], ("head", "seq"), scatter_dimension=0, tiled=True),
        lax.psum_scatter(summed[2], ("head", "seq"), scatter_dimension=0, tiled=True),
        lax.psum_scatter(summed[3], ("head", "seq"), scatter_dimension=0, tiled=True),
        lax.psum_scatter(summed[4], ("head", "seq"), scatter_dimension=0, tiled=True),
        lax.psum_scatter(summed[5], ("head", "seq"), scatter_dimension=0, tiled=True),
        lax.psum_scatter(summed[6], ("head", "seq"), scatter_dimension=0, tiled=True),
        lax.psum_scatter(summed[7], ("head", "seq"), scatter_dimension=0, tiled=True),
        lax.psum_scatter(summed[8], ("head", "seq"), scatter_dimension=0, tiled=True),
        lax.psum_scatter(summed[9], ("head", "seq"), scatter_dimension=1, tiled=True),
        lax.psum_scatter(summed[10], ("head", "seq"), scatter_dimension=0, tiled=True),
        lax.psum_scatter(summed[11], ("head", "seq"), scatter_dimension=1, tiled=True),
        lax.psum_scatter(summed[12], ("head", "seq"), scatter_dimension=0, tiled=True),
        lax.psum_scatter(summed[13], ("head", "seq"), scatter_dimension=0, tiled=True),
        lax.psum_scatter(summed[14], ("head", "seq"), scatter_dimension=0, tiled=True),
        lax.psum_scatter(summed[15], ("head", "seq"), scatter_dimension=0, tiled=True),
        lax.psum_scatter(summed[16], ("head", "seq"), scatter_dimension=0, tiled=True),
    )
    output_frames = jnp.stack(outputs_list)[:, None]
    grad_frames = jnp.stack(grad_list)[:, None]
    return (
        output_frames,
        grad_frames,
        shares[0],
        shares[1],
        shares[2],
        shares[3],
        shares[4],
        shares[5],
        shares[6],
        shares[7],
        shares[8],
        shares[9],
        shares[10],
        shares[11],
        shares[12],
        shares[13],
        shares[14],
        shares[15],
        shares[16],
    )


def solution(mesh):
    in_specs = (
        P(None, "seq", "head", None),
        P(None, "seq", "head", None),
        P(None, "seq", None),
        P(("head", "seq")),
        P(("head", "seq"), None),
        P(("head", "seq"), None),
        P(("head", "seq")),
        P(("head", "seq"), None),
        P(("head", "seq"), None),
        P(("head", "seq")),
        P(("head", "seq"), None),
        P(("head", "seq")),
        P(None, ("head", "seq")),
        P(("head", "seq"), None),
        P(None, ("head", "seq")),
        P(("head", "seq"), None),
        P(("head", "seq")),
        P(("head", "seq"), None),
        P(("head", "seq"), None),
        P(("head", "seq")),
    )
    out_specs = (
        P(None, "seq", "head", None),
        P(None, "seq", "head", None),
        P(("head", "seq")),
        P(("head", "seq"), None),
        P(("head", "seq"), None),
        P(("head", "seq")),
        P(("head", "seq"), None),
        P(("head", "seq"), None),
        P(("head", "seq")),
        P(("head", "seq"), None),
        P(("head", "seq")),
        P(None, ("head", "seq")),
        P(("head", "seq"), None),
        P(None, ("head", "seq")),
        P(("head", "seq"), None),
        P(("head", "seq")),
        P(("head", "seq"), None),
        P(("head", "seq"), None),
        P(("head", "seq")),
    )
    return jax.shard_map(
        on_device, mesh=mesh, in_specs=in_specs, out_specs=out_specs, check_vma=False
    )
```

profile of v0, /device:TPU:0, one launch (start us, length us, event | category | flops | bytes accessed | tf_op | source)
XLA Modules:
  0.0 1970.9 jit_solution(16230279963308774187)
XLA Ops:
  16.6 44.8 %all-gather = bf16[32,48,31]{1,2,0:T(8,128)(2,1)S(1)} all-gather(bf16[1,48,31]{1,2,0:T(8,128)(2,1)} %bitcast.599), channel_id=1, replica_groups=mesh['head'=4,'seq'=8] {'head','seq'}, dimensions={0}, use_global_device_ids=true | all-gather | bytes 98208 | tf_op jit(solution)/shard_map/all_gather | solution.py:397
  63.7 37.9 %all_gather.79 = bf16[31,1024]{0,1:T(8,128)(2,1)S(1)} all-gather(bf16[31,32]{0,1:T(8,128)(2,1)S(1)} %copy.268), channel_id=1, replica_groups=mesh['head'=4,'seq'=8] {'head','seq'}, dimensions={1}, use_global_device_ids=true | all-gather | bytes 65472 | tf_op jit(solution)/shard_map/all_gather | solution.py:399
  101.6 3.5 convert_reduce_fusion.32
  111.9 39.9 %all-reduce.13 = (bf16[512]{0:T(512)(128)(2,1)S(1)}, bf16[512]{0:T(512)(128)(2,1)S(1)}, bf16[512]{0:T(512)(128)(2,1)S(1)}, bf16[1536]{0:T(1024)(128)(2,1)S(1)}, ...) all-reduce(bf16[512]{0:T(512)(128)(2,1)S(1)} %dynamic-update-slice,, ...), channel_id=1, replica_groups=mesh['head'=4,'seq'=8] {'head','seq'}, use_global_device_ids=true, to_apply=%add | all-reduce | flops 4096 | bytes 16384
  160.0 26.1 %all-gather.14.cloned.1.call-done = bf16[512,1536]{1,0:T(8,128)(2,1)} async-done(((bf16[16,1536]{1,0:T(8,128)(2,1)}), bf16[512,1536]{1,0:T(8,128)(2,1)}) %all-gather.14.cloned.1.call-update) | async-done | bytes 1572880 | tf_op jit(solution)/shard_map/all_gather | solution.py:392
  189.0 4.2 all-to-all-start.2
  198.6 6.8 all-to-all-done.2
  205.5 3.5 all-to-all-start
  209.0 47.4 %all_gather.73 = bf16[512,512]{1,0:T(8,128)(2,1)} all-gather(bf16[16,512]{1,0:T(8,128)(2,1)S(1)} %copy-done.518), channel_id=1, replica_groups=mesh['head'=4,'seq'=8] {'head','seq'}, dimensions={0}, use_global_device_ids=true | all-gather | bytes 540672 | tf_op jit(solution)/shard_map/all_gather | solution.py:393
  266.8 7.3 while.110
  279.4 10.1 while.111
  292.7 4.0 all-to-all-start.3
  297.9 8.1 while.108
  309.6 10.1 while.109
  322.9 4.1 all-to-all-start.1
  328.6 4.1 all-to-all-done.1
  333.0 10.6 multiply_multiply_fusion.10
  345.0 9.7 multiply_multiply_fusion.11
  362.5 4.5 collective-permute-start
  369.6 16.8 multiply_convert_fusion.10
  389.4 4.9 collective-permute-start.6
  396.0 19.9 %multiply_convert_fusion.12 = (bf16[256,1536]{1,0:T(8,128)(2,1)S(1)}, f32[256,1536]{1,0:T(8,128)}) fusion(f32[256,3072]{1,0:T(8,128)S(1)} %copy-done.17, bf16[15,1536]{1,0:T(8,128)(2,1)} %collective-permute-done.1, bf16[256,1536]{1,0:T(8,128)(2,1)S(1)} %get-tuple-element.1684, f32[256]{0:T(256)} %get-tuple-element.1727, f32[1536]{0:T(1024)S(1)} %get-tuple-element.1355, ...), kind=kLoop, calls=%fused_computation.767 | loop fusion | flops 84148224 | bytes 5031936 | tf_op jit(solution)/shard_map/convert_element_type | solution.py:269
  419.3 6.1 collective-permute-start.2
  427.7 7.8 fusion.403
  439.7 3.9 fusion.695
  443.6 37.6 %all-gather.24.cloned.1.call-done = bf16[2048,512]{1,0:T(8,128)(2,1)} async-done(((bf16[64,512]{1,0:T(8,128)(2,1)}), bf16[2048,512]{1,0:T(8,128)(2,1)}) %all-gather.24.cloned.1.call-update) | async-done | bytes 2097168 | tf_op jit(solution)/shard_map/all_gather | solution.py:403
  486.3 7.3 fusion.402
  528.8 3.9 collective-permute-start.12
  537.2 5.5 stack.503
  544.7 4.5 collective-permute-start.8
  550.7 12.8 fusion.405
  563.6 7.5 fusion.206
  576.9 4.7 fusion.207
  588.1 10.3 fusion.404
  598.5 7.1 fusion.146
  611.9 5.6 fusion.147
  631.7 5.2 all-to-all-start.6
  642.2 4.6 all-to-all-start.4
  648.5 27.9 %while.115 = (s32[]{:T(128)}, f32[1024,64]{0,1:T(8,128)}, f32[1024,64]{0,1:T(8,128)}, f32[2,512,64]{1,0,2:T(2,128)}, s32[2]{0:T(128)S(1)}, /*index=5*/s32[1024]{...) while((s32[]{:T(128)}, f32[1024,64]{0,1:T(8,128)}, ...), condition=%wide.region_73.74_spmd.clone, body=%wide.region_71.73_spmd.clone.sunk | while | flops 341147136 | bytes 19026312 | solution.py:185
  677.1 23.3 %while.114 = (s32[]{:T(128)}, f32[1024,64]{0,1:T(8,128)}, f32[1024,64]{0,1:T(8,128)}, f32[2,512,64]{1,0,2:T(2,128)}, s32[2]{0:T(128)S(1)}, /*index=5*/s32[1024]{...) while((s32[]{:T(128)}, f32[1024,64]{0,1:T(8,128)}, ...), condition=%wide.region_70.71_spmd.clone, body=%wide.region_68.70_spmd.clone.sunk | while | flops 341147136 | bytes 19698104 | solution.py:185
  692.8 3.4 dynamic_update_slice.68
  703.1 25.4 %while.113 = (s32[]{:T(128)}, f32[1024,64]{0,1:T(8,128)}, f32[1024,64]{0,1:T(8,128)}, f32[2,512,64]{1,0,2:T(2,128)}, s32[2]{0:T(128)S(1)}, /*index=5*/s32[1024]{...) while((s32[]{:T(128)}, f32[1024,64]{0,1:T(8,128)}, ...), condition=%wide.region_55.56_spmd.clone, body=%wide.region_53.55_spmd.clone.sunk | while | flops 341147136 | bytes 20205888 | solution.py:185
  729.3 23.3 %while.112 = (s32[]{:T(128)}, f32[1024,64]{0,1:T(8,128)}, f32[1024,64]{0,1:T(8,128)}, f32[2,512,64]{1,0,2:T(2,128)}, s32[2]{0:T(128)S(1)}, /*index=5*/s32[1024]{...) while((s32[]{:T(128)}, f32[1024,64]{0,1:T(8,128)}, ...), condition=%wide.region_52.53_spmd.clone, body=%wide.region_50.52_spmd.clone.sunk | while | flops 341147136 | bytes 19681572 | solution.py:185
  733.8 3.5 dynamic_update_slice.66
  744.9 3.5 dynamic_update_slice.66
  760.5 4.2 all-to-all-start.5
  768.5 6.2 all-to-all-done.5
  774.7 3.5 all-to-all-start.7
  780.7 8.5 all-to-all-done.7
  789.2 4.5 convolution_add_fusion.6
  812.4 4.5 collective-permute-start.10
  823.4 16.5 multiply_reduce_fusion.4
  840.7 16.9 multiply_reduce_fusion.5
  868.0 3.8 convolution_add_fusion.4
  871.9 3.5 fusion.734
  907.4 41.4 %all-reduce.12 = (f32[512]{0:T(512)S(1)}, f32[512]{0:T(512)S(1)}, f32[512]{0:T(512)S(1)}, f32[1536]{0:T(1024)S(1)}, f32[512]{0:T(512)S(1)}, /*index=5*/f32[512]{0:T(512)S(1)}) all-reduce(f32[512]{0:T(512)S(1)} %add.1477, f32[512]{0:T(512)S(1)} %add.1480, f32[512]{0:T(512)S(1)} %add.1483, ...), channel_id=2, replica_groups=mesh['head'=4,'seq'=8] {'head','seq'}, use_global_device_ids=true, to_apply=%region_80.81.clone | all-reduce | flops 4096 | bytes 32768
  955.0 100.5 %reduce-scatter.28.cloned.1.call-done = f32[32,512]{1,0:T(8,128)} async-done(((f32[1024,512]{1,0:T(8,128)}), f32[32,512]{1,0:T(8,128)}) %reduce-scatter.28.cloned.1.call-update) | async-done | bytes 65552 | tf_op jit(solution)/shard_map/reduce_scatter | solution.py:425
  1055.5 105.0 %reduce-scatter.26.cloned.1.call-done = f32[48,512]{1,0:T(8,128)} async-done(((f32[1536,512]{1,0:T(8,128)}), f32[48,512]{1,0:T(8,128)}) %reduce-scatter.26.cloned.1.call-update) | async-done | bytes 98320 | tf_op jit(solution)/shard_map/reduce_scatter | solution.py:423
  1160.5 107.0 %reduce-scatter.20.cloned.1.call-done = f32[16,1536]{1,0:T(8,128)} async-done(((f32[512,1536]{1,0:T(8,128)}), f32[16,1536]{1,0:T(8,128)}) %reduce-scatter.20.cloned.1.call-update) | async-done | bytes 98320 | tf_op jit(solution)/shard_map/reduce_scatter | solution.py:417
  1267.5 145.6 %reduce-scatter.32.cloned.1.call-done = f32[64,512]{1,0:T(8,128)} async-done(((f32[2048,512]{1,0:T(8,128)}), f32[64,512]{1,0:T(8,128)}) %reduce-scatter.32.cloned.1.call-update) | async-done | bytes 131088 | tf_op jit(solution)/shard_map/reduce_scatter | solution.py:428
  1413.1 143.4 %reduce-scatter.30.cloned.1.call-done = f32[16,2048]{1,0:T(8,128)} async-done(((f32[512,2048]{1,0:T(8,128)}), f32[16,2048]{1,0:T(8,128)}) %reduce-scatter.30.cloned.1.call-update) | async-done | bytes 131088 | tf_op jit(solution)/shard_map/reduce_scatter | solution.py:427
  1556.5 118.0 %reduce-scatter.24.cloned.1.call-done = f32[16,3072]{1,0:T(8,128)} async-done(((f32[512,3072]{1,0:T(8,128)}), f32[16,3072]{1,0:T(8,128)}) %reduce-scatter.24.cloned.1.call-update) | async-done | bytes 196624 | tf_op jit(solution)/shard_map/reduce_scatter | solution.py:420
  1674.5 145.5 %reduce-scatter.18.cloned.1.call-done = f32[64,512]{1,0:T(8,128)} async-done(((f32[2048,512]{1,0:T(8,128)}), f32[64,512]{1,0:T(8,128)}) %reduce-scatter.18.cloned.1.call-update) | async-done | bytes 131088 | tf_op jit(solution)/shard_map/reduce_scatter | solution.py:415
  1820.0 144.2 %reduce-scatter.16.cloned.1.call-done = f32[16,2048]{1,0:T(8,128)} async-done(((f32[512,2048]{1,0:T(8,128)}), f32[16,2048]{1,0:T(8,128)}) %reduce-scatter.16.cloned.1.call-update) | async-done | bytes 131088 | tf_op jit(solution)/shard_map/reduce_scatter | solution.py:414
  (1824 shorter events, 375.9 us)
Async XLA Ops:
  7.2 56.4 %copy-start.549 = (bf16[31,32]{1,0:T(8,128)(2,1)S(1)}, bf16[31,32]{1,0:T(8,128)(2,1)}, u32[]{:S(2)}) copy-start(bf16[31,32]{1,0:T(8,128)(2,1)} %param.50) | copy-start | bytes 5956
  7.2 146.9 %all-gather.10.cloned.1.call-start = ((), (), s32[]{:S(2)}) async-start(), calls=%async_computation.19 | async-start | bytes 2162688 | tf_op jit(solution)/shard_map/all_gather | solution.py:389
  7.9 148.6 %all-gather.12.cloned.1.call-start = ((), (), s32[]{:S(2)}) async-start(), calls=%async_computation.20 | async-start | bytes 2162688 | tf_op jit(solution)/shard_map/all_gather | solution.py:390
  8.7 177.3 %all-gather.14.cloned.1.call-start = ((), (), s32[]{:S(2)}) async-start(), calls=%async_computation.21 | async-start | bytes 1622016 | tf_op jit(solution)/shard_map/all_gather | solution.py:392
  9.4 323.6 %all-gather.16.cloned.1.call-start = ((), (), s32[]{:S(2)}) async-start(), calls=%async_computation.22 | async-start | bytes 3244032 | tf_op jit(solution)/shard_map/all_gather | solution.py:395
  10.0 376.5 %all-gather.18.cloned.1.call-start = ((), (), s32[]{:S(2)}) async-start(), calls=%async_computation.23 | async-start | bytes 1622016 | tf_op jit(solution)/shard_map/all_gather | solution.py:398
  10.6 425.0 %all-gather.20.cloned.1.call-start = ((), (), s32[]{:S(2)}) async-start(), calls=%async_computation.24 | async-start | bytes 1081344 | tf_op jit(solution)/shard_map/all_gather | solution.py:400
  11.2 428.5 %all-gather.22.cloned.1.call-start = ((), (), s32[]{:S(2)}) async-start(), calls=%async_computation.25 | async-start | bytes 2162688 | tf_op jit(solution)/shard_map/all_gather | solution.py:402
  11.9 469.3 %all-gather.24.cloned.1.call-start = ((), (), s32[]{:S(2)}) async-start(), calls=%async_computation.26 | async-start | bytes 2162688 | tf_op jit(solution)/shard_map/all_gather | solution.py:403
  62.8 332.8 %copy-start.135 = (f32[1536]{0:T(1024)}, f32[1536]{0:T(1024)S(1)}, u32[]{:S(2)}) copy-start(f32[1536]{0:T(1024)S(1)} %get-tuple-element.1354) | copy-start | bytes 18436
  62.8 332.8 %copy-start.137 = (f32[1536]{0:T(1024)}, f32[1536]{0:T(1024)S(1)}, u32[]{:S(2)}) copy-start(f32[1536]{0:T(1024)S(1)} %get-tuple-element.1355) | copy-start | bytes 18436
  62.8 332.8 %copy-start.139 = (f32[1536]{0:T(1024)}, f32[1536]{0:T(1024)S(1)}, u32[]{:S(2)}) copy-start(f32[1536]{0:T(1024)S(1)} %get-tuple-element.1356) | copy-start | bytes 18436
  62.8 332.8 %copy-start.141 = (f32[1536]{0:T(1024)}, f32[1536]{0:T(1024)S(1)}, u32[]{:S(2)}) copy-start(f32[1536]{0:T(1024)S(1)} %get-tuple-element.1357) | copy-start | bytes 18436
  105.1 46.7 %copy-start.24 = (bf16[2,1,256,512]{3,2,1,0:T(8,128)(2,1)S(1)}, bf16[2,1,256,512]{3,2,1,0:T(8,128)(2,1)}, u32[]{:S(2)}) copy-start(bf16[2,1,256,512]{3,2,1,0:T(8,128)(2,1)} %param.36) | copy-start | bytes 1572868
  151.8 41.4 %copy-start.125 = (f32[512]{0:T(512)}, f32[512]{0:T(512)S(1)}, u32[]{:S(2)}) copy-start(f32[512]{0:T(512)S(1)} %convert_element_type.940) | copy-start | bytes 6148
  152.0 41.3 %copy-start.319 = (f32[256]{0:T(256)}, f32[256]{0:T(256)S(1)}, u32[]{:S(2)}) copy-start(f32[256]{0:T(256)S(1)} %get-tuple-element.1806) | copy-start | bytes 3076
  152.9 43.5 %copy-start.327 = (f32[512]{0:T(512)}, f32[512]{0:T(512)S(1)}, u32[]{:S(2)}) copy-start(f32[512]{0:T(512)S(1)} %convert_element_type.944) | copy-start | bytes 6148
  152.9 40.4 %copy-start.325 = (f32[256]{0:T(256)}, f32[256]{0:T(256)S(1)}, u32[]{:S(2)}) copy-start(f32[256]{0:T(256)S(1)} %fusion.663) | copy-start | bytes 3076
  152.9 191.2 %copy-start.133 = (f32[512]{0:T(512)}, f32[512]{0:T(512)S(1)}, u32[]{:S(2)}) copy-start(f32[512]{0:T(512)S(1)} %convert_element_type.955) | copy-start | bytes 6148
  152.9 202.3 %copy-start.186 = (f32[1536]{0:T(1024)}, f32[1536]{0:T(1024)S(1)}, u32[]{:S(2)}) copy-start(f32[1536]{0:T(1024)S(1)} %convert_element_type.959) | copy-start | bytes 18436
  159.7 275.9 %copy-start.22 = (f32[256,512]{1,0:T(8,128)}, f32[256,512]{1,0:T(8,128)S(1)}, u32[]{:S(2)}) copy-start(f32[256,512]{1,0:T(8,128)S(1)} %get-tuple-element.1788) | copy-start | bytes 1572868
  159.7 173.3 %copy-start.451 = (f32[256]{0:T(256)}, f32[256]{0:T(256)S(1)}, u32[]{:S(2)}) copy-start(f32[256]{0:T(256)S(1)} %broadcast_multiply_fusion.4) | copy-start | bytes 3076
  189.0 16.4 all-to-all-start.2
  196.2 147.9 %copy-start.336 = (f32[256]{0:T(256)}, f32[256]{0:T(256)S(1)}, u32[]{:S(2)}) copy-start(f32[256]{0:T(256)S(1)} %broadcast_multiply_fusion.8) | copy-start | bytes 3076
  197.0 147.1 %copy-start.453 = (f32[256]{0:T(256)}, f32[256]{0:T(256)S(1)}, u32[]{:S(2)}) copy-start(f32[256]{0:T(256)S(1)} %fusion.664) | copy-start | bytes 3076
  205.5 54.6 %all-to-all-start = ((bf16[256,4,384]{2,0,1:T(8,128)(2,1)}), bf16[256,4,384]{2,0,1:T(8,128)(2,1)S(1)}, u32[]{:S(2)}, u32[]{:S(2)}) async-start(bf16[256,4,384]{2,0,1:T(8,128)(2,1)} %bitcast.413), calls=%async_computation | async-start | bytes 1572864 | tf_op jit(solution)/shard_map/all_to_all | solution.py:228
  209.0 55.5 %copy-start.545 = (f32[32]{0:T(128)}, f32[32]{0:T(128)S(1)}, u32[]{:S(2)}) copy-start(f32[32]{0:T(128)S(1)} %multiply_exponential_fusion) | copy-start | bytes 388
  292.7 30.2 %all-to-all-start.3 = ((bf16[4,256,128]{1,2,0:T(8,128)(2,1)}), bf16[4,256,128]{1,2,0:T(8,128)(2,1)}, u32[]{:S(2)}, u32[]{:S(2)}) async-start(bf16[4,256,128]{1,2,0:T(8,128)(2,1)} %copy.279), calls=%async_computation.3 | async-start | bytes 524288 | tf_op jit(solution)/shard_map/all_to_all | solution.py:253
  322.9 9.7 all-to-all-start.1
  327.1 573.7 %reduce-scatter.36.cloned.1.call-start = ((), (), s32[]{:S(2)}) async-start(), calls=%async_computation.37 | async-start | bytes 540672
  328.5 60.8 %copy-start.54 = (bf16[256,512]{1,0:T(8,128)(2,1)}, bf16[256,512]{1,0:T(8,128)(2,1)S(1)}, u32[]{:S(2)}) copy-start(bf16[256,512]{1,0:T(8,128)(2,1)S(1)} %convolution_convert_fusion.7) | copy-start | bytes 786436
  357.4 11.2 collective-permute-start.4
  360.6 8.0 collective-permute-start.5
  362.5 33.1 %collective-permute-start = (bf16[15,1536]{1,0:T(8,128)(2,1)}, bf16[15,1536]{1,0:T(8,128)(2,1)S(1)}, u32[]{:S(2)}, u32[]{:S(2)}) collective-permute-start(bf16[15,1536]{1,0:T(8,128)(2,1)} %get-tuple-element.1607), channel_id=1, source_target_pairs={{0,8},{8,16},{16,24},{1,9},{9,17},{17,25},{2,10},{10,18},{18,26},{... | collective-permute-start | bytes 138248 | tf_op jit(solution)/shard_map/ppermute | solution.py:23
  367.1 28.5 %collective-permute-start.1 = (bf16[15,1536]{1,0:T(8,128)(2,1)}, bf16[15,1536]{1,0:T(8,128)(2,1)}, u32[]{:S(2)}, u32[]{:S(2)}) collective-permute-start(bf16[15,1536]{1,0:T(8,128)(2,1)} %get-tuple-element.1608), channel_id=1, source_target_pairs={{8,0},{16,8},{24,16},{9,1},{17,9},{25,17},{10,2},{18,10},{26,18},{... | collective-permute-start | bytes 138248 | tf_op jit(solution)/shard_map/ppermute | solution.py:24
  389.4 37.7 %collective-permute-start.6 = (bf16[15,1024]{1,0:T(8,128)(2,1)S(1)}, bf16[15,1024]{1,0:T(8,128)(2,1)S(1)}, u32[]{:S(2)}, u32[]{:S(2)}) collective-permute-start(bf16[15,1024]{1,0:T(8,128)(2,1)S(1)} %get-tuple-element.1644), channel_id=1, source_target_pairs={{0,8},{8,16},{16,24},{1,9},{9,17},{17,25},{2,10},{10,18},{18,26},{... | collective-permute-start | bytes 92168 | tf_op jit(solution)/shard_map/ppermute | solution.py:23
  394.3 32.8 %collective-permute-start.7 = (bf16[15,1024]{1,0:T(8,128)(2,1)S(1)}, bf16[15,1024]{1,0:T(8,128)(2,1)S(1)}, u32[]{:S(2)}, u32[]{:S(2)}) collective-permute-start(bf16[15,1024]{1,0:T(8,128)(2,1)S(1)} %get-tuple-element.1645), channel_id=1, source_target_pairs={{8,0},{16,8},{24,16},{9,1},{17,9},{25,17},{10,2},{18,10},{26,18},{... | collective-permute-start | bytes 92168 | tf_op jit(solution)/shard_map/ppermute | solution.py:24
  419.3 65.6 %collective-permute-start.2 = (bf16[15,1024]{1,0:T(8,128)(2,1)}, bf16[15,1024]{1,0:T(8,128)(2,1)}, u32[]{:S(2)}, u32[]{:S(2)}) collective-permute-start(bf16[15,1024]{1,0:T(8,128)(2,1)} %get-tuple-element.1640), channel_id=1, source_target_pairs={{0,8},{8,16},{16,24},{1,9},{9,17},{17,25},{2,10},{10,18},{18,26},{... | collective-permute-start | bytes 92168 | tf_op jit(solution)/shard_map/ppermute | solution.py:23
  425.4 59.5 %collective-permute-start.3 = (bf16[15,1024]{1,0:T(8,128)(2,1)}, bf16[15,1024]{1,0:T(8,128)(2,1)}, u32[]{:S(2)}, u32[]{:S(2)}) collective-permute-start(bf16[15,1024]{1,0:T(8,128)(2,1)} %get-tuple-element.1641), channel_id=1, source_target_pairs={{8,0},{16,8},{24,16},{9,1},{17,9},{25,17},{10,2},{18,10},{26,18},{... | collective-permute-start | bytes 92168 | tf_op jit(solution)/shard_map/ppermute | solution.py:24
  439.7 41.5 %copy-start.35 = (f32[256,512]{1,0:T(8,128)S(1)}, f32[256,512]{1,0:T(8,128)}, u32[]{:S(2)}) copy-start(f32[256,512]{1,0:T(8,128)} %copy-done.34) | copy-start | bytes 1572868
  518.5 107.8 %copy-start.67 = (f32[256,512]{1,0:T(8,128)}, f32[256,512]{1,0:T(8,128)S(1)}, u32[]{:S(2)}) copy-start(f32[256,512]{1,0:T(8,128)S(1)} %add_add_fusion.15) | copy-start | bytes 1572868
  528.8 21.7 %collective-permute-start.12 = (bf16[15,1024]{1,0:T(8,128)(2,1)}, bf16[15,1024]{1,0:T(8,128)(2,1)}, u32[]{:S(2)}, u32[]{:S(2)}) collective-permute-start(bf16[15,1024]{1,0:T(8,128)(2,1)} %get-tuple-element.1636), channel_id=1, source_target_pairs={{0,8},{8,16},{16,24},{1,9},{9,17},{17,25},{2,10},{10,18},{18,26},{... | collective-permute-start | bytes 92168 | tf_op jit(solution)/shard_map/ppermute | solution.py:23
  532.7 17.8 collective-permute-start.13
  544.6 357.5 %reduce-scatter.34.cloned.1.call-start = ((), (), s32[]{:S(2)}) async-start(), calls=%async_computation.36 | async-start | bytes 811008
  544.7 43.1 %collective-permute-start.8 = (bf16[15,1024]{1,0:T(8,128)(2,1)}, bf16[15,1024]{1,0:T(8,128)(2,1)S(1)}, u32[]{:S(2)}, u32[]{:S(2)}) collective-permute-start(bf16[15,1024]{1,0:T(8,128)(2,1)} %get-tuple-element.1634), channel_id=1, source_target_pairs={{0,8},{8,16},{16,24},{1,9},{9,17},{17,25},{2,10},{10,18},{18,26},{... | collective-permute-start | bytes 92168 | tf_op jit(solution)/shard_map/ppermute | solution.py:23
  549.2 38.6 %collective-permute-start.9 = (bf16[15,1024]{1,0:T(8,128)(2,1)}, bf16[15,1024]{1,0:T(8,128)(2,1)S(1)}, u32[]{:S(2)}, u32[]{:S(2)}) collective-permute-start(bf16[15,1024]{1,0:T(8,128)(2,1)} %get-tuple-element.1635), channel_id=1, source_target_pairs={{8,0},{16,8},{24,16},{9,1},{17,9},{25,17},{10,2},{18,10},{26,18},{... | collective-permute-start | bytes 92168 | tf_op jit(solution)/shard_map/ppermute | solution.py:24
  623.8 331.1 %reduce-scatter.22.cloned.1.call-start = ((), (), s32[]{:S(2)}) async-start(), calls=%async_computation.30 | async-start | bytes 1081344 | tf_op jit(solution)/shard_map/reduce_scatter | solution.py:418
  626.2 429.3 %reduce-scatter.28.cloned.1.call-start = ((), (), s32[]{:S(2)}) async-start(), calls=%async_computation.33 | async-start | bytes 2162688 | tf_op jit(solution)/shard_map/reduce_scatter | solution.py:425
  631.7 10.6 all-to-all-start.6
  636.8 523.6 %reduce-scatter.26.cloned.1.call-start = ((), (), s32[]{:S(2)}) async-start(), calls=%async_computation.32 | async-start | bytes 3244032 | tf_op jit(solution)/shard_map/reduce_scatter | solution.py:423
  642.2 58.2 %all-to-all-start.4 = ((bf16[256,4,128]{2,0,1:T(8,128)(2,1)}), bf16[256,4,128]{2,0,1:T(8,128)(2,1)}, u32[]{:S(2)}, u32[]{:S(2)}) async-start(bf16[256,4,128]{2,0,1:T(8,128)(2,1)} %bitcast.415), calls=%async_computation.4 | async-start | bytes 524288 | tf_op jit(solution)/shard_map/all_to_all | solution.py:312
  760.5 14.3 all-to-all-start.5
  774.7 14.5 all-to-all-start.7
  778.2 489.2 %reduce-scatter.20.cloned.1.call-start = ((), (), s32[]{:S(2)}) async-start(), calls=%async_computation.29 | async-start | bytes 3244032 | tf_op jit(solution)/shard_map/reduce_scatter | solution.py:417
  793.8 619.3 %reduce-scatter.32.cloned.1.call-start = ((), (), s32[]{:S(2)}) async-start(), calls=%async_computation.35 | async-start | bytes 4325376 | tf_op jit(solution)/shard_map/reduce_scatter | solution.py:428
  800.4 756.1 %reduce-scatter.30.cloned.1.call-start = ((), (), s32[]{:S(2)}) async-start(), calls=%async_computation.34 | async-start | bytes 4325376 | tf_op jit(solution)/shard_map/reduce_scatter | solution.py:427
  806.6 867.8 %reduce-scatter.24.cloned.1.call-start = ((), (), s32[]{:S(2)}) async-start(), calls=%async_computation.31 | async-start | bytes 6488064 | tf_op jit(solution)/shard_map/reduce_scatter | solution.py:420
  807.8 14.0 collective-permute-start.14
  811.1 10.7 collective-permute-start.15
  812.4 28.2 %collective-permute-start.10 = (bf16[15,1536]{1,0:T(8,128)(2,1)S(1)}, bf16[15,1536]{1,0:T(8,128)(2,1)S(1)}, u32[]{:S(2)}, u32[]{:S(2)}) collective-permute-start(bf16[15,1536]{1,0:T(8,128)(2,1)S(1)} %get-tuple-element.1603), channel_id=1, source_target_pairs={{0,8},{8,16},{16,24},{1,9},{9,17},{17,25},{2,10},{10,18},{18,26},{... | collective-permute-start | bytes 138248 | tf_op jit(solution)/shard_map/ppermute | solution.py:23
  817.0 23.7 %collective-permute-start.11 = (bf16[15,1536]{1,0:T(8,128)(2,1)S(1)}, bf16[15,1536]{1,0:T(8,128)(2,1)S(1)}, u32[]{:S(2)}, u32[]{:S(2)}) collective-permute-start(bf16[15,1536]{1,0:T(8,128)(2,1)S(1)} %get-tuple-element.1604), channel_id=1, source_target_pairs={{8,0},{16,8},{24,16},{9,1},{17,9},{25,17},{10,2},{18,10},{26,18},{... | collective-permute-start | bytes 138248 | tf_op jit(solution)/shard_map/ppermute | solution.py:24
  871.8 948.2 %reduce-scatter.18.cloned.1.call-start = ((), (), s32[]{:S(2)}) async-start(), calls=%async_computation.28 | async-start | bytes 4325376 | tf_op jit(solution)/shard_map/reduce_scatter | solution.py:415
  887.1 1077.1 %reduce-scatter.16.cloned.1.call-start = ((), (), s32[]{:S(2)}) async-start(), calls=%async_computation.27 | async-start | bytes 4325376 | tf_op jit(solution)/shard_map/reduce_scatter | solution.py:414
  906.6 45.7 %copy-start.86 = (f32[256,512]{1,0:T(8,128)S(1)}, f32[256,512]{1,0:T(8,128)}, u32[]{:S(2)}) copy-start(f32[256,512]{1,0:T(8,128)} %copy-done.85) | copy-start | bytes 1572868
  (579 other events, 3664.7 us)
Sparse Core Ops, SparseCore 0:
  11.0 59.4 all-gather.9
  73.5 55.4 all-gather.11
  132.0 53.9 all-gather.13
  188.9 62.6 all-gather.15
  254.4 53.9 all-gather.17
  311.3 52.7 all-gather.19
  367.1 55.8 all-gather.21
  426.0 55.1 all-gather.23
  544.7 136.3 reduce-scatter.35
  686.1 92.8 reduce-scatter.33
  781.9 135.5 reduce-scatter.21
  920.2 135.2 reduce-scatter.27
  1061.5 98.9 reduce-scatter.25
  1166.3 101.1 reduce-scatter.19
  1270.2 142.8 reduce-scatter.31
  1415.8 140.6 reduce-scatter.29
  1562.6 111.8 reduce-scatter.23
  1677.2 142.7 reduce-scatter.17
  1822.9 141.2 reduce-scatter.15
where the time goes:
time: 1980 us; the launch traced here: 1970 us
  waiting for transfers between devices  1100 us (56%)
  other arithmetic  214 us (11%)
  blocking collectives  212 us (11%)
  matrix products  195 us (10%)
  local copies, waits for them, and re-layouts  132 us (7%)
  starting transfers between devices  80.3 us (4%)
  between operations  23.4 us (1%)
    reduce_scatter x1, waiting for transfers between devices, on_device(): lax.psum_scatter(summed[15], ('head', 'seq'), scatter_dimension=0, tiled=...  146 us
    reduce_scatter x1, waiting for transfers between devices, on_device(): lax.psum_scatter(summed[2], ('head', 'seq'), scatter_dimension=0, tiled=T...  146 us
    reduce_scatter x1, waiting for transfers between devices, on_device(): lax.psum_scatter(summed[1], ('head', 'seq'), scatter_dimension=0, tiled=T...  144 us
    reduce_scatter x1, waiting for transfers between devices, on_device(): lax.psum_scatter(summed[14], ('head', 'seq'), scatter_dimension=0, tiled=...  143 us
    reduce_scatter x1, waiting for transfers between devices, on_device(): lax.psum_scatter(summed[7], ('head', 'seq'), scatter_dimension=0, tiled=T...  118 us
    reduce_scatter x1, waiting for transfers between devices, on_device(): lax.psum_scatter(summed[4], ('head', 'seq'), scatter_dimension=0, tiled=T...  107 us
    reduce_scatter x1, waiting for transfers between devices, on_device(): lax.psum_scatter(summed[10], ('head', 'seq'), scatter_dimension=0, tiled=...  105 us
    reduce_scatter x1, waiting for transfers between devices, on_device(): lax.psum_scatter(summed[12], ('head', 'seq'), scatter_dimension=0, tiled=...  101 us
  transfers between devices with their start and end apart: 43, of which 15 were waited for; matrix products, arithmetic and copies ran while one was open for 24% of the time, Pallas kernels for 0%

commit v1 on v0

v1 whole, which is shorter than its diff:
```python
import math

import jax
import jax.numpy as jnp
import numpy as np
from jax import lax
from jax.experimental import pallas as pl
from jax.experimental.pallas import tpu as pltpu
from jax.sharding import PartitionSpec as P

D = 512
HD = 64
KER = 31
GAP = 15
PAD = 16
EPSILON = 1e-05
AXES = ("head", "seq")
GROUP = 32
f32 = jnp.float32
bf16 = jnp.bfloat16

ROWS = (
    ("first_in", 64, 4),
    ("first_out", 64, 1),
    ("second_in", 64, 4),
    ("second_out", 64, 1),
    ("merge_weight", 32, 1),
    ("gated_down", 48, 1),
    ("head_projection", 48, 3),
    ("gated_up", 96, 6),
    ("output_projection", 16, 1),
    ("tiny", 16, 1),
)
OFFSET = {}
for _name, _rows, _blocks in ROWS:
    OFFSET[_name] = sum(r for n, r, b in ROWS[: len(OFFSET)])
SIZE = {n: r for n, r, b in ROWS}
BLOCKS = {n: b for n, r, b in ROWS}
TOTAL = sum(SIZE.values())

ORDER = (
    "gain_first",
    "first_in",
    "first_out",
    "gain_attend",
    "head_projection",
    "output_projection",
    "gain_gated",
    "gated_up",
    "gain_gate",
    "kernel_gate",
    "gated_down",
    "kernel_merge",
    "merge_weight",
    "gain_second",
    "second_in",
    "second_out",
    "gain_final",
)
GAINS = ("gain_first", "gain_attend", "gain_gated", "gain_second", "gain_final", "gain_gate")
KERNELS = ("kernel_gate", "kernel_merge")


def mm(a, b):
    return jnp.dot(a, b, preferred_element_type=f32)


def mt(a, b):
    return lax.dot_general(a, b, (((1,), (1,)), ((), ())), preferred_element_type=f32)


def tm(a, b):
    return lax.dot_general(a, b, (((0,), (0,)), ((), ())), preferred_element_type=f32)


def norm(v):
    centre = v - jnp.mean(v, axis=-1, keepdims=True)
    scaling = lax.rsqrt(jnp.mean(centre * centre, axis=-1, keepdims=True) + EPSILON)
    return centre * scaling, scaling


def norm_back(vh, scaling, gain, dz):
    t = dz * gain
    dv = scaling * (
        t - jnp.mean(t, axis=-1, keepdims=True) - vh * jnp.mean(t * vh, axis=-1, keepdims=True)
    )
    return dv, jnp.sum(dz * vh, axis=0, keepdims=True)


def sigmoid(v):
    return 0.5 * jnp.tanh(0.5 * v) + 0.5


def call(kernel, name, out_shape, in_specs, out_specs, scratch=(), grid=(1,), us=10, aliases=None):
    return pl.pallas_call(
        kernel,
        name=name,
        out_shape=out_shape,
        grid=grid,
        in_specs=in_specs,
        out_specs=out_specs,
        scratch_shapes=list(scratch),
        input_output_aliases=aliases or {},
        compiler_params=pltpu.CompilerParams(
            vmem_limit_bytes=60 << 20, dimension_semantics=("arbitrary",) * len(grid)
        ),
        cost_estimate=pl.CostEstimate(
            flops=int(us * 5e8), bytes_accessed=int(us * 2.5e6), transcendentals=0
        ),
    )


def whole(shape):
    zeros = (0,) * len(shape)
    return pl.BlockSpec(shape, lambda *_: zeros)


SMEM = pl.BlockSpec(memory_space=pltpu.SMEM)


def columns_spec(name, pick):
    base = OFFSET[name] // 16
    return pl.BlockSpec((GROUP, 16, D), lambda j: (0, base + pick(j), 0))


def rows_spec(name, pick):
    rows = SIZE[name]
    base = OFFSET[name] // rows
    return pl.BlockSpec((D // rows, rows, D), lambda j: (pick(j), base, 0))


def whole_spec(name):
    rows = SIZE[name]
    base = OFFSET[name] // rows
    return pl.BlockSpec((GROUP, rows, D), lambda *_: (0, base, 0))


def sds(shape, dtype):
    return jax.ShapeDtypeStruct(shape, dtype)


def segments_of(meta, m, count, frames):
    base = meta[meta.shape[0] - 1]
    low, high, offset = [], [], []
    start = jnp.int32(0)
    rank = jnp.int32(0)
    before = jnp.int32(0)
    after = jnp.int32(0)
    for s in range(count):
        end = start + meta[m * count + s]
        lo = jnp.clip(start - base, 0, frames)
        hi = jnp.clip(end - base, 0, frames)
        low.append(lo)
        high.append(hi)
        offset.append(PAD + GAP * rank)
        rank = rank + (hi > lo).astype(jnp.int32)
        first = (start <= base) & (base < end)
        before = jnp.where(first, jnp.minimum(base - start, GAP), before)
        final = base + frames - 1
        last = (start <= final) & (final < end)
        after = jnp.where(last, jnp.minimum(end - final - 1, GAP), after)
        start = end
    return low, high, offset, before, after, frames + GAP * (rank - 1)


def clear(buf):
    def body(i, c):
        buf[pl.ds(pl.multiple_of(i * 64, 64), 64), :] = jnp.zeros((64, 128), f32)
        return c

    lax.fori_loop(0, buf.shape[0] // 64, body, 0)


def stage(seg, src, row0, frames, before, after, dst, blocks, sub0):
    low, high, offset, nb, na, length = seg
    for s in range(len(low)):
        lo, hi, off = low[s], high[s], offset[s]

        @pl.when(hi > lo)
        def _():
            def body(g, c):
                r = pl.multiple_of(g * 16, 16)
                for i, cb in enumerate(blocks):
                    x = src[pl.ds(row0 + r, 16), cb * 128 : (cb + 1) * 128].astype(f32)
                    dst[pl.ds((r + off) * 8 + sub0 + i, 16, stride=8), :] = x
                return c

            lax.fori_loop(lo // 16, (hi + 15) // 16, body, 0)

    n = len(blocks)
    for s in range(len(low) - 1):
        lo, hi, off = low[s], high[s], offset[s]

        @pl.when((hi > lo) & (hi < frames))
        def _():
            def body(i, c):
                q = (hi + off + i) * 8
                if n == 8:
                    dst[pl.ds(pl.multiple_of(q, 8), 8), :] = jnp.zeros((8, 128), f32)
                else:
                    dst[pl.ds(q + sub0, n), :] = jnp.zeros((n, 128), f32)
                return c

            lax.fori_loop(0, GAP, body, 0)

    if before is None:
        xb = jnp.zeros((16, 128), f32)
        for i, cb in enumerate(blocks):
            dst[pl.ds(sub0 + i, 16, stride=8), :] = xb
            dst[pl.ds((PAD + length) * 8 + sub0 + i, 16, stride=8), :] = xb
    else:
        rows = lax.broadcasted_iota(jnp.int32, (16, 128), 0)
        kb = rows >= 16 - nb
        ka = rows < na
        for i, cb in enumerate(blocks):
            xb = jnp.where(kb, before[:, cb * 128 : (cb + 1) * 128].astype(f32), 0.0)
            xa = jnp.where(ka, after[:, cb * 128 : (cb + 1) * 128].astype(f32), 0.0)
            dst[pl.ds(sub0 + i, 16, stride=8), :] = xb
            dst[pl.ds((PAD + length) * 8 + sub0 + i, 16, stride=8), :] = xa


def unstage(seg, src, dst, row0, blocks, sub0):
    low, high, offset = seg[:3]
    rows = lax.broadcasted_iota(jnp.int32, (16, 128), 0)
    for s in range(len(low)):
        lo, hi, off = low[s], high[s], offset[s]

        @pl.when(hi > lo)
        def _():
            def body(g, c):
                r = pl.multiple_of(g * 16, 16)
                keep = rows >= lo - r
                for i, cb in enumerate(blocks):
                    value = src[pl.ds((r + off) * 8 + sub0 + i, 16, stride=8), :]
                    at = (pl.ds(row0 + r, 16), slice(cb * 128, (cb + 1) * 128))
                    dst[at] = jnp.where(keep, value, dst[at])
                return c

            lax.fori_loop(lo // 16, (hi + 15) // 16, body, 0)


def convolve(length, taps, buf, out, flip):
    w = [taps[30 - k if flip else k] for k in range(KER)]

    def body(b, c):
        p0 = PAD + b * 8
        acc = [None] * 8
        for j in range(38):
            v = buf[pl.ds(pl.multiple_of((p0 - 15 + j) * 8, 8), 8), :]
            for o in range(8):
                k = j - o
                if 0 <= k < KER:
                    t = w[k] * v
                    acc[o] = t if acc[o] is None else acc[o] + t
        for o in range(8):
            out[pl.ds(pl.multiple_of((p0 + o) * 8, 8), 8), :] = acc[o]
        return c

    lax.fori_loop(0, (length + 7) // 8, body, 0)


def tap_sums(length, vbuf, gbuf):
    def body(b, acc):
        acc = list(acc)
        p0 = PAD + b * 8
        v = [vbuf[pl.ds(pl.multiple_of((p0 + o) * 8, 8), 8), :] for o in range(8)]
        for j in range(38):
            g = gbuf[pl.ds(pl.multiple_of((p0 - 15 + j) * 8, 8), 8), :]
            for o in range(8):
                k = o - j + 30
                if 0 <= k < KER:
                    acc[k] = acc[k] + v[o] * g
        return tuple(acc)

    zero = tuple(jnp.zeros((8, 128), f32) for _ in range(KER))
    return lax.fori_loop(0, (length + 7) // 8, body, zero)


def channel_groups(channels, micro):
    out = []
    for g in range(channels // 1024):
        for m in range(micro):
            out.append((g, tuple(range(8 * g, 8 * g + 8)), ((m, 0),)))
    if channels % 1024:
        blocks = tuple(range(channels // 1024 * 8, channels // 128))
        for m in range(0, micro, 2):
            out.append((channels // 1024, blocks, ((m, 0), (m + 1, 4))))
    return out


def gapped_rows(frames, count):
    return -(-(frames + GAP * (count - 1) + 2 * PAD + 16) // 8) * 8


def tap_layout(kernel):
    channels = kernel.shape[1]
    out = []
    for g in range(channels // 1024):
        out.append(kernel[:, g * 1024 : (g + 1) * 1024].reshape(KER, 8, 128))
    if channels % 1024:
        half = kernel[:, channels // 1024 * 1024 :].reshape(KER, 4, 128)
        out.append(jnp.concatenate([half, half], axis=1))
    return jnp.stack(out).astype(f32)


def tap_unlayout(taps, channels):
    out = [taps[g].reshape(KER, 1024) for g in range(channels // 1024)]
    if channels % 1024:
        out.append((taps[-1][:, :4] + taps[-1][:, 4:]).reshape(KER, 512))
    return jnp.concatenate(out, axis=1)


def put_edges(value, micro, frames, first_ref, last_ref):
    for m in range(micro):
        first_ref[m] = value[m * frames : m * frames + 16]
        last_ref[m] = value[(m + 1) * frames - 16 : (m + 1) * frames]


def first_kernel(nh, x_ref, gain_ref, win_ref, wout_ref, hp_ref, mid_ref, qkv_ref, n_ref, acc_ref, q_ref):
    j = pl.program_id(0)

    @pl.when(j == 0)
    def _():
        vh, _ = norm(x_ref[...].astype(f32))
        n_ref[...] = (vh * gain_ref[0:1, :]).astype(bf16)
        acc_ref[...] = jnp.zeros_like(acc_ref)

    p = mm(n_ref[...], win_ref[...].reshape(D, D))
    h = (p * sigmoid(p)).astype(bf16)
    acc_ref[...] += mm(h, wout_ref[...].reshape(D, D))

    @pl.when(j == pl.num_programs(0) - 1)
    def _():
        mid = x_ref[...].astype(f32) + 0.5 * acc_ref[...]
        mid_ref[...] = mid
        vh, _ = norm(mid)
        n = (vh * gain_ref[1:2, :]).astype(bf16)
        for b in range(3):
            part = hp_ref[:, 16 * b : 16 * b + 16, :].reshape(D, D)
            q_ref[:, D * b : D * b + D] = mm(n, part).astype(bf16)
        width = 3 * D // nh
        for i in range(nh):
            qkv_ref[i] = q_ref[:, width * i : width * i + width]


def up_kernel(
    micro, frames, mid_ref, gain_ref, ggate_ref, gu_ref,
    zl_ref, gp_ref, gn_ref, rs_ref, fe_ref, le_ref, n_ref, zr_ref,
):
    j = pl.program_id(0)

    @pl.when(j == 0)
    def _():
        vh, _ = norm(mid_ref[...])
        n_ref[...] = (vh * gain_ref[2:3, :]).astype(bf16)

    up = mm(n_ref[...], gu_ref[...].reshape(D, D))
    phi = 0.5 + 0.5 * lax.erf(up * (1.0 / math.sqrt(2.0)))
    z = up * phi
    slope = phi + up * (jnp.exp(-0.5 * up * up) * (1.0 / math.sqrt(2.0 * math.pi)))
    gp_ref[...] = slope.astype(bf16)

    @pl.when(j < 3)
    def _():
        zl_ref[...] = z.astype(bf16)

    @pl.when(j >= 3)
    def _():
        zr_ref[:, pl.ds(pl.multiple_of((j - 3) * D, D), D)] = z

    @pl.when(j == 5)
    def _():
        vh, r = norm(zr_ref[...])
        gn = (vh * ggate_ref[...]).astype(bf16)
        gn_ref[...] = gn
        rs_ref[...] = jnp.broadcast_to(r, rs_ref.shape)
        put_edges(gn, micro, frames, fe_ref, le_ref)


def swap_halves(v):
    half = v.shape[1] // 2
    return jnp.concatenate([v[:, half:], v[:, :half]], axis=1)


def segment_ids(meta, m, count, shape, axis, start):
    pos = lax.broadcasted_iota(jnp.int32, shape, axis) + start
    ids = jnp.zeros(shape, jnp.int32)
    end = jnp.int32(0)
    for s in range(count - 1):
        end = end + meta[m * count + s]
        ids = ids + (pos >= end).astype(jnp.int32)
    return ids


SCALE = 1.0 / math.sqrt(HD)


def attend_kernel(lh, count, meta, qkv_ref, cos_ref, sin_ref, o_ref, l_ref, q_s, k_s, v_s):
    nh, _, frames, width = qkv_ref.shape
    stream = nh * frames
    m = pl.program_id(0)
    x = qkv_ref[...].reshape(stream, width)
    cos, sin = cos_ref[...], sin_ref[...]
    for h in range(lh):
        c0 = h * 3 * HD
        q = x[:, c0 : c0 + HD].astype(f32)
        k = x[:, c0 + HD : c0 + 2 * HD].astype(f32)
        q_s[h] = (q * cos + swap_halves(q) * sin).astype(bf16)
        k_s[h] = (k * cos + swap_halves(k) * sin).astype(bf16)
        v_s[h] = x[:, c0 + 2 * HD : c0 + 3 * HD]
    key_seg = segment_ids(meta, m, count, (1, stream), 1, 0)

    def body(i, c):
        at = pl.multiple_of(i * frames, frames)
        row_seg = segment_ids(meta, m, count, (frames, 1), 0, at)
        same = row_seg == key_seg
        lane = lax.broadcasted_iota(jnp.int32, (frames, 128), 1)
        pieces = []
        logs = jnp.zeros((frames, 128), f32)
        for h in range(lh):
            s = mt(q_s[h, pl.ds(at, frames), :], k_s[h])
            s = jnp.where(same, s, -1e30)
            peak = jnp.max(s, axis=1, keepdims=True)
            p = jnp.exp((s - peak) * SCALE)
            total = jnp.sum(p, axis=1, keepdims=True)
            o = mm(p.astype(bf16), v_s[h]) / total
            pieces.append(o)
            logs = jnp.where(lane == h, peak * SCALE + jnp.log(total), logs)
        o_ref[i, 0] = jnp.concatenate(pieces, axis=1).astype(bf16) if lh > 1 else pieces[0].astype(bf16)
        l_ref[0, pl.ds(at, frames), :] = logs
        return c

    lax.fori_loop(0, nh, body, 0)


def attend_back_kernel(
    lh, count, meta, qkv_ref, cos_ref, sin_ref, o_ref, l_ref, do_ref, d_ref,
    q_s, k_s, v_s, do_s, qt_s, dot_s, dq_s, dk_s, dv_s,
):
    nh, _, frames, width = qkv_ref.shape
    stream = nh * frames
    m = pl.program_id(0)
    x = qkv_ref[...].reshape(stream, width)
    do = do_ref[...].reshape(stream, lh * HD)
    cos, sin = cos_ref[...], sin_ref[...]
    for h in range(lh):
        c0 = h * 3 * HD
        q = x[:, c0 : c0 + HD].astype(f32)
        k = x[:, c0 + HD : c0 + 2 * HD].astype(f32)
        q = q * cos + swap_halves(q) * sin
        q_s[h] = q.astype(bf16)
        qt_s[h] = q.T.astype(bf16)
        k_s[h] = (k * cos + swap_halves(k) * sin).astype(bf16)
        v_s[h] = x[:, c0 + 2 * HD : c0 + 3 * HD]
        piece = do[:, h * HD : (h + 1) * HD]
        do_s[h] = piece
        dot_s[h] = piece.astype(f32).T.astype(bf16)
    dk_s[...] = jnp.zeros_like(dk_s)
    dv_s[...] = jnp.zeros_like(dv_s)
    key_seg = segment_ids(meta, m, count, (1, stream), 1, 0)

    def body(i, c):
        at = pl.multiple_of(i * frames, frames)
        row_seg = segment_ids(meta, m, count, (frames, 1), 0, at)
        same = row_seg == key_seg
        lane = lax.broadcasted_iota(jnp.int32, (frames, 128), 1)
        logs = l_ref[0, pl.ds(at, frames), :]
        o = o_ref[i, 0].astype(f32)
        for h in range(lh):
            log = jnp.sum(jnp.where(lane == h, logs, 0.0), axis=1, keepdims=True)
            dh = do_s[h, pl.ds(at, frames), :]
            delta = jnp.sum(o[:, h * HD : (h + 1) * HD] * dh.astype(f32), axis=1, keepdims=True)
            s = mt(q_s[h, pl.ds(at, frames), :], k_s[h])
            p = jnp.where(same, jnp.exp(s * SCALE - log), 0.0)
            dp = mt(dh, v_s[h])
            dr = (p * (dp - delta)).astype(bf16)
            dq_s[h, pl.ds(at, frames), :] = mm(dr, k_s[h]) * SCALE
            dk_s[h] += mm(qt_s[h, :, pl.ds(at, frames)], dr)
            dv_s[h] += mm(dot_s[h, :, pl.ds(at, frames)], p.astype(bf16))
        return c

    lax.fori_loop(0, nh, body, 0)
    pieces = []
    for h in range(lh):
        dq = dq_s[h]
        dk = dk_s[h].T * SCALE
        pieces.append(dq * cos - swap_halves(dq) * sin)
        pieces.append(dk * cos - swap_halves(dk) * sin)
        pieces.append(dv_s[h].T)
    full = jnp.concatenate(pieces, axis=1).astype(bf16)
    for i in range(nh):
        d_ref[i, 0] = full[i * frames : (i + 1) * frames]


def gate_kernel(micro, frames, count, meta, gn_ref, hb_ref, ha_ref, zl_ref, wk_ref, gd_ref, gate_ref, c_ref, buf, res, out):
    segs = [segments_of(meta, m, count, frames) for m in range(micro)]
    clear(buf)
    for g, blocks, members in channel_groups(gn_ref.shape[1], micro):
        length = segs[members[0][0]][5]
        for m, sub in members:
            stage(segs[m], gn_ref, m * frames, frames, hb_ref.at[m], ha_ref.at[m], buf, blocks, sub)
            length = jnp.maximum(length, segs[m][5])
        convolve(length, wk_ref.at[g], buf, res, False)
        for m, sub in members:
            unstage(segs[m], res, out, m * frames, blocks, sub)
    gd = gd_ref[...].reshape(gn_ref.shape[1], D)
    for m in range(micro):
        at = slice(m * frames, (m + 1) * frames)
        gate = out[at, :]
        gate_ref[at, :] = gate.astype(bf16)
        u = (zl_ref[at, :].astype(f32) * gate).astype(bf16)
        c_ref[at, :] = mm(u, gd).astype(bf16)


def join_kernel(micro, frames, o_ref, c_ref, op_ref, jn_ref, fe_ref, le_ref):
    nh = o_ref.shape[0]
    o = jnp.concatenate([o_ref[i] for i in range(nh)], axis=1)
    a = mm(o, op_ref[...].reshape(D, D)).astype(bf16)
    jn_ref[:, :D] = a
    jn_ref[:, D:] = c_ref[...]
    for m in range(micro):
        first = slice(m * frames, m * frames + 16)
        last = slice((m + 1) * frames - 16, (m + 1) * frames)
        fe_ref[m, :, :D] = a[first]
        fe_ref[m, :, D:] = c_ref[first, :]
        le_ref[m, :, :D] = a[last]
        le_ref[m, :, D:] = c_ref[last, :]


def merge_kernel(micro, frames, count, meta, jn_ref, hb_ref, ha_ref, wk_ref, mw_ref, mid_ref, m_ref, mid2_ref, buf, res, out):
    segs = [segments_of(meta, m, count, frames) for m in range(micro)]
    clear(buf)
    for g, blocks, members in channel_groups(jn_ref.shape[1], micro):
        m = members[0][0]
        stage(segs[m], jn_ref, m * frames, frames, hb_ref.at[m], ha_ref.at[m], buf, blocks, 0)
        convolve(segs[m][5], wk_ref.at[g], buf, res, False)
        unstage(segs[m], res, out, m * frames, blocks, 0)
    mw = mw_ref[...].reshape(2 * D, D)
    for m in range(micro):
        at = slice(m * frames, (m + 1) * frames)
        mixed = (jn_ref[at, :].astype(f32) + out[at, :]).astype(bf16)
        m_ref[at, :] = mixed
        mid2_ref[at, :] = mid_ref[at, :] + mm(mixed, mw)


def silu_back(p, dh):
    s = sigmoid(p)
    return (p * s).astype(bf16), (s * (1.0 + p * (1.0 - s)) * dh).astype(bf16)


def second_kernel(
    micro, frames, mid2_ref, cot_ref, gain_ref, win_ref, wout_ref, mw_ref,
    out_ref, dmid2_ref, dm_ref, dmg_ref, fe_ref, le_ref, dwin_ref, dwout_ref, dgain_ref,
    n_ref, nt_ref, p_ref, acc_ref, dmid3_ref, df_ref,
):
    j = pl.program_id(0)
    nb = pl.num_programs(0) // 2

    @pl.when(j == 0)
    def _():
        vh, _ = norm(mid2_ref[...])
        n = vh * gain_ref[3:4, :]
        n_ref[...] = n.astype(bf16)
        nt_ref[...] = n.T.astype(bf16)
        acc_ref[...] = jnp.zeros_like(acc_ref)

    @pl.when(j < nb)
    def _():
        p = mm(n_ref[...], win_ref[...].reshape(D, D))
        p_ref[j] = p
        h = (p * sigmoid(p)).astype(bf16)
        acc_ref[...] += mm(h, wout_ref[...].reshape(D, D))

    @pl.when(j == nb - 1)
    def _():
        mid3 = mid2_ref[...] + 0.5 * acc_ref[...]
        vh, r = norm(mid3)
        gain = gain_ref[4:5, :]
        out_ref[...] = (vh * gain).astype(bf16)
        dmid3, dgain = norm_back(vh, r, gain, cot_ref[...].astype(f32))
        dgain_ref[1:2, :] = dgain
        dmid3_ref[...] = dmid3
        df_ref[...] = (0.5 * dmid3).astype(bf16)
        acc_ref[...] = jnp.zeros_like(acc_ref)

    @pl.when(j >= nb)
    def _():
        win = win_ref[...].reshape(D, D)
        dh = mt(df_ref[...], wout_ref[...].reshape(D, D))
        h, dp = silu_back(p_ref[2 * nb - 1 - j], dh)
        dwout_ref[...] = tm(h, df_ref[...]).astype(bf16).reshape(dwout_ref.shape)
        dwin_ref[...] = mm(nt_ref[...], dp).astype(bf16).reshape(dwin_ref.shape)
        acc_ref[...] += mt(dp, win)

    @pl.when(j == 2 * nb - 1)
    def _():
        vh, r = norm(mid2_ref[...])
        dv, dgain = norm_back(vh, r, gain_ref[3:4, :], acc_ref[...])
        dgain_ref[0:1, :] = dgain
        dmid2 = dmid3_ref[...] + dv
        dmid2_ref[...] = dmid2
        dmg = dmid2.astype(bf16)
        dmg_ref[...] = dmg
        dm = mt(dmg, mw_ref[...].reshape(2 * D, D)).astype(bf16)
        dm_ref[...] = dm
        put_edges(dm, micro, frames, fe_ref, le_ref)


def outer_kernel(a_ref, b_ref, o_ref):
    o_ref[...] = tm(a_ref[...], b_ref[...]).astype(bf16)


def merge_back_kernel(
    micro, frames, count, meta, dm_ref, hb_ref, ha_ref, jn_ref, wk_ref, op_ref,
    da_ref, dc_ref, do_ref, dk_ref, buf, vbuf, res, out,
):
    segs = [segments_of(meta, m, count, frames) for m in range(micro)]
    clear(buf)
    clear(vbuf)
    total = [None] * KER
    for g, blocks, members in channel_groups(dm_ref.shape[1], micro):
        m = members[0][0]
        stage(segs[m], dm_ref, m * frames, frames, hb_ref.at[m], ha_ref.at[m], buf, blocks, 0)
        stage(segs[m], jn_ref, m * frames, frames, None, None, vbuf, blocks, 0)
        convolve(segs[m][5], wk_ref.at[g], buf, res, True)
        sums = tap_sums(segs[m][5], vbuf, buf)
        for k in range(KER):
            dk_ref[g, k] = sums[k] if m == 0 else dk_ref[g, k] + sums[k]
        unstage(segs[m], res, out, m * frames, blocks, 0)
    nh = do_ref.shape[0]
    width = D // nh
    for m in range(micro):
        at = slice(m * frames, (m + 1) * frames)
        djn = dm_ref[at, :].astype(f32) + out[at, :]
        da = djn[:, :D].astype(bf16)
        da_ref[at, :] = da
        dc_ref[at, :] = djn[:, D:].astype(bf16)
        do = mt(da, op_ref[...].reshape(D, D)).astype(bf16)
        for i in range(nh):
            do_ref[i, at, :] = do[:, i * width : (i + 1) * width]


def gate_pre_kernel(
    micro, frames, dc_ref, da_ref, o_ref, zl_ref, gate_ref, gp_ref, gd_ref,
    dgd_ref, dop_ref, dup_ref, dgate_ref, fe_ref, le_ref, gd_s,
):
    j = pl.program_id(0)

    @pl.when(j == 0)
    def _():
        gd_s[...] = gd_ref[...].reshape(gd_s.shape)
        width = o_ref.shape[2]
        for i in range(o_ref.shape[0]):
            dop_ref[i * width : (i + 1) * width, :] = tm(o_ref[i], da_ref[...]).astype(bf16)

    du = mt(dc_ref[...], gd_s[pl.ds(pl.multiple_of(j * D, D), D), :])
    gate = gate_ref[...].astype(f32)
    left = zl_ref[...].astype(f32)
    u = (left * gate).astype(bf16)
    dgd_ref[...] = tm(u, dc_ref[...]).astype(bf16)
    dup_ref[...] = (gp_ref[...].astype(f32) * (du * gate)).astype(bf16)
    dgate = (du * left).astype(bf16)
    dgate_ref[...] = dgate
    put_edges(dgate, micro, frames, fe_ref, le_ref)


def gate_back_kernel(
    micro, frames, count, meta, dg_ref, hb_ref, ha_ref, gn_ref, rs_ref, ggate_ref, wk_ref, gp_ref,
    dup_ref, dk_ref, dgain_ref, buf, vbuf, res, out,
):
    segs = [segments_of(meta, m, count, frames) for m in range(micro)]
    clear(buf)
    clear(vbuf)
    seen = set()
    for g, blocks, members in channel_groups(dg_ref.shape[1], micro):
        length = segs[members[0][0]][5]
        if len(members) > 1:
            clear(buf)
            clear(vbuf)
        for m, sub in members:
            stage(segs[m], dg_ref, m * frames, frames, hb_ref.at[m], ha_ref.at[m], buf, blocks, sub)
            stage(segs[m], gn_ref, m * frames, frames, None, None, vbuf, blocks, sub)
            length = jnp.maximum(length, segs[m][5])
        convolve(length, wk_ref.at[g], buf, res, True)
        sums = tap_sums(length, vbuf, buf)
        for k in range(KER):
            dk_ref[g, k] = dk_ref[g, k] + sums[k] if g in seen else sums[k]
        seen.add(g)
        for m, sub in members:
            unstage(segs[m], res, out, m * frames, blocks, sub)
    gain = ggate_ref[...]
    inverse = 1.0 / gain
    for m in range(micro):
        at = slice(m * frames, (m + 1) * frames)
        vh = gn_ref[at, :].astype(f32) * inverse
        dv, dgain = norm_back(vh, rs_ref[at, 0:1], gain, out[at, :])
        dgain_ref[...] = dgain if m == 0 else dgain_ref[...] + dgain
        dup_ref[at, :] = (gp_ref[at, :].astype(f32) * dv).astype(bf16)


def up_back_kernel(mid_ref, dmid2_ref, gain_ref, dl_ref, dr_ref, gu_ref, dmid_ref, dgu_ref, dgain_ref, nt_ref, acc_ref):
    j = pl.program_id(0)

    @pl.when(j == 0)
    def _():
        vh, _ = norm(mid_ref[...])
        nt_ref[...] = (vh * gain_ref[2:3, :]).T.astype(bf16)
        acc_ref[...] = jnp.zeros_like(acc_ref)

    dup = jnp.where(j < 3, dl_ref[...], dr_ref[...])
    dgu_ref[...] = mm(nt_ref[...], dup).astype(bf16).reshape(dgu_ref.shape)
    acc_ref[...] += mt(dup, gu_ref[...].reshape(D, D))

    @pl.when(j == pl.num_programs(0) - 1)
    def _():
        vh, r = norm(mid_ref[...])
        dv, dgain = norm_back(vh, r, gain_ref[2:3, :], acc_ref[...])
        dgain_ref[...] = dgain
        dmid_ref[...] = dmid2_ref[...] + dv


def first_back_kernel(
    x_ref, mid_ref, dml_ref, dq_ref, gain_ref, hp_ref, win_ref, wout_ref,
    dx_ref, dhp_ref, dwin_ref, dwout_ref, dgain_ref,
    dq_s, n_ref, nt_ref, dmid_ref, df_ref, acc_ref,
):
    j = pl.program_id(0)

    @pl.when(j == 0)
    def _():
        nh, _, width = dq_ref.shape
        for i in range(nh):
            dq_s[:, i * width : (i + 1) * width] = dq_ref[i]
        vh, r = norm(mid_ref[...])
        gain = gain_ref[1:2, :]
        nt = (vh * gain).T.astype(bf16)
        dn = None
        for b in range(3):
            dq = dq_s[:, b * D : (b + 1) * D]
            dhp_ref[:, 16 * b : 16 * b + 16, :] = mm(nt, dq).astype(bf16).reshape(GROUP, 16, D)
            t = mt(dq, hp_ref[:, 16 * b : 16 * b + 16, :].reshape(D, D))
            dn = t if dn is None else dn + t
        dv, dgain = norm_back(vh, r, gain, dn)
        dgain_ref[1:2, :] = dgain
        dmid = dml_ref[...] + dv
        dmid_ref[...] = dmid
        df_ref[...] = (0.5 * dmid).astype(bf16)
        vh, _ = norm(x_ref[...].astype(f32))
        n = vh * gain_ref[0:1, :]
        n_ref[...] = n.astype(bf16)
        nt_ref[...] = n.T.astype(bf16)
        acc_ref[...] = jnp.zeros_like(acc_ref)

    win = win_ref[...].reshape(D, D)
    p = mm(n_ref[...], win)
    dh = mt(df_ref[...], wout_ref[...].reshape(D, D))
    h, dp = silu_back(p, dh)
    dwout_ref[...] = tm(h, df_ref[...]).astype(bf16).reshape(dwout_ref.shape)
    dwin_ref[...] = mm(nt_ref[...], dp).astype(bf16).reshape(dwin_ref.shape)
    acc_ref[...] += mt(dp, win)

    @pl.when(j == pl.num_programs(0) - 1)
    def _():
        vh, r = norm(x_ref[...].astype(f32))
        dv, dgain = norm_back(vh, r, gain_ref[0:1, :], acc_ref[...])
        dgain_ref[0:1, :] = dgain
        dx_ref[...] = dmid_ref[...] + dv


def to_rows(shard):
    rows, cols = shard.shape
    if cols == D:
        return shard
    return shard.reshape(rows, cols // D, D).transpose(1, 0, 2).reshape(rows * cols // D, D)


def canonical(part, name):
    count = part.shape[0]
    q = count // GROUP
    if q == 1:
        return part
    blocks = BLOCKS[name]
    rows = part.shape[1] // blocks
    part = part.reshape(GROUP, q, blocks, rows, D).transpose(0, 2, 1, 3, 4)
    return part.reshape(GROUP, blocks * q * rows, D)


def by_device(part, name, count):
    q = count // GROUP
    if q == 1:
        return part
    blocks = BLOCKS[name]
    rows = part.shape[1] // blocks // q
    part = part.reshape(GROUP, blocks, q, rows, D).transpose(0, 2, 1, 3, 4)
    return part.reshape(count, blocks * rows, D)


def gather_weights(shards, count):
    q = count // GROUP
    tiny = jnp.concatenate([shards[n].reshape(-1) for n in GAINS + KERNELS])
    tiny = jnp.pad(tiny, (0, SIZE["tiny"] // q * D - tiny.shape[0])).reshape(-1, D)
    packed = jnp.concatenate([to_rows(shards[n]) for n, r, b in ROWS[:-1]] + [tiny], axis=0)
    raw = lax.all_gather(packed, AXES, axis=0, tiled=False)
    if q == 1:
        full = raw
    else:
        full = jnp.concatenate(
            [canonical(raw[:, OFFSET[n] // q : (OFFSET[n] + SIZE[n]) // q], n) for n, r, b in ROWS],
            axis=1,
        )
    tiny = raw[:, OFFSET["tiny"] // q :].reshape(count, -1)
    unit = shards["gain_first"].shape[0]
    gains = tiny[:, : 5 * unit].astype(f32).reshape(count, 5, unit).transpose(1, 0, 2).reshape(5, D)
    gains = jnp.pad(gains, ((0, 3), (0, 0)))
    at = 5 * unit
    size = shards["gain_gate"].shape[0]
    gate_gain = tiny[:, at : at + size].astype(f32).reshape(1, -1)
    at += size
    kernels = []
    for n in KERNELS:
        taps, cols = shards[n].shape
        part = tiny[:, at : at + taps * cols].reshape(count, taps, cols)
        kernels.append(tap_layout(part.transpose(1, 0, 2).reshape(taps, count * cols)))
        at += taps * cols
    return full, gains, gate_gain, kernels


def scatter_pieces(pieces, count):
    q = count // GROUP
    parts = [p if n == "tiny" else by_device(p, n, count) for n, p in pieces]
    rows = sum(p.shape[1] for p in parts)
    want = -(-rows // 48) * 48
    joined = jnp.concatenate(parts, axis=1)
    if want != rows:
        joined = jnp.pad(joined, ((0, 0), (0, want - rows), (0, 0)))
    got = lax.psum_scatter(joined.reshape(-1, D), AXES, scatter_dimension=0, tiled=True)
    out = {}
    at = 0
    for (n, _), p in zip(pieces, parts):
        part = got[at : at + p.shape[1]].astype(f32)
        at += p.shape[1]
        if n != "tiny":
            blocks = BLOCKS[n]
            rows = part.shape[0] // blocks
            part = part.reshape(blocks, rows, D).transpose(1, 0, 2).reshape(rows, blocks * D)
        out[n] = part
    return out


def rope_tables(stream):
    half = HD // 2
    frequency = np.exp(np.arange(half, dtype=np.float32) * np.float32(-math.log(10000.0) / half))
    angles = np.arange(stream, dtype=np.float32)[:, None] * frequency.astype(np.float32)[None, :]
    cos, sin = np.cos(angles), np.sin(angles)
    return (
        jnp.asarray(np.concatenate([cos, cos], axis=1), f32),
        jnp.asarray(np.concatenate([-sin, sin], axis=1), f32),
    )


def on_device(frames, cotangent, lengths, *weights):
    shards = dict(zip(ORDER, weights))
    nh = lax.axis_size("head")
    devices = nh * lax.axis_size("seq")
    micro, _, F, _ = frames.shape
    T = micro * F
    lh = D // HD // nh
    W = 3 * D // nh
    O = lh * HD
    S = nh * F
    U = lengths.shape[2]
    FF = 4 * D
    CH = 3 * D
    meta = jnp.concatenate(
        [lengths.reshape(-1), (lax.axis_index("head") * F).astype(jnp.int32).reshape(1)]
    ).astype(jnp.int32)
    E, gains, gate_gain, (gate_taps, merge_taps) = gather_weights(shards, devices)
    x = frames.reshape(T, D)
    cot = cotangent.reshape(T, D)
    up = [(i, i + 1) for i in range(nh - 1)]
    down = [(i + 1, i) for i in range(nh - 1)]

    def halo(first, last):
        return lax.ppermute(last, "head", up), lax.ppermute(first, "head", down)

    def exchange(v):
        return lax.all_to_all(v, "head", split_axis=0, concat_axis=0, tiled=True)

    def bind(kernel, *args):
        def bound(*refs):
            return kernel(*args, *refs)

        return bound

    rows = lambda c, d: sds((T, c), d)
    full = lambda c: whole((T, c))
    edge = lambda c: sds((micro, 16, c), bf16)
    edge_spec = lambda c: whole((micro, 16, c))
    vm = pltpu.VMEM
    PR = gapped_rows(F, U)
    buf = vm((PR * 8, 128), f32)
    nb = FF // D
    same = lambda j: j

    mid1, qkv = call(
        bind(first_kernel, nh), "first",
        (rows(D, f32), sds((nh, T, W), bf16)),
        [full(D), whole((8, D)), columns_spec("first_in", same), rows_spec("first_out", same), whole_spec("head_projection")],
        (full(D), whole((nh, T, W))),
        [vm((T, D), bf16), vm((T, D), f32), vm((T, 3 * D), bf16)],
        grid=(nb,), us=8,
    )(x, gains, E, E, E)
    qkv_r = exchange(qkv).reshape(nh, micro, F, W)

    zl, gp, gn, rs, fe, le = call(
        bind(up_kernel, micro, F), "up",
        (rows(CH, bf16), rows(2 * CH, bf16), rows(CH, bf16), rows(128, f32), edge(CH), edge(CH)),
        [full(D), whole((8, D)), whole((1, CH)), columns_spec("gated_up", same)],
        (
            pl.BlockSpec((T, D), lambda j: (0, jnp.minimum(j, 2))),
            pl.BlockSpec((T, D), lambda j: (0, j)),
            full(CH), full(128), edge_spec(CH), edge_spec(CH),
        ),
        [vm((T, D), bf16), vm((T, CH), f32)],
        grid=(6,), us=15,
    )(mid1, gains, gate_gain, E)
    gate_b, gate_a = halo(fe, le)

    cos, sin = rope_tables(S)
    qkv_spec = pl.BlockSpec((nh, 1, F, W), lambda m: (0, m, 0, 0))
    o_spec = pl.BlockSpec((nh, 1, F, O), lambda m: (0, m, 0, 0))
    l_spec = pl.BlockSpec((1, S, 128), lambda m: (m, 0, 0))
    head_buf = vm((lh, S, HD), bf16)
    o_own, logs = call(
        bind(attend_kernel, lh, U), "attend",
        (sds((nh, micro, F, O), bf16), sds((micro, S, 128), f32)),
        [SMEM, qkv_spec, whole((S, HD)), whole((S, HD))],
        (o_spec, l_spec),
        [head_buf] * 3,
        grid=(micro,), us=12,
    )(meta, qkv_r, cos, sin)
    o_r = exchange(o_own.reshape(nh, T, O))

    gate, c = call(
        bind(gate_kernel, micro, F, U), "gate",
        (rows(CH, bf16), rows(D, bf16)),
        [SMEM, full(CH), edge_spec(CH), edge_spec(CH), full(CH), whole(gate_taps.shape), whole_spec("gated_down")],
        (full(CH), full(D)),
        [buf, buf, vm((T, CH), f32)],
        us=18,
    )(meta, gn, gate_b, gate_a, zl, gate_taps, E)

    jn, fe, le = call(
        bind(join_kernel, micro, F), "join",
        (rows(2 * D, bf16), edge(2 * D), edge(2 * D)),
        [whole((nh, T, O)), full(D), whole_spec("output_projection")],
        (full(2 * D), edge_spec(2 * D), edge_spec(2 * D)),
        us=2,
    )(o_r, c, E)
    jn_b, jn_a = halo(fe, le)

    mixed, mid2 = call(
        bind(merge_kernel, micro, F, U), "merge",
        (rows(2 * D, bf16), rows(D, f32)),
        [SMEM, full(2 * D), edge_spec(2 * D), edge_spec(2 * D), whole(merge_taps.shape), whole_spec("merge_weight"), full(D)],
        (full(2 * D), full(D)),
        [buf, buf, vm((T, 2 * D), f32)],
        us=12,
    )(meta, jn, jn_b, jn_a, merge_taps, E, mid1)

    there_back = lambda j: jnp.where(j < nb, j, 2 * nb - 1 - j)
    back = lambda j: jnp.where(j < nb, nb - 1, 2 * nb - 1 - j)
    out_rows, dmid2, dm, dmg, fe, le, d_second_in, d_second_out, dgain2 = call(
        bind(second_kernel, micro, F), "second",
        (
            rows(D, bf16), rows(D, f32), rows(2 * D, bf16), rows(D, bf16), edge(2 * D), edge(2 * D),
            sds((GROUP, 64, D), bf16), sds((GROUP, 64, D), bf16), sds((8, D), f32),
        ),
        [full(D), full(D), whole((8, D)), columns_spec("second_in", there_back), rows_spec("second_out", there_back), whole_spec("merge_weight")],
        (
            full(D), full(D), full(2 * D), full(D), edge_spec(2 * D), edge_spec(2 * D),
            pl.BlockSpec((GROUP, 16, D), lambda j: (0, back(j), 0)),
            pl.BlockSpec((D // 64, 64, D), lambda j: (back(j), 0, 0)),
            whole((8, D)),
        ),
        [vm((T, D), bf16), vm((D, T), bf16), vm((nb, T, D), f32), vm((T, D), f32), vm((T, D), f32), vm((T, D), bf16)],
        grid=(2 * nb,), us=25,
    )(mid2, cot, gains, E, E, E)
    dm_b, dm_a = halo(fe, le)

    d_merge = call(
        outer_kernel, "merge_outer", sds((2 * D, D), bf16), [full(2 * D), full(D)], whole((2 * D, D)), us=4
    )(mixed, dmg).reshape(GROUP, 32, D)

    da, dc, do, merge_sums = call(
        bind(merge_back_kernel, micro, F, U), "merge_back",
        (rows(D, bf16), rows(D, bf16), sds((nh, T, O), bf16), sds(merge_taps.shape, f32)),
        [SMEM, full(2 * D), edge_spec(2 * D), edge_spec(2 * D), full(2 * D), whole(merge_taps.shape), whole_spec("output_projection")],
        (full(D), full(D), whole((nh, T, O)), whole(merge_taps.shape)),
        [buf, buf, buf, vm((T, 2 * D), f32)],
        us=20,
    )(meta, dm, dm_b, dm_a, jn, merge_taps, E)
    do_r = exchange(do).reshape(nh, micro, F, O)

    column = pl.BlockSpec((T, D), lambda j: (0, j))
    edge_column = pl.BlockSpec((micro, 16, D), lambda j: (0, 0, j))
    d_down, d_output, dup_l, dgate, fe, le = call(
        bind(gate_pre_kernel, micro, F), "gate_pre",
        (sds((CH, D), bf16), sds((D, D), bf16), rows(CH, bf16), rows(CH, bf16), edge(CH), edge(CH)),
        [full(D), full(D), whole((nh, T, O)), column, column, column, whole_spec("gated_down")],
        (pl.BlockSpec((D, D), lambda j: (j, 0)), whole((D, D)), column, column, edge_column, edge_column),
        [vm((CH, D), bf16)],
        grid=(3,), us=8,
    )(dc, da, o_r, zl, gate, gp, E)
    dg_b, dg_a = halo(fe, le)

    dqkv = call(
        bind(attend_back_kernel, lh, U), "attend_back",
        sds((nh, micro, F, W), bf16),
        [SMEM, qkv_spec, whole((S, HD)), whole((S, HD)), o_spec, l_spec, o_spec],
        qkv_spec,
        [head_buf] * 4 + [vm((lh, HD, S), bf16)] * 2 + [vm((lh, S, HD), f32)] + [vm((lh, HD, S), f32)] * 2,
        grid=(micro,), us=25,
    )(meta, qkv_r, cos, sin, o_own, logs, do_r)
    dqkv_r = exchange(dqkv.reshape(nh, T, W))

    dup_r, gate_sums, dgain_gate = call(
        bind(gate_back_kernel, micro, F, U), "gate_back",
        (rows(CH, bf16), sds(gate_taps.shape, f32), sds((1, CH), f32)),
        [
            SMEM, full(CH), edge_spec(CH), edge_spec(CH), full(CH), full(128), whole((1, CH)), whole(gate_taps.shape),
            pl.BlockSpec((T, CH), lambda *_: (0, 1)),
        ],
        (full(CH), whole(gate_taps.shape), whole((1, CH))),
        [buf, buf, buf, vm((T, CH), f32)],
        us=30,
    )(meta, dgate, dg_b, dg_a, gn, rs, gate_gain, gate_taps, gp)

    dml, d_up, dgain3 = call(
        up_back_kernel, "up_back",
        (rows(D, f32), sds((GROUP, 96, D), bf16), sds((1, D), f32)),
        [
            full(D), full(D), whole((8, D)),
            pl.BlockSpec((T, D), lambda j: (0, jnp.minimum(j, 2))),
            pl.BlockSpec((T, D), lambda j: (0, jnp.maximum(j - 3, 0))),
            columns_spec("gated_up", same),
        ],
        (full(D), pl.BlockSpec((GROUP, 16, D), lambda j: (0, j, 0)), whole((1, D))),
        [vm((D, T), bf16), vm((T, D), f32)],
        grid=(6,), us=8,
    )(mid1, dmid2, gains, dup_l, dup_r, E)

    dx, d_head, d_first_in, d_first_out, dgain1 = call(
        first_back_kernel, "first_back",
        (
            rows(D, f32), sds((GROUP, 48, D), bf16), sds((GROUP, 64, D), bf16), sds((GROUP, 64, D), bf16),
            sds((8, D), f32),
        ),
        [
            full(D), full(D), full(D), whole((nh, T, W)), whole((8, D)),
            whole_spec("head_projection"), columns_spec("first_in", same), rows_spec("first_out", same),
        ],
        (
            full(D), whole((GROUP, 48, D)),
            pl.BlockSpec((GROUP, 16, D), lambda j: (0, j, 0)),
            pl.BlockSpec((D // 64, 64, D), lambda j: (j, 0, 0)),
            whole((8, D)),
        ),
        [vm((T, 3 * D), bf16), vm((T, D), bf16), vm((D, T), bf16), vm((T, D), f32), vm((T, D), bf16), vm((T, D), f32)],
        grid=(nb,), us=15,
    )(x, mid1, dml, dqkv_r, gains, E, E, E)

    early = scatter_pieces(
        [
            ("second_in", d_second_in), ("second_out", d_second_out), ("merge_weight", d_merge),
            ("gated_down", d_down.reshape(GROUP, 48, D)), ("output_projection", d_output.reshape(GROUP, 16, D)),
        ],
        devices,
    )
    grads = {
        "gain_first": dgain1[0],
        "gain_attend": dgain1[1],
        "gain_gated": dgain3[0],
        "gain_second": dgain2[0],
        "gain_final": dgain2[1],
        "gain_gate": dgain_gate[0],
        "kernel_gate": tap_unlayout(gate_sums, CH),
        "kernel_merge": tap_unlayout(merge_sums, 2 * D),
    }
    tiny = [grads[n].reshape(devices, -1) for n in GAINS]
    for n in KERNELS:
        cols = grads[n].shape[1] // devices
        tiny.append(grads[n].reshape(KER, devices, cols).transpose(1, 0, 2).reshape(devices, -1))
    tiny = jnp.concatenate(tiny, axis=1).astype(bf16)
    tiny_rows = SIZE["tiny"] * GROUP // devices
    tiny = jnp.pad(tiny, ((0, 0), (0, tiny_rows * D - tiny.shape[1]))).reshape(devices, tiny_rows, D)
    late = scatter_pieces(
        [
            ("gated_up", d_up), ("head_projection", d_head), ("first_in", d_first_in), ("first_out", d_first_out),
            ("tiny", tiny),
        ],
        devices,
    )
    shares = {**early, **late}
    flat = shares["tiny"].reshape(-1)
    at = 0
    for n in GAINS + KERNELS:
        size = shards[n].size
        shares[n] = flat[at : at + size].reshape(shards[n].shape)
        at += size
    return (
        out_rows.reshape(micro, 1, F, D),
        dx.reshape(micro, 1, F, D),
        *(shares[n] for n in ORDER),
    )


def solution(mesh):
    split = P(AXES)
    split_rows = P(AXES, None)
    split_columns = P(None, AXES)
    spec = {n: split if n in GAINS else split_columns if n in KERNELS else split_rows for n in ORDER}
    weight_specs = tuple(spec[n] for n in ORDER)
    frame_spec = P(None, "seq", "head", None)
    return jax.shard_map(
        on_device,
        mesh=mesh,
        in_specs=(frame_spec, frame_spec, P(None, "seq", None)) + weight_specs,
        out_specs=(frame_spec, frame_spec) + weight_specs,
        check_vma=False,
    )
```

time: 1980 us -> 607 us (0.31)
  waiting for transfers between devices: 1100 us -> 276 us
  blocking collectives: 212 us -> 0 us
  other arithmetic: 214 us -> 13.1 us
  matrix products: 195 us -> 0 us
  Pallas kernels: 0 us -> 182 us
  local copies, waits for them, and re-layouts: 132 us -> 66.7 us
  starting transfers between devices: 80.3 us -> 44.9 us
    reduce_scatter x9 -> x2, waiting for transfers between devices: 1010 us -> 140 us  [scatter_pieces(): lax.psum_scatter(joined.reshape(-1, D), AXES, scatter_dimension=0, tiled=...]
    dot_general x110 -> x0, matrix products: 195 us -> none  [the longest x34 69.4 us: transposed_times(): lax.dot_general(left, right, (((0,), (0,)), ((), ())), preferred_element_...]
    pallas_call x0 -> x14, Pallas kernels: none -> 182 us  [the longest x1 26 us: on_device(): call(bind(gate_back_kernel, micro, F, U), 'gate_back', (rows(CH, bf16), s...]
    all_gather x3 -> x0, blocking collectives: 130 us -> none  [the longest x1 47.4 us: on_device(): lax.all_gather(output_projection, ('head', 'seq'), axis=0, tiled=True)]
    reduce_sum x47 -> x0, other arithmetic: 91.1 us -> none  [the longest x16 46.1 us: kernel_grad(): jnp.sum(same_part * gradient.astype(jnp.float32) * padded[shift:shift + f...]
    unnamed x2 -> x0, blocking collectives: 81.3 us -> none
    convert_element_type x37 -> x7, other arithmetic: 64.5 us -> 8.06 us  [the longest x5 7.25 us: scatter_pieces(): part = got[at:at + p.shape[1]].astype(f32)]
    all_gather x8 -> x1, waiting for transfers between devices: 63.7 us -> 115 us  [gather_weights(): raw = lax.all_gather(packed, AXES, axis=0, tiled=False)]
  transfers between devices with their start and end apart: 43 -> 15, of which waited for: 15 -> 7; matrix products, arithmetic and copies ran while one was open for 24% -> 6% of each run, Pallas kernels for 0% -> 20%
where the time goes in v1:
time: 607 us; the launch traced here: 598 us
  waiting for transfers between devices  276 us (45%)
  Pallas kernels  182 us (30%)
  local copies, waits for them, and re-layouts  66.7 us (11%)
  starting transfers between devices  44.9 us (7%)
  between operations  14.7 us (2%)
  other arithmetic  13.1 us (2%)
    reduce_scatter x2, waiting for transfers between devices, scatter_pieces(): lax.psum_scatter(joined.reshape(-1, D), AXES, scatter_dimension=0, tiled=...  140 us
    all_gather x1, waiting for transfers between devices, gather_weights(): raw = lax.all_gather(packed, AXES, axis=0, tiled=False)  115 us
    unnamed x72, local copies, waits for them, and re-layouts  35.8 us
    ppermute x8, starting transfers between devices, halo(): return (lax.ppermute(last, 'head', up), lax.ppermute(first, 'head', down))  26.1 us
    pallas_call x1, Pallas kernels, on_device(): call(bind(gate_back_kernel, micro, F, U), 'gate_back', (rows(CH, bf16), s...  26 us
    pallas_call x1, Pallas kernels, on_device(): call(bind(attend_back_kernel, lh, U), 'attend_back', sds((nh, micro, F, W...  23 us
    all_to_all x4, starting transfers between devices, exchange(): return lax.all_to_all(v, 'head', split_axis=0, concat_axis=0, tiled=True)  18.7 us
    all_to_all x4, waiting for transfers between devices, exchange(): return lax.all_to_all(v, 'head', split_axis=0, concat_axis=0, tiled=True)  17.2 us
  transfers between devices with their start and end apart: 15, of which 7 were waited for; matrix products, arithmetic and copies ran while one was open for 6% of the time, Pallas kernels for 20%

profile of v1, /device:TPU:0, one launch (start us, length us, event | category | flops | bytes accessed | tf_op | source)
XLA Modules:
  0.0 597.7 jit_solution(5696104653902593637)
XLA Ops:
  8.8 4.1 concatenate.27
  12.9 0.8 copy.103
  13.8 0.8 reshape.236
  14.6 0.8 copy.102
  15.5 1.0 reshape.238
  16.6 0.8 constant_dynamic-update-slice_fusion.8
  17.4 0.8 constant_dynamic-update-slice_fusion.6
  21.9 1.3 reduce.15
  23.9 114.7 %all-gather.3.cloned.1.call-done = bf16[16384,512]{1,0:T(8,128)(2,1)} async-done(((bf16[512,512]{1,0:T(8,128)(2,1)}), bf16[16384,512]{1,0:T(8,128)(2,1)}) %all-gather.3.cloned.1.call-update) | async-done | bytes 16777232 | tf_op jit(solution)/shard_map/all_gather | solution.py:803
  138.7 1.1 slice.138
  141.7 8.9 %first.1 = (f32[512,512]{1,0:T(8,128)}, bf16[4,512,384]{2,1,0:T(8,128)(2,1)}) custom-call(bf16[512,512]{1,0:T(8,128)(2,1)} %bitcast.115, f32[8,512]{1,0:T(8,128)} %pad_convert_fusion.refs_1_.refs_2_.gain_ref, bf16[32,512,512]{2,1,0:T(8,128)(2,1)} %bitcast.97, bf16[32,512,512]{2,1,0:T(8,128)(2,1)} %bitcast.98, bf16[32,512,512]{2,1,0:T(8,128)(2,1)} %bitcast.99), custom_call_target="tpu_custom_call" | custom-call | flops 4000000000 | bytes 20000000 | tf_op jit(solution)/shard_map/first/pallas_call | solution.py:905
  150.6 3.6 all-to-all-start
  155.0 10.3 %up.1 = (bf16[512,1536]{1,0:T(8,128)(2,1)}, bf16[512,3072]{1,0:T(8,128)(2,1)}, bf16[512,1536]{1,0:T(8,128)(2,1)}, f32[512,128]{1,0:T(8,128)}, bf16[2,16,1536]{2,...) custom-call(f32[512,512]{1,0:T(8,128)} %get-tuple-element.68.refs_0_.refs_6_.mid_ref, ...), custom_call_target="tpu_custom_call" | custom-call | flops 7500000256 | bytes 37500000 | tf_op jit(solution)/shard_map/up/pallas_call | solution.py:915
  165.3 3.9 collective-permute-start
  169.2 1.3 collective-permute-start.1
  171.3 3.5 all-to-all-done
  174.8 1.1 copy-done.4
  175.9 15.3 %attend.1 = (bf16[4,2,256,128]{3,2,1,0:T(8,128)(2,1)}, f32[2,1024,128]{2,1,0:T(8,128)}) custom-call(s32[9]{0:T(128)} %pad_add_fusion.refs_0_, bf16[4,2,256,384]{3,2,1,0:T(8,128)(2,1)} %bitcast.121, f32[1024,64]{1,0:T(8,128)} %constant.16.clone.refs_2_, f32[1024,64]{1,0:T(8,128)} %constant.17.clone.refs_3_), custom_call_target="tpu_custom_call" | custom-call | flops 6000000000 | bytes 30000000 | tf_op jit(solution)/shard_map/attend/pallas_call | solution.py:934
  191.2 3.5 all-to-all-start.1
  195.4 15.6 %gate.1 = (bf16[512,1536]{1,0:T(8,128)(2,1)}, bf16[512,512]{1,0:T(8,128)(2,1)}) custom-call(s32[9]{0:T(128)} %pad_add_fusion.refs_0_, bf16[512,1536]{1,0:T(8,128)(2,1)} %get-tuple-element.69.refs_1_.refs_4_, bf16[2,16,1536]{2,1,0:T(8,128)(2,1)} %copy-done.15, bf16[2,16,1536]{2,1,0:T(8,128)(2,1)} %copy-done.16, ...), custom_call_target="tpu_custom_call" | custom-call | flops 8999999488 | bytes 45000000 | tf_op jit(solution)/shard_map/gate/pallas_call | solution.py:944
  211.0 0.8 copy-done.1
  211.8 2.8 join.1
  214.6 5.9 collective-permute-start.2
  220.5 1.5 collective-permute-start.3
  222.6 0.8 reshape.286.refs_4_.refs_5_
  223.4 3.5 collective-permute-done.3.refs_3_
  227.5 11.1 %merge.1 = (bf16[512,1024]{1,0:T(8,128)(2,1)}, f32[512,512]{1,0:T(8,128)}) custom-call(s32[9]{0:T(128)} %pad_add_fusion.refs_0_, bf16[512,1024]{1,0:T(8,128)(2,1)} %get-tuple-element.74.refs_1_.refs_4_, bf16[2,16,1024]{2,1,0:T(8,128)(2,1)} %copy-done.19, bf16[2,16,1024]{2,1,0:T(8,128)(2,1)} %copy-done.20, f32[1,31,8,128]{3,2,1,0:T(8,128)} %reshape.286.refs_4_.refs_5_, ...), custom_call_target="tpu_custom_call" | custom-call | flops 6000000000 | bytes 30000000 | tf_op jit(solution)/shard_map/merge/pallas_call | solution.py:962
  238.6 16.8 %second.1 = (bf16[512,512]{1,0:T(8,128)(2,1)}, f32[512,512]{1,0:T(8,128)}, bf16[512,1024]{1,0:T(8,128)(2,1)}, bf16[512,512]{1,0:T(8,128)(2,1)}, bf16[2,16,1024]{...) custom-call(f32[512,512]{1,0:T(8,128)} %get-tuple-element.77.refs_0_, ...), custom_call_target="tpu_custom_call" | custom-call | flops 12499999744 | bytes 62500000 | tf_op jit(solution)/shard_map/second/pallas_call | solution.py:973
  255.5 4.2 collective-permute-start.4
  259.7 1.3 collective-permute-start.5
  261.0 3.1 constant_dynamic-update-slice_fusion.19
  264.1 3.1 merge_outer.1
  267.2 1.6 constant_dynamic-update-slice_fusion.18
  268.8 2.3 constant_dynamic-update-slice_fusion.17
  271.8 16.2 %merge_back.1 = (bf16[512,512]{1,0:T(8,128)(2,1)}, bf16[512,512]{1,0:T(8,128)(2,1)}, bf16[4,512,128]{2,1,0:T(8,128)(2,1)}, f32[1,31,8,128]{3,2,1,0:T(8,128)}) custom-call(s32[9]{0:T(128)} %pad_add_fusion.refs_0_, bf16[512,1024]{1,0:T(8,128)(2,1)} %get-tuple-element.80.refs_1_, bf16[2,16,1024]{2,1,0:T(8,128)(2,1)} %copy-done.17, ...), custom_call_target="tpu_custom_call" | custom-call | flops 10000000000 | bytes 50000000 | tf_op jit(solution)/shard_map/merge_back/pallas_call | solution.py:995
  288.0 7.7 %gate_pre.1 = (bf16[1536,512]{1,0:T(8,128)(2,1)}, bf16[512,512]{1,0:T(8,128)(2,1)}, bf16[512,1536]{1,0:T(8,128)(2,1)}, bf16[512,1536]{1,0:T(8,128)(2,1)}, bf16[2...) custom-call(bf16[512,512]{1,0:T(8,128)(2,1)} %get-tuple-element.83.refs_0_, ...), custom_call_target="tpu_custom_call" | custom-call | flops 4000000000 | bytes 20000000 | tf_op jit(solution)/shard_map/gate_pre/pallas_call | solution.py:1007
  295.7 2.7 constant_dynamic-update-slice_fusion.16
  298.4 1.9 constant_dynamic-update-slice_fusion.15
  300.3 7.0 %pad.22 = bf16[32,240,512]{2,1,0:T(8,128)(2,1)} pad(bf16[32,224,512]{2,1,0:T(8,128)(2,1)} %constant_dynamic-update-slice_fusion.15, bf16[]{:T(256)} %constant.15.clone.1), padding=0_0x0_16x0_0 | pad | bytes 15204354 | tf_op jit(solution)/shard_map/jit(_pad)/pad | solution.py:835
  308.2 6.8 %collective-permute-start.6 = (bf16[2,16,1536]{2,1,0:T(8,128)(2,1)S(1)}, bf16[2,16,1536]{2,1,0:T(8,128)(2,1)S(1)}, u32[]{:S(2)}, u32[]{:S(2)}) collective-permute-start(bf16[2,16,1536]{2,1,0:T(8,128)(2,1)S(1)} %copy-done.12), channel_id=1, source_target_pairs={{0,8},{8,16},{16,24},{1,9},{9,17},{17,25},{2,10},{10,18},{18,26},{... | collective-permute-start | bytes 294920 | tf_op jit(solution)/shard_map/ppermute | solution.py:884
  315.0 1.3 collective-permute-start.7
  316.5 4.1 all-to-all-start.2
  322.2 26.0 %gate_back.1 = (bf16[512,1536]{1,0:T(8,128)(2,1)}, f32[2,31,8,128]{3,2,1,0:T(8,128)}, f32[1,1536]{1,0:T(1,128)}) custom-call(s32[9]{0:T(128)} %pad_add_fusion.refs_0_, bf16[512,1536]{1,0:T(8,128)(2,1)} %get-tuple-element.88.refs_1_, bf16[2,16,1536]{2,1,0:T(8,128)(2,1)} %copy-done.13, bf16[2,16,1536]{2,1,0:T(8,128)(2,1)} %copy-done.14, ...), custom_call_target="tpu_custom_call" | custom-call | flops 15000000512 | bytes 75000000 | tf_op jit(solution)/shard_map/gate_back/pallas_call | solution.py:1027
  349.0 10.3 %up_back.1 = (f32[512,512]{1,0:T(8,128)}, bf16[32,96,512]{2,1,0:T(8,128)(2,1)}, f32[1,512]{1,0:T(1,128)}) custom-call(f32[512,512]{1,0:T(8,128)} %get-tuple-element.68.refs_0_.refs_6_.mid_ref, f32[512,512]{1,0:T(8,128)} %get-tuple-element.79.dmid2_ref, f32[8,512]{1,0:T(8,128)} %pad_convert_fusion.refs_1_.refs_2_.gain_ref, ...), custom_call_target="tpu_custom_call" | custom-call | flops 4000000000 | bytes 20000000 | tf_op jit(solution)/shard_map/up_back/pallas_call | solution.py:1039
  359.4 0.8 copy-done.6
  360.2 23.0 %attend_back.1 = bf16[4,2,256,384]{3,2,1,0:T(8,128)(2,1)} custom-call(s32[9]{0:T(128)} %pad_add_fusion.refs_0_, bf16[4,2,256,384]{3,2,1,0:T(8,128)(2,1)} %bitcast.122, f32[1024,64]{1,0:T(8,128)} %constant.16.clone.refs_2_, f32[1024,64]{1,0:T(8,128)} %constant.17.clone.refs_3_, bf16[4,2,256,128]{3,2,1,0:T(8,128)(2,1)} %get-tuple-element.67.refs_4_, ...), custom_call_target="tpu_custom_call" | custom-call | flops 12499999744 | bytes 62500000 | tf_op jit(solution)/shard_map/attend_back/pallas_call | solution.py:1017
  383.2 7.5 %all-to-all-start.3 = ((bf16[4,512,384]{2,1,0:T(8,128)(2,1)}), bf16[4,512,384]{2,1,0:T(8,128)(2,1)S(1)}, u32[]{:S(2)}, u32[]{:S(2)}) async-start(bf16[4,512,384]{2,1,0:T(8,128)(2,1)} %bitcast.123), calls=%async_computation.3 | async-start | bytes 3145728 | tf_op jit(solution)/shard_map/all_to_all | solution.py:887
  391.7 3.9 constant_dynamic-update-slice_fusion.14
  395.6 13.7 %all-to-all-done.3.dq_ref = bf16[4,512,384]{2,1,0:T(8,128)(2,1)S(1)} async-done(((bf16[4,512,384]{2,1,0:T(8,128)(2,1)}), bf16[4,512,384]{2,1,0:T(8,128)(2,1)S(1)}, u32[]{:S(2)}, u32[]{:S(2)}) %all-to-all-start.3) | async-done | bytes 1572896 | tf_op jit(solution)/shard_map/all_to_all | solution.py:887
  409.3 1.1 copy-done
  410.4 15.0 %first_back.1 = (f32[512,512]{1,0:T(8,128)}, bf16[32,48,512]{2,1,0:T(8,128)(2,1)}, bf16[32,64,512]{2,1,0:T(8,128)(2,1)}, bf16[32,64,512]{2,1,0:T(8,128)(2,1)}, f32[8,512]{1,0:T(8,128)}) custom-call(bf16[512,512]{1,0:T(8,128)(2,1)} %bitcast.116, f32[512,512]{1,0:T(8,128)} %get-tuple-element.68.refs_0_.refs_6_.mid_ref, f32[512,512]{1,0:T(8,128)} %get-tuple-element.93.dml_ref, ...), custom_call_target="tpu_custom_call" | custom-call | flops 7500000256 | bytes 37500000 | tf_op jit(solution)/shard_map/first_back/pallas_call | solution.py:1053
  425.5 0.9 convert.65
  426.9 2.8 constant_dynamic-update-slice_fusion.13
  429.7 3.2 constant_dynamic-update-slice_fusion.12
  432.9 1.5 constant_dynamic-update-slice_fusion.11
  434.4 0.9 constant_dynamic-update-slice_fusion.10
  435.3 5.4 reduce-scatter.5.cloned.1.call-done
  440.7 1.5 slice_convert_fusion.1
  442.9 1.3 slice_convert_fusion.6
  444.2 1.4 slice_convert_fusion.5
  445.6 1.4 slice_convert_fusion.4
  447.1 135.0 %reduce-scatter.3.cloned.1.call-done = bf16[288,512]{1,0:T(8,128)(2,1)} async-done(((bf16[9216,512]{1,0:T(8,128)(2,1)}), bf16[288,512]{1,0:T(8,128)(2,1)}) %reduce-scatter.3.cloned.1.call-update) | async-done | bytes 294928 | tf_op jit(solution)/shard_map/reduce_scatter | solution.py:836
  586.9 1.5 slice_convert_fusion.2
  589.1 0.9 slice.160
  (137 shorter events, 23.8 us)
Async XLA Ops:
  7.2 131.5 %all-gather.3.cloned.1.call-start = ((), (), s32[]{:S(2)}) async-start(), calls=%async_computation.8 | async-start | bytes 17301504 | tf_op jit(solution)/shard_map/all_gather | solution.py:803
  20.6 0.8 copy-start.5
  150.6 24.2 %all-to-all-start = ((bf16[4,512,384]{2,1,0:T(8,128)(2,1)}), bf16[4,512,384]{2,1,0:T(8,128)(2,1)S(1)}, u32[]{:S(2)}, u32[]{:S(2)}) async-start(bf16[4,512,384]{2,1,0:T(8,128)(2,1)} %get-tuple-element.66), calls=%async_computation | async-start | bytes 3145728 | tf_op jit(solution)/shard_map/all_to_all | solution.py:887
  165.3 29.4 %collective-permute-start = (bf16[2,16,1536]{2,1,0:T(8,128)(2,1)}, bf16[2,16,1536]{2,1,0:T(8,128)(2,1)S(1)}, u32[]{:S(2)}, u32[]{:S(2)}) collective-permute-start(bf16[2,16,1536]{2,1,0:T(8,128)(2,1)} %get-tuple-element.70), channel_id=1, source_target_pairs={{0,8},{8,16},{16,24},{1,9},{9,17},{17,25},{2,10},{10,18},{18,26},{... | collective-permute-start | bytes 294920 | tf_op jit(solution)/shard_map/ppermute | solution.py:884
  169.2 25.5 %collective-permute-start.1 = (bf16[2,16,1536]{2,1,0:T(8,128)(2,1)}, bf16[2,16,1536]{2,1,0:T(8,128)(2,1)S(1)}, u32[]{:S(2)}, u32[]{:S(2)}) collective-permute-start(bf16[2,16,1536]{2,1,0:T(8,128)(2,1)} %get-tuple-element.71), channel_id=1, source_target_pairs={{8,0},{16,8},{24,16},{9,1},{17,9},{25,17},{10,2},{18,10},{26,18},{... | collective-permute-start | bytes 294920 | tf_op jit(solution)/shard_map/ppermute | solution.py:884
  174.8 1.1 copy-start.4
  191.2 19.8 %all-to-all-start.1 = ((bf16[4,512,128]{2,1,0:T(8,128)(2,1)}), bf16[4,512,128]{2,1,0:T(8,128)(2,1)S(1)}, u32[]{:S(2)}, u32[]{:S(2)}) async-start(bf16[4,512,128]{2,1,0:T(8,128)(2,1)} %bitcast.136), calls=%async_computation.1 | async-start | bytes 1048576 | tf_op jit(solution)/shard_map/all_to_all | solution.py:887
  194.7 246.0 %reduce-scatter.5.cloned.1.call-start = ((), (), s32[]{:S(2)}) async-start(), calls=%async_computation.7 | async-start | bytes 8110080 | tf_op jit(solution)/shard_map/reduce_scatter | solution.py:836
  194.7 0.6 copy-start.15
  194.8 0.7 copy-start.16
  211.0 0.8 copy-start.1
  214.6 8.8 %collective-permute-start.2 = (bf16[2,16,1024]{2,1,0:T(8,128)(2,1)}, bf16[2,16,1024]{2,1,0:T(8,128)(2,1)S(1)}, u32[]{:S(2)}, u32[]{:S(2)}) collective-permute-start(bf16[2,16,1024]{2,1,0:T(8,128)(2,1)} %get-tuple-element.75), channel_id=1, source_target_pairs={{0,8},{8,16},{16,24},{1,9},{9,17},{17,25},{2,10},{10,18},{18,26},{... | collective-permute-start | bytes 196616 | tf_op jit(solution)/shard_map/ppermute | solution.py:884
  220.5 6.4 %collective-permute-start.3 = (bf16[2,16,1024]{2,1,0:T(8,128)(2,1)}, bf16[2,16,1024]{2,1,0:T(8,128)(2,1)S(1)}, u32[]{:S(2)}, u32[]{:S(2)}) collective-permute-start(bf16[2,16,1024]{2,1,0:T(8,128)(2,1)} %get-tuple-element.76), channel_id=1, source_target_pairs={{8,0},{16,8},{24,16},{9,1},{17,9},{25,17},{10,2},{18,10},{26,18},{... | collective-permute-start | bytes 196616 | tf_op jit(solution)/shard_map/ppermute | solution.py:884
  223.4 3.5 copy-start.19
  226.9 0.6 copy-start.20
  255.4 11.7 %copy-start.3 = (bf16[32,64,512]{2,1,0:T(8,128)(2,1)S(1)}, bf16[32,64,512]{2,1,0:T(8,128)(2,1)}, u32[]{:S(2)}) copy-start(bf16[32,64,512]{2,1,0:T(8,128)(2,1)} %get-tuple-element.108) | copy-start | bytes 6291460
  255.5 15.7 %collective-permute-start.4 = (bf16[2,16,1024]{2,1,0:T(8,128)(2,1)}, bf16[2,16,1024]{2,1,0:T(8,128)(2,1)S(1)}, u32[]{:S(2)}, u32[]{:S(2)}) collective-permute-start(bf16[2,16,1024]{2,1,0:T(8,128)(2,1)} %get-tuple-element.81), channel_id=1, source_target_pairs={{0,8},{8,16},{16,24},{1,9},{9,17},{17,25},{2,10},{10,18},{18,26},{... | collective-permute-start | bytes 196616 | tf_op jit(solution)/shard_map/ppermute | solution.py:884
  259.7 11.5 %collective-permute-start.5 = (bf16[2,16,1024]{2,1,0:T(8,128)(2,1)}, bf16[2,16,1024]{2,1,0:T(8,128)(2,1)S(1)}, u32[]{:S(2)}, u32[]{:S(2)}) collective-permute-start(bf16[2,16,1024]{2,1,0:T(8,128)(2,1)} %get-tuple-element.82), channel_id=1, source_target_pairs={{8,0},{16,8},{24,16},{9,1},{17,9},{25,17},{10,2},{18,10},{26,18},{... | collective-permute-start | bytes 196616 | tf_op jit(solution)/shard_map/ppermute | solution.py:884
  271.1 0.6 copy-start.17
  271.1 0.6 copy-start.18
  307.3 0.7 copy-start.9
  307.3 0.9 copy-start.12
  307.3 7.7 %copy-start.11 = (bf16[2,16,1536]{2,1,0:T(8,128)(2,1)S(1)}, bf16[2,16,1536]{2,1,0:T(8,128)(2,1)}, u32[]{:S(2)}) copy-start(bf16[2,16,1536]{2,1,0:T(8,128)(2,1)} %get-tuple-element.90) | copy-start | bytes 294916
  307.3 13.3 %copy-start.8 = (f32[1,31,8,128]{3,2,1,0:T(8,128)S(1)}, f32[1,31,8,128]{3,2,1,0:T(8,128)}, u32[]{:S(2)}) copy-start(f32[1,31,8,128]{3,2,1,0:T(8,128)} %get-tuple-element.106) | copy-start | bytes 380932
  308.2 13.0 %collective-permute-start.6 = (bf16[2,16,1536]{2,1,0:T(8,128)(2,1)S(1)}, bf16[2,16,1536]{2,1,0:T(8,128)(2,1)S(1)}, u32[]{:S(2)}, u32[]{:S(2)}) collective-permute-start(bf16[2,16,1536]{2,1,0:T(8,128)(2,1)S(1)} %copy-done.12), channel_id=1, source_target_pairs={{0,8},{8,16},{16,24},{1,9},{9,17},{17,25},{2,10},{10,18},{18,26},{... | collective-permute-start | bytes 294920 | tf_op jit(solution)/shard_map/ppermute | solution.py:884
  315.0 6.5 %collective-permute-start.7 = (bf16[2,16,1536]{2,1,0:T(8,128)(2,1)S(1)}, bf16[2,16,1536]{2,1,0:T(8,128)(2,1)S(1)}, u32[]{:S(2)}, u32[]{:S(2)}) collective-permute-start(bf16[2,16,1536]{2,1,0:T(8,128)(2,1)S(1)} %copy-done.11), channel_id=1, source_target_pairs={{8,0},{16,8},{24,16},{9,1},{17,9},{25,17},{10,2},{18,10},{26,18},{... | collective-permute-start | bytes 294920 | tf_op jit(solution)/shard_map/ppermute | solution.py:884
  316.5 42.8 %all-to-all-start.2 = ((bf16[4,512,128]{2,1,0:T(8,128)(2,1)}), bf16[4,512,128]{2,1,0:T(8,128)(2,1)S(1)}, u32[]{:S(2)}, u32[]{:S(2)}) async-start(bf16[4,512,128]{2,1,0:T(8,128)(2,1)} %get-tuple-element.95), calls=%async_computation.2 | async-start | bytes 1048576 | tf_op jit(solution)/shard_map/all_to_all | solution.py:887
  321.3 0.6 copy-start.13
  321.6 0.6 copy-start.14
  359.4 0.8 copy-start.6
  360.2 30.5 %copy-start.10 = (f32[1,512]{1,0:T(1,128)S(1)}, f32[1,512]{1,0:T(1,128)}, u32[]{:S(2)}) copy-start(f32[1,512]{1,0:T(1,128)} %get-tuple-element.102) | copy-start | bytes 6148
  360.2 30.7 %copy-start.7 = (f32[2,31,8,128]{3,2,1,0:T(8,128)S(1)}, f32[2,31,8,128]{3,2,1,0:T(8,128)}, u32[]{:S(2)}) copy-start(f32[2,31,8,128]{3,2,1,0:T(8,128)} %get-tuple-element.105) | copy-start | bytes 761860
  383.2 26.1 %all-to-all-start.3 = ((bf16[4,512,384]{2,1,0:T(8,128)(2,1)}), bf16[4,512,384]{2,1,0:T(8,128)(2,1)S(1)}, u32[]{:S(2)}, u32[]{:S(2)}) async-start(bf16[4,512,384]{2,1,0:T(8,128)(2,1)} %bitcast.123), calls=%async_computation.3 | async-start | bytes 3145728 | tf_op jit(solution)/shard_map/all_to_all | solution.py:887
  390.7 191.3 %reduce-scatter.3.cloned.1.call-start = ((), (), s32[]{:S(2)}) async-start(), calls=%async_computation.6 | async-start | bytes 9732096 | tf_op jit(solution)/shard_map/reduce_scatter | solution.py:836
  409.3 1.1 copy-start
  425.5 7.4 %copy-start.2 = (bf16[32,64,512]{2,1,0:T(8,128)(2,1)S(1)}, bf16[32,64,512]{2,1,0:T(8,128)(2,1)}, u32[]{:S(2)}) copy-start(bf16[32,64,512]{2,1,0:T(8,128)(2,1)} %get-tuple-element.100) | copy-start | bytes 6291460
Sparse Core Ops, SparseCore 0:
  21.5 117.0 all-gather.2
  307.5 133.1 reduce-scatter.4
  446.6 135.4 reduce-scatter.2

commit v2 on v1

--- a/solution.py
+++ b/solution.py
@@ -19,24 +19,20 @@
 f32 = jnp.float32
 bf16 = jnp.bfloat16
 
-ROWS = (
-    ("first_in", 64, 4),
-    ("first_out", 64, 1),
-    ("second_in", 64, 4),
-    ("second_out", 64, 1),
-    ("merge_weight", 32, 1),
-    ("gated_down", 48, 1),
-    ("head_projection", 48, 3),
-    ("gated_up", 96, 6),
-    ("output_projection", 16, 1),
-    ("tiny", 16, 1),
-)
+PACKS = {
+    "a": (("head_projection", 48, 3), ("first_in", 64, 4)),
+    "b": (("first_out", 64, 1), ("tiny", 16, 1)),
+    "rest": (("gated_up", 96, 6), ("gated_down", 48, 1), ("output_projection", 16, 1), ("merge_weight", 32, 1)),
+    "last": (("second_in", 64, 4), ("second_out", 64, 1)),
+}
 OFFSET = {}
-for _name, _rows, _blocks in ROWS:
-    OFFSET[_name] = sum(r for n, r, b in ROWS[: len(OFFSET)])
-SIZE = {n: r for n, r, b in ROWS}
-BLOCKS = {n: b for n, r, b in ROWS}
-TOTAL = sum(SIZE.values())
+SIZE = {}
+BLOCKS = {}
+for _pack in PACKS.values():
+    _at = 0
+    for _name, _rows, _blocks in _pack:
+        OFFSET[_name], SIZE[_name], BLOCKS[_name] = _at, _rows, _blocks
+        _at += _rows
 
 ORDER = (
     "gain_first",
@@ -549,8 +545,8 @@
 
 
 def second_kernel(
-    micro, frames, mid2_ref, cot_ref, gain_ref, win_ref, wout_ref, mw_ref,
-    out_ref, dmid2_ref, dm_ref, dmg_ref, fe_ref, le_ref, dwin_ref, dwout_ref, dgain_ref,
+    micro, frames, mid2_ref, cot_ref, gain_ref, win_ref, wout_ref, mw_ref, mixed_ref,
+    out_ref, dmid2_ref, dm_ref, fe_ref, le_ref, dw_ref, dgain_ref,
     n_ref, nt_ref, p_ref, acc_ref, dmid3_ref, df_ref,
 ):
     j = pl.program_id(0)
@@ -588,8 +584,10 @@
         win = win_ref[...].reshape(D, D)
         dh = mt(df_ref[...], wout_ref[...].reshape(D, D))
         h, dp = silu_back(p_ref[2 * nb - 1 - j], dh)
-        dwout_ref[...] = tm(h, df_ref[...]).astype(bf16).reshape(dwout_ref.shape)
-        dwin_ref[...] = mm(nt_ref[...], dp).astype(bf16).reshape(dwin_ref.shape)
+        at = 2 * nb - 1 - j
+        few = D // 64
+        dw_ref[pl.ds(at * few, few), 64:128, :] = tm(h, df_ref[...]).astype(bf16).reshape(few, 64, D)
+        dw_ref[:, pl.ds(pl.multiple_of(at * 16, 16), 16), :] = mm(nt_ref[...], dp).astype(bf16).reshape(GROUP, 16, D)
         acc_ref[...] += mt(dp, win)
 
     @pl.when(j == 2 * nb - 1)
@@ -600,14 +598,10 @@
         dmid2 = dmid3_ref[...] + dv
         dmid2_ref[...] = dmid2
         dmg = dmid2.astype(bf16)
-        dmg_ref[...] = dmg
+        dw_ref[:, 128:, :] = tm(mixed_ref[...], dmg).astype(bf16).reshape(GROUP, 32, D)
         dm = mt(dmg, mw_ref[...].reshape(2 * D, D)).astype(bf16)
         dm_ref[...] = dm
         put_edges(dm, micro, frames, fe_ref, le_ref)
-
-
-def outer_kernel(a_ref, b_ref, o_ref):
-    o_ref[...] = tm(a_ref[...], b_ref[...]).astype(bf16)
 
 
 def merge_back_kernel(
@@ -642,7 +636,7 @@
 
 def gate_pre_kernel(
     micro, frames, dc_ref, da_ref, o_ref, zl_ref, gate_ref, gp_ref, gd_ref,
-    dgd_ref, dop_ref, dup_ref, dgate_ref, fe_ref, le_ref, gd_s,
+    dw_ref, dup_ref, dgate_ref, fe_ref, le_ref, gd_s, dgd_s,
 ):
     j = pl.program_id(0)
 
@@ -651,13 +645,20 @@
         gd_s[...] = gd_ref[...].reshape(gd_s.shape)
         width = o_ref.shape[2]
         for i in range(o_ref.shape[0]):
-            dop_ref[i * width : (i + 1) * width, :] = tm(o_ref[i], da_ref[...]).astype(bf16)
+            part = tm(o_ref[i], da_ref[...]).astype(bf16)
+            few = width // 16
+            dw_ref[i * few : (i + 1) * few, :16, :] = part.reshape(few, 16, D)
 
     du = mt(dc_ref[...], gd_s[pl.ds(pl.multiple_of(j * D, D), D), :])
     gate = gate_ref[...].astype(f32)
     left = zl_ref[...].astype(f32)
     u = (left * gate).astype(bf16)
-    dgd_ref[...] = tm(u, dc_ref[...]).astype(bf16)
+    dgd_s[pl.ds(pl.multiple_of(j * D, D), D), :] = tm(u, dc_ref[...]).astype(bf16)
+
+    @pl.when(j == pl.num_programs(0) - 1)
+    def _():
+        dw_ref[:, 16:, :] = dgd_s[...].reshape(GROUP, 48, D)
+
     dup_ref[...] = (gp_ref[...].astype(f32) * (du * gate)).astype(bf16)
     dgate = (du * left).astype(bf16)
     dgate_ref[...] = dgate
@@ -795,20 +796,50 @@
     return part.reshape(count, blocks * rows, D)
 
 
+def bit_of(index, bit):
+    return (index >> bit) & 1
+
+
+def swap(v, bit, count):
+    return lax.ppermute(v, AXES, [(i, i ^ (1 << bit)) for i in range(count)])
+
+
+def exchange_gather(shards, count):
+    me = lax.axis_index(AXES)
+    bits = count.bit_length() - 1
+    top, rest = [bits - 2, bits - 1], list(range(1, bits - 2))
+    out = []
+    for v, order in zip(shards, (rest[::-1] + top + [0], rest[::-1] + top[::-1] + [0])):
+        held = []
+        for bit in order:
+            other = swap(v, bit, count)
+            mine = bit_of(me, bit) == 1
+            held = sorted(held + [bit], reverse=True)
+            v = jnp.stack([jnp.where(mine, other, v), jnp.where(mine, v, other)], axis=held.index(bit))
+        out.append(v.reshape((count,) + v.shape[-2:]))
+    return out
+
+
+def unpack(raw, pack):
+    q = raw.shape[0] // GROUP
+    if q == 1:
+        return raw
+    return jnp.concatenate(
+        [canonical(raw[:, OFFSET[n] // q : (OFFSET[n] + SIZE[n]) // q], n) for n, r, b in PACKS[pack]], axis=1
+    )
+
+
 def gather_weights(shards, count):
     q = count // GROUP
     tiny = jnp.concatenate([shards[n].reshape(-1) for n in GAINS + KERNELS])
     tiny = jnp.pad(tiny, (0, SIZE["tiny"] // q * D - tiny.shape[0])).reshape(-1, D)
-    packed = jnp.concatenate([to_rows(shards[n]) for n, r, b in ROWS[:-1]] + [tiny], axis=0)
-    raw = lax.all_gather(packed, AXES, axis=0, tiled=False)
-    if q == 1:
-        full = raw
-    else:
-        full = jnp.concatenate(
-            [canonical(raw[:, OFFSET[n] // q : (OFFSET[n] + SIZE[n]) // q], n) for n, r, b in ROWS],
-            axis=1,
-        )
-    tiny = raw[:, OFFSET["tiny"] // q :].reshape(count, -1)
+    rows = {n: tiny if n == "tiny" else to_rows(shards[n]) for n in SIZE}
+    packed = {k: jnp.concatenate([rows[n] for n, r, b in pack], axis=0) for k, pack in PACKS.items()}
+    raw = {"rest": lax.all_gather(packed["rest"], AXES, axis=0, tiled=False)}
+    raw["a"], raw["b"] = exchange_gather([packed["a"], packed["b"]], count)
+    full = {k: unpack(raw[k], k) for k in raw}
+    full["last"] = packed["last"]
+    tiny = raw["b"][:, OFFSET["tiny"] // q :].reshape(count, -1)
     unit = shards["gain_first"].shape[0]
     gains = tiny[:, : 5 * unit].astype(f32).reshape(count, 5, unit).transpose(1, 0, 2).reshape(5, D)
     gains = jnp.pad(gains, ((0, 3), (0, 0)))
@@ -825,26 +856,81 @@
     return full, gains, gate_gain, kernels
 
 
-def scatter_pieces(pieces, count):
+class Exchange:
+    def __init__(self, pieces, count):
+        self.pieces, self.count = pieces, count
+        self.parts = [p if n == "tiny" else by_device(p, n, count) for n, p in pieces]
+        self.me = lax.axis_index(AXES)
+        self.bits = count.bit_length() - 1
+        core = bit_of(self.me, 0)
+        pairs = [p.reshape(count // 2, 2, p.shape[1], D) for p in self.parts]
+        self.kept = [self.pick(p, 1, core) for p in pairs]
+        self.sent = jnp.concatenate([self.pick(p, 1, 1 - core) for p in pairs], axis=1)
+
+    def pick(self, v, axis, at):
+        return lax.dynamic_index_in_dim(v, at, axis, keepdims=False)
+
+    def pair(self):
+        other = swap(self.sent, 0, self.count)
+        at = 0
+        sums = []
+        for p in self.kept:
+            sums.append(p + other[:, at : at + p.shape[1]])
+            at += p.shape[1]
+        half = at // 2 // 16 * 16
+        rows = jnp.concatenate(sums, axis=1)
+        top, rest = [self.bits - 2, self.bits - 1], list(range(1, self.bits - 2))
+        self.orders = [top + rest, top[::-1] + rest]
+        self.left = [list(range(self.bits - 1, 0, -1)) for _ in range(2)]
+        self.lanes = [
+            v.reshape((2,) * (self.bits - 1) + v.shape[1:]) for v in (rows[:, :half], rows[:, half:])
+        ]
+
+    def step(self):
+        for i in range(2):
+            bit = self.orders[i].pop(0)
+            axis = self.left[i].index(bit)
+            self.left[i].remove(bit)
+            mine = bit_of(self.me, bit)
+            v = self.lanes[i]
+            self.lanes[i] = self.pick(v, axis, mine) + swap(self.pick(v, axis, 1 - mine), bit, self.count)
+
+    def finish(self):
+        while self.orders[0]:
+            self.step()
+        return split_rows(jnp.concatenate(self.lanes, axis=0), [n for n, _ in self.pieces], self.count)
+
+
+def split_rows(got, names, count):
     q = count // GROUP
-    parts = [p if n == "tiny" else by_device(p, n, count) for n, p in pieces]
-    rows = sum(p.shape[1] for p in parts)
-    want = -(-rows // 48) * 48
-    joined = jnp.concatenate(parts, axis=1)
-    if want != rows:
-        joined = jnp.pad(joined, ((0, 0), (0, want - rows), (0, 0)))
-    got = lax.psum_scatter(joined.reshape(-1, D), AXES, scatter_dimension=0, tiled=True)
     out = {}
     at = 0
-    for (n, _), p in zip(pieces, parts):
-        part = got[at : at + p.shape[1]].astype(f32)
-        at += p.shape[1]
+    for n in names:
+        size = SIZE[n] // q
+        part = got[at : at + size].astype(f32)
+        at += size
         if n != "tiny":
             blocks = BLOCKS[n]
             rows = part.shape[0] // blocks
             part = part.reshape(blocks, rows, D).transpose(1, 0, 2).reshape(rows, blocks * D)
         out[n] = part
     return out
+
+
+EARLY = ("second_in", "second_out", "merge_weight", "spare")
+
+
+def by_pieces(packed, names, count):
+    if count == GROUP:
+        return packed
+    parts = []
+    at = 0
+    for n in names[:-1]:
+        parts.append(by_device(packed[:, at : at + SIZE[n]], n, count))
+        at += SIZE[n]
+    q = count // GROUP
+    parts.append(packed[:, at:].reshape(count, -1, D))
+    return jnp.concatenate(parts, axis=1)
 
 
 def rope_tables(stream):
@@ -874,7 +960,8 @@
     meta = jnp.concatenate(
         [lengths.reshape(-1), (lax.axis_index("head") * F).astype(jnp.int32).reshape(1)]
     ).astype(jnp.int32)
-    E, gains, gate_gain, (gate_taps, merge_taps) = gather_weights(shards, devices)
+    packs, gains, gate_gain, (gate_taps, merge_taps) = gather_weights(shards, devices)
+    EA, EB, E = packs["a"], packs["b"], packs["rest"]
     x = frames.reshape(T, D)
     cot = cotangent.reshape(T, D)
     up = [(i, i + 1) for i in range(nh - 1)]
@@ -909,8 +996,10 @@
         (full(D), whole((nh, T, W))),
         [vm((T, D), bf16), vm((T, D), f32), vm((T, 3 * D), bf16)],
         grid=(nb,), us=8,
-    )(x, gains, E, E, E)
+    )(x, gains, EA, EB, EA)
     qkv_r = exchange(qkv).reshape(nh, micro, F, W)
+    mid1, last = lax.optimization_barrier((mid1, packs["last"]))
+    EL = unpack(lax.all_gather(last, AXES, axis=0, tiled=False), "last")
 
     zl, gp, gn, rs, fe, le = call(
         bind(up_kernel, micro, F), "up",
@@ -969,28 +1058,25 @@
     )(meta, jn, jn_b, jn_a, merge_taps, E, mid1)
 
     there_back = lambda j: jnp.where(j < nb, j, 2 * nb - 1 - j)
-    back = lambda j: jnp.where(j < nb, nb - 1, 2 * nb - 1 - j)
-    out_rows, dmid2, dm, dmg, fe, le, d_second_in, d_second_out, dgain2 = call(
+    out_rows, dmid2, dm, fe, le, d_early, dgain2 = call(
         bind(second_kernel, micro, F), "second",
         (
-            rows(D, bf16), rows(D, f32), rows(2 * D, bf16), rows(D, bf16), edge(2 * D), edge(2 * D),
-            sds((GROUP, 64, D), bf16), sds((GROUP, 64, D), bf16), sds((8, D), f32),
+            rows(D, bf16), rows(D, f32), rows(2 * D, bf16), edge(2 * D), edge(2 * D),
+            sds((GROUP, 192, D), bf16), sds((8, D), f32),
         ),
-        [full(D), full(D), whole((8, D)), columns_spec("second_in", there_back), rows_spec("second_out", there_back), whole_spec("merge_weight")],
+        [full(D), full(D), whole((8, D)), columns_spec("second_in", there_back), rows_spec("second_out", there_back), whole_spec("merge_weight"), full(2 * D)],
         (
-            full(D), full(D), full(2 * D), full(D), edge_spec(2 * D), edge_spec(2 * D),
-            pl.BlockSpec((GROUP, 16, D), lambda j: (0, back(j), 0)),
-            pl.BlockSpec((D // 64, 64, D), lambda j: (back(j), 0, 0)),
+            full(D), full(D), full(2 * D), edge_spec(2 * D), edge_spec(2 * D),
+            whole((GROUP, 160, D)),
             whole((8, D)),
         ),
         [vm((T, D), bf16), vm((D, T), bf16), vm((nb, T, D), f32), vm((T, D), f32), vm((T, D), f32), vm((T, D), bf16)],
         grid=(2 * nb,), us=25,
-    )(mid2, cot, gains, E, E, E)
+    )(mid2, cot, gains, EL, EL, E, mixed)
+    early = lax.psum_scatter(
+        by_pieces(d_early, EARLY, devices).reshape(-1, D), AXES, scatter_dimension=0, tiled=True
+    )
     dm_b, dm_a = halo(fe, le)
-
-    d_merge = call(
-        outer_kernel, "merge_outer", sds((2 * D, D), bf16), [full(2 * D), full(D)], whole((2 * D, D)), us=4
-    )(mixed, dmg).reshape(GROUP, 32, D)
 
     da, dc, do, merge_sums = call(
         bind(merge_back_kernel, micro, F, U), "merge_back",
@@ -1004,12 +1090,12 @@
 
     column = pl.BlockSpec((T, D), lambda j: (0, j))
     edge_column = pl.BlockSpec((micro, 16, D), lambda j: (0, 0, j))
-    d_down, d_output, dup_l, dgate, fe, le = call(
+    d_down, dup_l, dgate, fe, le = call(
         bind(gate_pre_kernel, micro, F), "gate_pre",
-        (sds((CH, D), bf16), sds((D, D), bf16), rows(CH, bf16), rows(CH, bf16), edge(CH), edge(CH)),
+        (sds((GROUP, 64, D), bf16), rows(CH, bf16), rows(CH, bf16), edge(CH), edge(CH)),
         [full(D), full(D), whole((nh, T, O)), column, column, column, whole_spec("gated_down")],
-        (pl.BlockSpec((D, D), lambda j: (j, 0)), whole((D, D)), column, column, edge_column, edge_column),
-        [vm((CH, D), bf16)],
+        (whole((GROUP, 64, D)), column, column, edge_column, edge_column),
+        [vm((CH, D), bf16), vm((CH, D), bf16)],
         grid=(3,), us=8,
     )(dc, da, o_r, zl, gate, gp, E)
     dg_b, dg_a = halo(fe, le)
@@ -1020,8 +1106,9 @@
         [SMEM, qkv_spec, whole((S, HD)), whole((S, HD)), o_spec, l_spec, o_spec],
         qkv_spec,
         [head_buf] * 4 + [vm((lh, HD, S), bf16)] * 2 + [vm((lh, S, HD), f32)] + [vm((lh, HD, S), f32)] * 2,
-        grid=(micro,), us=25,
+        grid=(micro,), us=1,
     )(meta, qkv_r, cos, sin, o_own, logs, do_r)
+    dgate, dqkv = lax.optimization_barrier((dgate, dqkv))
     dqkv_r = exchange(dqkv.reshape(nh, T, W))
 
     dup_r, gate_sums, dgain_gate = call(
@@ -1033,9 +1120,10 @@
         ],
         (full(CH), whole(gate_taps.shape), whole((1, CH))),
         [buf, buf, buf, vm((T, CH), f32)],
-        us=30,
+        us=1,
     )(meta, dgate, dg_b, dg_a, gn, rs, gate_gain, gate_taps, gp)
 
+    dup_r, dqkv_r = lax.optimization_barrier((dup_r, dqkv_r))
     dml, d_up, dgain3 = call(
         up_back_kernel, "up_back",
         (rows(D, f32), sds((GROUP, 96, D), bf16), sds((1, D), f32)),
@@ -1047,8 +1135,14 @@
         ],
         (full(D), pl.BlockSpec((GROUP, 16, D), lambda j: (0, j, 0)), whole((1, D))),
         [vm((D, T), bf16), vm((T, D), f32)],
-        grid=(6,), us=8,
+        grid=(6,), us=1,
     )(mid1, dmid2, gains, dup_l, dup_r, E)
+
+    middle = Exchange(
+        [("gated_up", d_up), ("output_projection", d_down[:, :16]), ("gated_down", d_down[:, 16:])], devices
+    )
+    middle.pair()
+    dml, middle.lanes, early = lax.optimization_barrier((dml, middle.lanes, early))
 
     dx, d_head, d_first_in, d_first_out, dgain1 = call(
         first_back_kernel, "first_back",
@@ -1067,16 +1161,9 @@
             whole((8, D)),
         ),
         [vm((T, 3 * D), bf16), vm((T, D), bf16), vm((D, T), bf16), vm((T, D), f32), vm((T, D), bf16), vm((T, D), f32)],
-        grid=(nb,), us=15,
-    )(x, mid1, dml, dqkv_r, gains, E, E, E)
-
-    early = scatter_pieces(
-        [
-            ("second_in", d_second_in), ("second_out", d_second_out), ("merge_weight", d_merge),
-            ("gated_down", d_down.reshape(GROUP, 48, D)), ("output_projection", d_output.reshape(GROUP, 16, D)),
-        ],
-        devices,
-    )
+        grid=(nb,), us=1,
+    )(x, mid1, dml, dqkv_r, gains, EA, EA, EB)
+
     grads = {
         "gain_first": dgain1[0],
         "gain_attend": dgain1[1],
@@ -1094,14 +1181,16 @@
     tiny = jnp.concatenate(tiny, axis=1).astype(bf16)
     tiny_rows = SIZE["tiny"] * GROUP // devices
     tiny = jnp.pad(tiny, ((0, 0), (0, tiny_rows * D - tiny.shape[1]))).reshape(devices, tiny_rows, D)
-    late = scatter_pieces(
-        [
-            ("gated_up", d_up), ("head_projection", d_head), ("first_in", d_first_in), ("first_out", d_first_out),
-            ("tiny", tiny),
-        ],
-        devices,
+    late = Exchange(
+        [("head_projection", d_head), ("first_in", d_first_in), ("first_out", d_first_out), ("tiny", tiny)], devices
     )
-    shares = {**early, **late}
+    middle.step()
+    late.sent, middle.lanes = lax.optimization_barrier((late.sent, middle.lanes))
+    late.pair()
+    late = late.finish()
+    middle = middle.finish()
+    early = split_rows(early, EARLY[:-1], devices)
+    shares = {**early, **middle, **late}
     flat = shares["tiny"].reshape(-1)
     at = 0
     for n in GAINS + KERNELS:

time: 607 us -> 498 us (0.82)
  waiting for transfers between devices: 276 us -> 143 us
  starting transfers between devices: 44.9 us -> 65.7 us
  other arithmetic: 13.1 us -> 33.5 us
  local copies, waits for them, and re-layouts: 66.7 us -> 49.2 us
    reduce_scatter x2 -> x1, waiting for transfers between devices: 140 us -> 0.02 us  [on_device(): lax.psum_scatter(by_pieces(d_early, EARLY, devices).reshape(-1, D), AXES,...]
    ppermute x0 -> x28, waiting for transfers between devices: none -> 117 us  [swap(): return lax.ppermute(v, AXES, [(i, i ^ 1 << bit) for i in range(count)])]
    all_gather x1 -> x2, waiting for transfers between devices: 115 us -> 0.01 us  [the longest x1 0.01 us: on_device(): EL = unpack(lax.all_gather(last, AXES, axis=0, tiled=False), 'last')]
    ppermute x0 -> x28, starting transfers between devices: none -> 27.9 us  [swap(): return lax.ppermute(v, AXES, [(i, i ^ 1 << bit) for i in range(count)])]
    unnamed x72 -> x90, local copies, waits for them, and re-layouts: 35.8 us -> 11.9 us
    ppermute x8, waiting for transfers between devices: 3.78 us -> 21.5 us  [halo(): return (lax.ppermute(last, 'head', up), lax.ppermute(first, 'head', down))]
    all_to_all x4, waiting for transfers between devices: 17.2 us -> 3.67 us  [exchange(): return lax.all_to_all(v, 'head', split_axis=0, concat_axis=0, tiled=True)]
    squeeze x0 -> x23, local copies, waits for them, and re-layouts: none -> 8.55 us  [pick(): return lax.dynamic_index_in_dim(v, at, axis, keepdims=False)]
  transfers between devices with their start and end apart: 15 -> 43, of which waited for: 7 -> 28; matrix products, arithmetic and copies ran while one was open for 6% -> 13% of each run, Pallas kernels for 20% -> 34%
where the time goes in v2:
time: 498 us; the launch traced here: 489 us
  Pallas kernels  183 us (37%)
  waiting for transfers between devices  143 us (29%)
  starting transfers between devices  65.7 us (13%)
  local copies, waits for them, and re-layouts  49.2 us (10%)
  other arithmetic  33.5 us (7%)
  between operations  15.2 us (3%)
    ppermute x28, waiting for transfers between devices, swap(): return lax.ppermute(v, AXES, [(i, i ^ 1 << bit) for i in range(count)])  117 us
    ppermute x28, starting transfers between devices, swap(): return lax.ppermute(v, AXES, [(i, i ^ 1 << bit) for i in range(count)])  27.9 us
    pallas_call x1, Pallas kernels, on_device(): call(bind(gate_back_kernel, micro, F, U), 'gate_back', (rows(CH, bf16), s...  26.1 us
    pallas_call x1, Pallas kernels, on_device(): call(bind(attend_back_kernel, lh, U), 'attend_back', sds((nh, micro, F, W...  22.9 us
    ppermute x8, starting transfers between devices, halo(): return (lax.ppermute(last, 'head', up), lax.ppermute(first, 'head', down))  21.9 us
    ppermute x8, waiting for transfers between devices, halo(): return (lax.ppermute(last, 'head', up), lax.ppermute(first, 'head', down))  21.5 us
    pallas_call x1, Pallas kernels, on_device(): call(bind(second_kernel, micro, F), 'second', (rows(D, bf16), rows(D, f32...  18.8 us
    pallas_call x1, Pallas kernels, on_device(): call(bind(merge_back_kernel, micro, F, U), 'merge_back', (rows(D, bf16),...  16.3 us
  transfers between devices with their start and end apart: 43, of which 28 were waited for; matrix products, arithmetic and copies ran while one was open for 13% of the time, Pallas kernels for 34%

profile of v2, /device:TPU:0, one launch (start us, length us, event | category | flops | bytes accessed | tf_op | source)
XLA Modules:
  0.0 489.0 jit_solution(13151698849780379196)
XLA Ops:
  11.5 4.1 concatenate.52
  16.5 4.1 collective-permute-start
  22.4 2.3 collective-permute-done
  24.8 4.9 %collective-permute-start.1 = (bf16[2,80,512]{2,1,0:T(8,128)(2,1)S(1)}, bf16[2,80,512]{2,1,0:T(8,128)(2,1)S(1)}, u32[]{:S(2)}, u32[]{:S(2)}) collective-permute-start(bf16[2,80,512]{2,1,0:T(8,128)(2,1)S(1)} %pad_maximum_fusion.17), channel_id=1, source_target_pairs={{0,2},{1,3},{2,0},{3,1},{4,6},{5,7},{6,4},{7,5},{8,10},{9,11},{10,... | collective-permute-start | bytes 491528 | tf_op jit(solution)/shard_map/ppermute | solution.py:804
  29.7 3.6 collective-permute-done.5
  33.5 4.5 collective-permute-done.1
  39.6 3.0 collective-permute-done.6
  42.7 1.6 collective-permute-start.7
  44.3 5.7 %collective-permute-done.2 = bf16[2,2,80,512]{3,2,0,1:T(8,128)(2,1)S(1)} collective-permute-done((bf16[2,2,80,512]{3,2,0,1:T(8,128)(2,1)S(1)}, bf16[2,2,80,512]{3,2,0,1:T(8,128)(2,1)S(1)}, u32[]{:S(2)}, u32[]{:S(2)}) %collective-permute-start.2) | collective-permute-done | bytes 327712 | tf_op jit(solution)/shard_map/ppermute | solution.py:804
  50.2 1.8 collective-permute-start.3
  52.0 9.1 %collective-permute-done.7 = bf16[2,2,112,512]{3,2,1,0:T(8,128)(2,1)S(1)} collective-permute-done((bf16[2,2,112,512]{3,2,1,0:T(8,128)(2,1)S(1)}, bf16[2,2,112,512]{3,2,1,0:T(8,128)(2,1)S(1)}, u32[]{:S(2)}, u32[]{:S(2)}) %collective-permute-start.7) | collective-permute-done | bytes 458784 | tf_op jit(solution)/shard_map/ppermute | solution.py:804
  62.8 17.9 %collective-permute-done.3 = bf16[2,2,2,80,512]{4,3,1,2,0:T(8,128)(2,1)S(1)} collective-permute-done((bf16[2,2,2,80,512]{4,3,1,2,0:T(8,128)(2,1)S(1)}, bf16[2,2,2,80,512]{4,3,1,2,0:T(8,128)(2,1)S(1)}, u32[]{:S(2)}, u32[]{:S(2)}) %collective-permute-start.3) | collective-permute-done | bytes 655392 | tf_op jit(solution)/shard_map/ppermute | solution.py:804
  81.0 13.2 %collective-permute-done.8 = bf16[2,2,2,112,512]{4,3,2,1,0:T(8,128)(2,1)S(1)} collective-permute-done((bf16[2,2,2,112,512]{4,3,2,1,0:T(8,128)(2,1)S(1)}, bf16[2,2,2,112,512]{4,3,2,1,0:T(8,128)(2,1)S(1)}, u32[]{:S(2)}, u32[]{:S(2)}) %collective-permute-start.8) | collective-permute-done | bytes 917536 | tf_op jit(solution)/shard_map/ppermute | solution.py:804
  98.3 1.6 select_bitcast_fusion.3
  105.4 2.0 select_bitcast_fusion.1
  107.4 2.1 pad_maximum_fusion
  109.5 8.9 %first.1 = (f32[512,512]{1,0:T(8,128)}, bf16[4,512,384]{2,1,0:T(8,128)(2,1)}) custom-call(bf16[512,512]{1,0:T(8,128)(2,1)} %bitcast.292, f32[8,512]{1,0:T(8,128)} %pad_convert_fusion.refs_1_.refs_2_.gain_ref, bf16[32,112,512]{2,1,0:T(8,128)(2,1)} %bitcast.237, bf16[32,80,512]{2,1,0:T(8,128)(2,1)} %bitcast.250, bf16[32,112,512]{2,1,0:T(8,128)(2,1)} %bitcast.238), custom_call_target="tpu_custom_call" | custom-call | flops 4000000000 | bytes 20000000 | tf_op jit(solution)/shard_map/first/pallas_call | solution.py:992
  122.0 3.6 all-to-all-start
  127.8 10.3 %up.1 = (bf16[512,1536]{1,0:T(8,128)(2,1)}, bf16[512,3072]{1,0:T(8,128)(2,1)}, bf16[512,1536]{1,0:T(8,128)(2,1)}, f32[512,128]{1,0:T(8,128)}, bf16[2,16,1536]{2,...) custom-call(f32[512,512]{1,0:T(8,128)} %get-tuple-element.79.refs_0_.refs_6_.mid_ref, ...), custom_call_target="tpu_custom_call" | custom-call | flops 7500000256 | bytes 37500000 | tf_op jit(solution)/shard_map/up/pallas_call | solution.py:1004
  138.1 3.9 collective-permute-start.10
  143.5 3.7 all-to-all-done
  148.4 15.3 %attend.1 = (bf16[4,2,256,128]{3,2,1,0:T(8,128)(2,1)}, f32[2,1024,128]{2,1,0:T(8,128)}) custom-call(s32[9]{0:T(128)} %pad_add_fusion.refs_0_, bf16[4,2,256,384]{3,2,1,0:T(8,128)(2,1)} %bitcast.259, f32[1024,64]{1,0:T(8,128)} %constant.155.clone.refs_2_, f32[1024,64]{1,0:T(8,128)} %constant.156.clone.refs_3_), custom_call_target="tpu_custom_call" | custom-call | flops 6000000000 | bytes 30000000 | tf_op jit(solution)/shard_map/attend/pallas_call | solution.py:1023
  163.7 3.5 all-to-all-start.1
  167.9 16.1 %gate.1 = (bf16[512,1536]{1,0:T(8,128)(2,1)}, bf16[512,512]{1,0:T(8,128)(2,1)}) custom-call(s32[9]{0:T(128)} %pad_add_fusion.refs_0_, bf16[512,1536]{1,0:T(8,128)(2,1)} %get-tuple-element.80.refs_1_.refs_4_, bf16[2,16,1536]{2,1,0:T(8,128)(2,1)} %copy-done.30, bf16[2,16,1536]{2,1,0:T(8,128)(2,1)} %copy-done.31, ...), custom_call_target="tpu_custom_call" | custom-call | flops 8999999488 | bytes 45000000 | tf_op jit(solution)/shard_map/gate/pallas_call | solution.py:1033
  184.7 2.8 join.1
  187.6 3.9 collective-permute-start.12
  195.1 2.9 collective-permute-done.13.refs_3_
  198.6 11.3 %merge.1 = (bf16[512,1024]{1,0:T(8,128)(2,1)}, f32[512,512]{1,0:T(8,128)}) custom-call(s32[9]{0:T(128)} %pad_add_fusion.refs_0_, bf16[512,1024]{1,0:T(8,128)(2,1)} %get-tuple-element.85.refs_1_.refs_4_, bf16[2,16,1024]{2,1,0:T(8,128)(2,1)} %copy-done.34, bf16[2,16,1024]{2,1,0:T(8,128)(2,1)} %copy-done.35, f32[1,31,8,128]{3,2,1,0:T(8,128)} %reshape.314.refs_4_.refs_5_, ...), custom_call_target="tpu_custom_call" | custom-call | flops 6000000000 | bytes 30000000 | tf_op jit(solution)/shard_map/merge/pallas_call | solution.py:1051
  209.9 18.8 %second.1 = (bf16[512,512]{1,0:T(8,128)(2,1)}, f32[512,512]{1,0:T(8,128)}, bf16[512,1024]{1,0:T(8,128)(2,1)}, bf16[2,16,1024]{2,1,0:T(8,128)(2,1)}, bf16[2,16,10...) custom-call(f32[512,512]{1,0:T(8,128)} %get-tuple-element.88.refs_0_, ...), custom_call_target="tpu_custom_call" | custom-call | flops 12499999744 | bytes 62500000 | tf_op jit(solution)/shard_map/second/pallas_call | solution.py:1061
  229.5 4.8 collective-permute-start.14
  236.2 4.3 collective-permute-done.15.refs_3_
  241.1 16.3 %merge_back.1 = (bf16[512,512]{1,0:T(8,128)(2,1)}, bf16[512,512]{1,0:T(8,128)(2,1)}, bf16[4,512,128]{2,1,0:T(8,128)(2,1)}, f32[1,31,8,128]{3,2,1,0:T(8,128)}) custom-call(s32[9]{0:T(128)} %pad_add_fusion.refs_0_, bf16[512,1024]{1,0:T(8,128)(2,1)} %get-tuple-element.93.refs_1_, bf16[2,16,1024]{2,1,0:T(8,128)(2,1)} %copy-done.36, ...), custom_call_target="tpu_custom_call" | custom-call | flops 10000000000 | bytes 50000000 | tf_op jit(solution)/shard_map/merge_back/pallas_call | solution.py:1081
  257.4 4.5 all-to-all-start.2
  262.0 8.4 %gate_pre.1 = (bf16[32,64,512]{2,1,0:T(8,128)(2,1)}, bf16[512,1536]{1,0:T(8,128)(2,1)}, bf16[512,1536]{1,0:T(8,128)(2,1)}, bf16[2,16,1536]{2,1,0:T(8,128)(2,1)}, bf16[2,16,1536]{2,1,0:T(8,128)(2,1)}) custom-call(bf16[512,512]{1,0:T(8,128)(2,1)} %get-tuple-element.96.refs_0_, bf16[512,512]{1,0:T(8,128)(2,1)} %get-tuple-element.97.refs_1_, ...), custom_call_target="tpu_custom_call" | custom-call | flops 4000000000 | bytes 20000000 | tf_op jit(solution)/shard_map/gate_pre/pallas_call | solution.py:1093
  271.2 22.9 %attend_back.1 = bf16[4,2,256,384]{3,2,1,0:T(8,128)(2,1)} custom-call(s32[9]{0:T(128)} %pad_add_fusion.refs_0_, bf16[4,2,256,384]{3,2,1,0:T(8,128)(2,1)} %bitcast.260, f32[1024,64]{1,0:T(8,128)} %constant.155.clone.refs_2_, f32[1024,64]{1,0:T(8,128)} %constant.156.clone.refs_3_, bf16[4,2,256,128]{3,2,1,0:T(8,128)(2,1)} %get-tuple-element.77.refs_4_, ...), custom_call_target="tpu_custom_call" | custom-call | flops 500000000 | bytes 2500000 | tf_op jit(solution)/shard_map/attend_back/pallas_call | solution.py:1103
  294.1 4.2 all-to-all-start.3
  301.0 3.9 collective-permute-start.16
  307.2 8.9 %collective-permute-done.16.refs_2_ = bf16[2,16,1536]{2,1,0:T(8,128)(2,1)S(1)} collective-permute-done((bf16[2,16,1536]{2,1,0:T(8,128)(2,1)S(1)}, bf16[2,16,1536]{2,1,0:T(8,128)(2,1)S(1)}, u32[]{:S(2)}, u32[]{:S(2)}) %collective-permute-start.16) | collective-permute-done | bytes 98336 | tf_op jit(solution)/shard_map/ppermute | solution.py:971
  316.1 4.8 collective-permute-done.17.refs_3_
  321.6 26.1 %gate_back.1 = (bf16[512,1536]{1,0:T(8,128)(2,1)}, f32[2,31,8,128]{3,2,1,0:T(8,128)}, f32[1,1536]{1,0:T(1,128)}) custom-call(s32[9]{0:T(128)} %pad_add_fusion.refs_0_, bf16[512,1536]{1,0:T(8,128)(2,1)} %get-tuple-element.104.refs_1_, bf16[2,16,1536]{2,1,0:T(8,128)(2,1)} %copy-done.22, bf16[2,16,1536]{2,1,0:T(8,128)(2,1)} %copy-done.23, ...), custom_call_target="tpu_custom_call" | custom-call | flops 500000000 | bytes 2500000 | tf_op jit(solution)/shard_map/gate_back/pallas_call | solution.py:1114
  347.6 10.9 %up_back.1 = (f32[512,512]{1,0:T(8,128)}, bf16[32,96,512]{2,1,0:T(8,128)(2,1)}, f32[1,512]{1,0:T(1,128)}) custom-call(f32[512,512]{1,0:T(8,128)} %get-tuple-element.79.refs_0_.refs_6_.mid_ref, f32[512,512]{1,0:T(8,128)} %get-tuple-element.92.dmid2_ref, f32[8,512]{1,0:T(8,128)} %pad_convert_fusion.refs_1_.refs_2_.gain_ref, ...), custom_call_target="tpu_custom_call" | custom-call | flops 500000000 | bytes 2500000 | tf_op jit(solution)/shard_map/up_back/pallas_call | solution.py:1127
  358.5 1.6 dynamic-slice_bitcast_fusion
  360.2 1.7 pad_maximum_fusion.3
  369.4 1.6 slice_add_fusion
  372.2 1.7 collective-permute-start.20
  374.8 2.5 collective-permute-start.19
  377.3 14.9 %first_back.1 = (f32[512,512]{1,0:T(8,128)}, bf16[32,48,512]{2,1,0:T(8,128)(2,1)}, bf16[32,64,512]{2,1,0:T(8,128)(2,1)}, bf16[32,64,512]{2,1,0:T(8,128)(2,1)}, f32[8,512]{1,0:T(8,128)}) custom-call(bf16[512,512]{1,0:T(8,128)(2,1)} %bitcast.293, f32[512,512]{1,0:T(8,128)} %get-tuple-element.79.refs_0_.refs_6_.mid_ref, f32[512,512]{1,0:T(8,128)} %get-tuple-element.115.dml_ref, ...), custom_call_target="tpu_custom_call" | custom-call | flops 500000000 | bytes 2500000 | tf_op jit(solution)/shard_map/first_back/pallas_call | solution.py:1147
  395.6 1.6 dynamic-slice_bitcast_fusion.1
  398.1 2.0 pad_maximum_fusion.1
  400.1 2.1 bitcast_add_fusion.2
  403.1 1.6 slice_convert_fusion.3
  409.4 7.2 %collective-permute-done.33 = bf16[2,2,80,512]{3,2,1,0:T(8,128)(2,1)S(1)} collective-permute-done((bf16[2,2,80,512]{3,2,1,0:T(8,128)(2,1)S(1)}, bf16[2,2,80,512]{3,2,1,0:T(8,128)(2,1)S(1)}, u32[]{:S(2)}, u32[]{:S(2)}) %collective-permute-start.33) | collective-permute-done | bytes 327712 | tf_op jit(solution)/shard_map/ppermute | solution.py:804
  416.8 2.3 collective-permute-done.30
  419.2 4.5 collective-permute-done.34
  423.8 3.1 collective-permute-done.31
  428.0 4.2 collective-permute-done.35
  434.5 12.2 %collective-permute-done.26 = bf16[2,2,2,96,512]{4,3,2,1,0:T(8,128)(2,1)S(1)} collective-permute-done((bf16[2,2,2,96,512]{4,3,2,1,0:T(8,128)(2,1)S(1)}, bf16[2,2,2,96,512]{4,3,2,1,0:T(8,128)(2,1)S(1)}, u32[]{:S(2)}, u32[]{:S(2)}) %collective-permute-start.26) | collective-permute-done | bytes 786464 | tf_op jit(solution)/shard_map/ppermute | solution.py:804
  448.0 5.6 %collective-permute-done.22 = bf16[2,2,2,96,512]{4,3,2,1,0:T(8,128)(2,1)S(1)} collective-permute-done((bf16[2,2,2,96,512]{4,3,2,1,0:T(8,128)(2,1)S(1)}, bf16[2,2,2,96,512]{4,3,2,1,0:T(8,128)(2,1)S(1)}, u32[]{:S(2)}, u32[]{:S(2)}) %collective-permute-start.22) | collective-permute-done | bytes 786464 | tf_op jit(solution)/shard_map/ppermute | solution.py:804
  453.8 2.1 collective-permute-start.23
  457.2 3.2 collective-permute-done.27
  462.7 6.2 %collective-permute-done.28 = bf16[2,96,512]{2,1,0:T(8,128)(2,1)S(1)} collective-permute-done((bf16[2,96,512]{2,1,0:T(8,128)(2,1)S(1)}, bf16[2,96,512]{2,1,0:T(8,128)(2,1)S(1)}, u32[]{:S(2)}, u32[]{:S(2)}) %collective-permute-start.28) | collective-permute-done | bytes 196640 | tf_op jit(solution)/shard_map/ppermute | solution.py:804
  469.0 2.0 collective-permute-done.24
  472.1 3.3 collective-permute-done.29
  475.4 2.2 collective-permute-done.25
  (283 shorter events, 78.2 us)
Async XLA Ops:
  7.2 120.6 %all-gather.5.cloned.1.call-start = ((), (), s32[]{:S(2)}) async-start(), calls=%async_computation.6 | async-start | bytes 6488064 | tf_op jit(solution)/shard_map/all_gather | solution.py:838
  9.9 200.0 %all-gather.7.cloned.1.call-start = ((), (), s32[]{:S(2)}) async-start(), calls=%async_computation.7 | async-start | bytes 4325376 | tf_op jit(solution)/shard_map/all_gather | solution.py:1002
  16.5 8.3 %collective-permute-start = (bf16[80,512]{1,0:T(8,128)(2,1)S(1)}, bf16[80,512]{1,0:T(8,128)(2,1)S(1)}, u32[]{:S(2)}, u32[]{:S(2)}) collective-permute-start(bf16[80,512]{1,0:T(8,128)(2,1)S(1)} %constant_dynamic-update-slice_fusion), channel_id=1, source_target_pairs={{0,4},{1,5},{2,6},{3,7},{4,0},{5,1},{6,2},{7,3},{8,12},{9,13},{10,... | collective-permute-start | bytes 245768 | tf_op jit(solution)/shard_map/ppermute | solution.py:804
  22.3 11.0 %collective-permute-start.5 = (bf16[112,512]{1,0:T(8,128)(2,1)S(1)}, bf16[112,512]{1,0:T(8,128)(2,1)S(1)}, u32[]{:S(2)}, u32[]{:S(2)}) collective-permute-start(bf16[112,512]{1,0:T(8,128)(2,1)S(1)} %pad_maximum_fusion.19), channel_id=1, source_target_pairs={{0,4},{1,5},{2,6},{3,7},{4,0},{5,1},{6,2},{7,3},{8,12},{9,13},{10,... | collective-permute-start | bytes 344072 | tf_op jit(solution)/shard_map/ppermute | solution.py:804
  24.8 13.2 %collective-permute-start.1 = (bf16[2,80,512]{2,1,0:T(8,128)(2,1)S(1)}, bf16[2,80,512]{2,1,0:T(8,128)(2,1)S(1)}, u32[]{:S(2)}, u32[]{:S(2)}) collective-permute-start(bf16[2,80,512]{2,1,0:T(8,128)(2,1)S(1)} %pad_maximum_fusion.17), channel_id=1, source_target_pairs={{0,2},{1,3},{2,0},{3,1},{4,6},{5,7},{6,4},{7,5},{8,10},{9,11},{10,... | collective-permute-start | bytes 491528 | tf_op jit(solution)/shard_map/ppermute | solution.py:804
  33.4 9.2 %collective-permute-start.6 = (bf16[2,112,512]{2,1,0:T(8,128)(2,1)S(1)}, bf16[2,112,512]{2,1,0:T(8,128)(2,1)S(1)}, u32[]{:S(2)}, u32[]{:S(2)}) collective-permute-start(bf16[2,112,512]{2,1,0:T(8,128)(2,1)S(1)} %pad_maximum_fusion.15), channel_id=1, source_target_pairs={{0,2},{1,3},{2,0},{3,1},{4,6},{5,7},{6,4},{7,5},{8,10},{9,11},{10,... | collective-permute-start | bytes 688136 | tf_op jit(solution)/shard_map/ppermute | solution.py:804
  38.0 12.0 %collective-permute-start.2 = (bf16[2,2,80,512]{3,2,0,1:T(8,128)(2,1)S(1)}, bf16[2,2,80,512]{3,2,0,1:T(8,128)(2,1)S(1)}, u32[]{:S(2)}, u32[]{:S(2)}) collective-permute-start(bf16[2,2,80,512]{3,2,0,1:T(8,128)(2,1)S(1)} %pad_maximum_fusion.14), channel_id=1, source_target_pairs={{0,16},{1,17},{2,18},{3,19},{4,20},{5,21},{6,22},{7,23},{8,24},{9,... | collective-permute-start | bytes 983048 | tf_op jit(solution)/shard_map/ppermute | solution.py:804
  42.7 18.3 %collective-permute-start.7 = (bf16[2,2,112,512]{3,2,1,0:T(8,128)(2,1)S(1)}, bf16[2,2,112,512]{3,2,1,0:T(8,128)(2,1)S(1)}, u32[]{:S(2)}, u32[]{:S(2)}) collective-permute-start(bf16[2,2,112,512]{3,2,1,0:T(8,128)(2,1)S(1)} %pad_maximum_fusion.13), channel_id=1, source_target_pairs={{0,8},{1,9},{2,10},{3,11},{4,12},{5,13},{6,14},{7,15},{8,0},{9,1},... | collective-permute-start | bytes 1376264 | tf_op jit(solution)/shard_map/ppermute | solution.py:804
  50.2 30.5 %collective-permute-start.3 = (bf16[2,2,2,80,512]{4,3,1,2,0:T(8,128)(2,1)S(1)}, bf16[2,2,2,80,512]{4,3,1,2,0:T(8,128)(2,1)S(1)}, u32[]{:S(2)}, u32[]{:S(2)}) collective-permute-start(bf16[2,2,2,80,512]{4,3,1,2,0:T(8,128)(2,1)S(1)} %pad_maximum_fusion.12), channel_id=1, source_target_pairs={{0,8},{1,9},{2,10},{3,11},{4,12},{5,13},{6,14},{7,15},{8,0},{9,1},... | collective-permute-start | bytes 1966088 | tf_op jit(solution)/shard_map/ppermute | solution.py:804
  61.2 33.0 %collective-permute-start.8 = (bf16[2,2,2,112,512]{4,3,2,1,0:T(8,128)(2,1)S(1)}, bf16[2,2,2,112,512]{4,3,2,1,0:T(8,128)(2,1)S(1)}, u32[]{:S(2)}, u32[]{:S(2)}) collective-permute-start(bf16[2,2,2,112,512]{4,3,2,1,0:T(8,128)(2,1)S(1)} %pad_maximum_fusion.11), channel_id=1, source_target_pairs={{0,16},{1,17},{2,18},{3,19},{4,20},{5,21},{6,22},{7,23},{8,24},{9,... | collective-permute-start | bytes 2752520 | tf_op jit(solution)/shard_map/ppermute | solution.py:804
  80.9 17.4 %collective-permute-start.4 = (bf16[2,2,2,2,80,512]{5,4,2,3,0,1:T(8,128)(2,1)S(1)}, bf16[2,2,2,2,80,512]{5,4,2,3,0,1:T(8,128)(2,1)}, u32[]{:S(2)}, u32[]{:S(2)}) collective-permute-start(bf16[2,2,2,2,80,512]{5,4,2,3,0,1:T(8,128)(2,1)S(1)} %pad_maximum_fusion.10), channel_id=1, source_target_pairs={{0,1},{1,0},{2,3},{3,2},{4,5},{5,4},{6,7},{7,6},{8,9},{9,8},{10,11... | collective-permute-start | bytes 3932168 | tf_op jit(solution)/shard_map/ppermute | solution.py:804
  95.9 9.5 %collective-permute-start.9 = (bf16[2,2,2,2,112,512]{5,4,3,2,1,0:T(8,128)(2,1)}, bf16[2,2,2,2,112,512]{5,4,3,2,1,0:T(8,128)(2,1)}, u32[]{:S(2)}, u32[]{:S(2)}) collective-permute-start(bf16[2,2,2,2,112,512]{5,4,3,2,1,0:T(8,128)(2,1)} %pad_maximum_fusion.4), channel_id=1, source_target_pairs={{0,1},{1,0},{2,3},{3,2},{4,5},{5,4},{6,7},{7,6},{8,9},{9,8},{10,11... | collective-permute-start | bytes 5505032 | tf_op jit(solution)/shard_map/ppermute | solution.py:804
  100.4 7.0 %copy-start = (bf16[2,2,2,2,2,80,512]{6,5,4,3,2,1,0:T(8,128)(2,1)}, bf16[2,2,2,2,2,80,512]{6,5,4,3,2,1,0:T(8,128)(2,1)S(1)}, u32[]{:S(2)}) copy-start(bf16[2,2,2,2,2,80,512]{6,5,4,3,2,1,0:T(8,128)(2,1)S(1)} %copy.72) | copy-start | bytes 7864324
  109.5 9.5 %copy-start.27 = (s32[2,1,4]{2,1,0:T(1,128)S(1)}, s32[2,1,4]{2,1,0:T(1,128)}, u32[]{:S(2)}) copy-start(s32[2,1,4]{2,1,0:T(1,128)} %param.24) | copy-start | bytes 100
  122.0 25.2 %all-to-all-start = ((bf16[4,512,384]{2,1,0:T(8,128)(2,1)}), bf16[4,512,384]{2,1,0:T(8,128)(2,1)S(1)}, u32[]{:S(2)}, u32[]{:S(2)}) async-start(bf16[4,512,384]{2,1,0:T(8,128)(2,1)} %get-tuple-element.76), calls=%async_computation | async-start | bytes 3145728 | tf_op jit(solution)/shard_map/all_to_all | solution.py:974
  138.1 29.1 %collective-permute-start.10 = (bf16[2,16,1536]{2,1,0:T(8,128)(2,1)}, bf16[2,16,1536]{2,1,0:T(8,128)(2,1)S(1)}, u32[]{:S(2)}, u32[]{:S(2)}) collective-permute-start(bf16[2,16,1536]{2,1,0:T(8,128)(2,1)} %get-tuple-element.81), channel_id=1, source_target_pairs={{0,8},{8,16},{16,24},{1,9},{9,17},{17,25},{2,10},{10,18},{18,26},{... | collective-permute-start | bytes 294920 | tf_op jit(solution)/shard_map/ppermute | solution.py:971
  142.0 25.2 %collective-permute-start.11 = (bf16[2,16,1536]{2,1,0:T(8,128)(2,1)}, bf16[2,16,1536]{2,1,0:T(8,128)(2,1)S(1)}, u32[]{:S(2)}, u32[]{:S(2)}) collective-permute-start(bf16[2,16,1536]{2,1,0:T(8,128)(2,1)} %get-tuple-element.82), channel_id=1, source_target_pairs={{8,0},{16,8},{24,16},{9,1},{17,9},{25,17},{10,2},{18,10},{26,18},{... | collective-permute-start | bytes 294920 | tf_op jit(solution)/shard_map/ppermute | solution.py:971
  163.7 20.3 %all-to-all-start.1 = ((bf16[4,512,128]{2,1,0:T(8,128)(2,1)}), bf16[4,512,128]{2,1,0:T(8,128)(2,1)S(1)}, u32[]{:S(2)}, u32[]{:S(2)}) async-start(bf16[4,512,128]{2,1,0:T(8,128)(2,1)} %bitcast.272), calls=%async_computation.1 | async-start | bytes 1048576 | tf_op jit(solution)/shard_map/all_to_all | solution.py:974
  167.1 204.1 %reduce-scatter.2.cloned.1.call-start = ((), (), s32[]{:S(2)}) async-start(), calls=%async_computation.5 | async-start | bytes 6488064 | tf_op jit(solution)/shard_map/reduce_scatter | solution.py:1076
  187.6 7.5 %collective-permute-start.12 = (bf16[2,16,1024]{2,1,0:T(8,128)(2,1)}, bf16[2,16,1024]{2,1,0:T(8,128)(2,1)S(1)}, u32[]{:S(2)}, u32[]{:S(2)}) collective-permute-start(bf16[2,16,1024]{2,1,0:T(8,128)(2,1)} %get-tuple-element.86), channel_id=1, source_target_pairs={{0,8},{8,16},{16,24},{1,9},{9,17},{17,25},{2,10},{10,18},{18,26},{... | collective-permute-start | bytes 196616 | tf_op jit(solution)/shard_map/ppermute | solution.py:971
  191.5 6.5 %collective-permute-start.13 = (bf16[2,16,1024]{2,1,0:T(8,128)(2,1)}, bf16[2,16,1024]{2,1,0:T(8,128)(2,1)S(1)}, u32[]{:S(2)}, u32[]{:S(2)}) collective-permute-start(bf16[2,16,1024]{2,1,0:T(8,128)(2,1)} %get-tuple-element.87), channel_id=1, source_target_pairs={{8,0},{16,8},{24,16},{9,1},{17,9},{25,17},{10,2},{18,10},{26,18},{... | collective-permute-start | bytes 196616 | tf_op jit(solution)/shard_map/ppermute | solution.py:971
  195.1 2.9 copy-start.34
  228.7 5.7 %copy-start.32 = (bf16[2,16,1024]{2,1,0:T(8,128)(2,1)S(1)}, bf16[2,16,1024]{2,1,0:T(8,128)(2,1)}, u32[]{:S(2)}) copy-start(bf16[2,16,1024]{2,1,0:T(8,128)(2,1)} %get-tuple-element.95) | copy-start | bytes 196612
  229.5 6.7 %collective-permute-start.14 = (bf16[2,16,1024]{2,1,0:T(8,128)(2,1)S(1)}, bf16[2,16,1024]{2,1,0:T(8,128)(2,1)S(1)}, u32[]{:S(2)}, u32[]{:S(2)}) collective-permute-start(bf16[2,16,1024]{2,1,0:T(8,128)(2,1)S(1)} %copy-done.33), channel_id=1, source_target_pairs={{0,8},{8,16},{16,24},{1,9},{9,17},{17,25},{2,10},{10,18},{18,26},{... | collective-permute-start | bytes 196616 | tf_op jit(solution)/shard_map/ppermute | solution.py:971
  234.3 6.2 %collective-permute-start.15 = (bf16[2,16,1024]{2,1,0:T(8,128)(2,1)S(1)}, bf16[2,16,1024]{2,1,0:T(8,128)(2,1)S(1)}, u32[]{:S(2)}, u32[]{:S(2)}) collective-permute-start(bf16[2,16,1024]{2,1,0:T(8,128)(2,1)S(1)} %copy-done.32), channel_id=1, source_target_pairs={{8,0},{16,8},{24,16},{9,1},{17,9},{25,17},{10,2},{18,10},{26,18},{... | collective-permute-start | bytes 196616 | tf_op jit(solution)/shard_map/ppermute | solution.py:971
  236.2 4.3 copy-start.36
  257.4 13.0 %all-to-all-start.2 = ((bf16[4,512,128]{2,1,0:T(8,128)(2,1)}), bf16[4,512,128]{2,1,0:T(8,128)(2,1)S(1)}, u32[]{:S(2)}, u32[]{:S(2)}) async-start(bf16[4,512,128]{2,1,0:T(8,128)(2,1)} %get-tuple-element.103), calls=%async_computation.2 | async-start | bytes 1048576 | tf_op jit(solution)/shard_map/all_to_all | solution.py:974
  294.1 53.6 %all-to-all-start.3 = ((bf16[4,512,384]{2,1,0:T(8,128)(2,1)}), bf16[4,512,384]{2,1,0:T(8,128)(2,1)S(1)}, u32[]{:S(2)}, u32[]{:S(2)}) async-start(bf16[4,512,384]{2,1,0:T(8,128)(2,1)} %bitcast.261), calls=%async_computation.3 | async-start | bytes 3145728 | tf_op jit(solution)/shard_map/all_to_all | solution.py:974
  298.3 2.7 copy-start.29
  298.3 6.6 %copy-start.28 = (bf16[2,16,1536]{2,1,0:T(8,128)(2,1)S(1)}, bf16[2,16,1536]{2,1,0:T(8,128)(2,1)}, u32[]{:S(2)}) copy-start(bf16[2,16,1536]{2,1,0:T(8,128)(2,1)} %get-tuple-element.106) | copy-start | bytes 294916
  300.9 6.2 %copy-start.13 = (bf16[32,16,512]{2,1,0:T(8,128)(2,1)}, bf16[32,16,512]{2,1,0:T(8,128)(2,1)S(1)}, u32[]{:S(2)}) copy-start(bf16[32,16,512]{2,1,0:T(8,128)(2,1)S(1)} %slice.153) | copy-start | bytes 1572868
  301.0 15.1 %collective-permute-start.16 = (bf16[2,16,1536]{2,1,0:T(8,128)(2,1)S(1)}, bf16[2,16,1536]{2,1,0:T(8,128)(2,1)S(1)}, u32[]{:S(2)}, u32[]{:S(2)}) collective-permute-start(bf16[2,16,1536]{2,1,0:T(8,128)(2,1)S(1)} %copy-done.29), channel_id=1, source_target_pairs={{0,8},{8,16},{16,24},{1,9},{9,17},{17,25},{2,10},{10,18},{18,26},{... | collective-permute-start | bytes 294920 | tf_op jit(solution)/shard_map/ppermute | solution.py:971
  304.9 16.0 %collective-permute-start.17 = (bf16[2,16,1536]{2,1,0:T(8,128)(2,1)S(1)}, bf16[2,16,1536]{2,1,0:T(8,128)(2,1)S(1)}, u32[]{:S(2)}, u32[]{:S(2)}) collective-permute-start(bf16[2,16,1536]{2,1,0:T(8,128)(2,1)S(1)} %copy-done.28), channel_id=1, source_target_pairs={{8,0},{16,8},{24,16},{9,1},{17,9},{25,17},{10,2},{18,10},{26,18},{... | collective-permute-start | bytes 294920 | tf_op jit(solution)/shard_map/ppermute | solution.py:971
  316.1 4.8 copy-start.22
  347.6 10.9 %copy-start.3 = (bf16[4,512,384]{2,1,0:T(8,128)(2,1)}, bf16[4,512,384]{2,1,0:T(8,128)(2,1)S(1)}, u32[]{:S(2)}) copy-start(bf16[4,512,384]{2,1,0:T(8,128)(2,1)S(1)} %all-to-all-done.3.dq_ref) | copy-start | bytes 4718596
  360.2 2.6 copy-start.21
  360.2 3.8 copy-start.20
  361.9 5.3 %collective-permute-start.18 = (bf16[16,160,512]{2,1,0:T(8,128)(2,1)}, bf16[16,160,512]{2,1,0:T(8,128)(2,1)}, u32[]{:S(2)}, u32[]{:S(2)}) collective-permute-start(bf16[16,160,512]{2,1,0:T(8,128)(2,1)} %pad_maximum_fusion.3), channel_id=1, source_target_pairs={{0,1},{1,0},{2,3},{3,2},{4,5},{5,4},{6,7},{7,6},{8,9},{9,8},{10,11... | collective-permute-start | bytes 7864328 | tf_op jit(solution)/shard_map/ppermute | solution.py:804
  362.7 2.8 copy-start.26
  362.7 4.4 copy-start.14
  366.2 3.2 copy-start.5
  372.2 27.9 %collective-permute-start.20 = (bf16[2,2,2,80,512]{4,3,2,1,0:T(8,128)(2,1)}, bf16[2,2,2,80,512]{4,3,2,1,0:T(8,128)(2,1)}, u32[]{:S(2)}, u32[]{:S(2)}) collective-permute-start(bf16[2,2,2,80,512]{4,3,2,1,0:T(8,128)(2,1)} %dynamic-slice_bitcast_fusion.7), channel_id=1, source_target_pairs={{0,16},{1,17},{2,18},{3,19},{4,20},{5,21},{6,22},{7,23},{8,24},{9,... | collective-permute-start | bytes 1966088 | tf_op jit(solution)/shard_map/ppermute | solution.py:804
  374.8 27.3 %collective-permute-start.19 = (bf16[2,2,2,80,512]{4,3,2,1,0:T(8,128)(2,1)}, bf16[2,2,2,80,512]{4,3,2,1,0:T(8,128)(2,1)S(1)}, u32[]{:S(2)}, u32[]{:S(2)}) collective-permute-start(bf16[2,2,2,80,512]{4,3,2,1,0:T(8,128)(2,1)} %dynamic-slice_bitcast_fusion.8), channel_id=1, source_target_pairs={{0,8},{1,9},{2,10},{3,11},{4,12},{5,13},{6,14},{7,15},{8,0},{9,1},... | collective-permute-start | bytes 1966088 | tf_op jit(solution)/shard_map/ppermute | solution.py:804
  403.1 29.2 %collective-permute-start.21 = (bf16[16,192,512]{2,1,0:T(8,128)(2,1)}, bf16[16,192,512]{2,1,0:T(8,128)(2,1)S(1)}, u32[]{:S(2)}, u32[]{:S(2)}) collective-permute-start(bf16[16,192,512]{2,1,0:T(8,128)(2,1)} %pad_maximum_fusion.1), channel_id=1, source_target_pairs={{0,1},{1,0},{2,3},{3,2},{4,5},{5,4},{6,7},{7,6},{8,9},{9,8},{10,11... | collective-permute-start | bytes 9437192 | tf_op jit(solution)/shard_map/ppermute | solution.py:804
  403.1 13.5 %copy-start.7 = (bf16[2,2,2,80,512]{4,3,2,1,0:T(8,128)(2,1)S(1)}, bf16[2,2,2,80,512]{4,3,2,1,0:T(8,128)(2,1)}, u32[]{:S(2)}) copy-start(bf16[2,2,2,80,512]{4,3,2,1,0:T(8,128)(2,1)} %bitcast_add_fusion.3) | copy-start | bytes 1966084
  403.1 16.0 %copy-start.6 = (bf16[2,2,2,80,512]{4,3,2,1,0:T(8,128)(2,1)S(1)}, bf16[2,2,2,80,512]{4,3,2,1,0:T(8,128)(2,1)}, u32[]{:S(2)}) copy-start(bf16[2,2,2,80,512]{4,3,2,1,0:T(8,128)(2,1)} %bitcast_add_fusion.2) | copy-start | bytes 1966084
  406.4 10.2 %collective-permute-start.33 = (bf16[2,2,80,512]{3,2,1,0:T(8,128)(2,1)S(1)}, bf16[2,2,80,512]{3,2,1,0:T(8,128)(2,1)S(1)}, u32[]{:S(2)}, u32[]{:S(2)}) collective-permute-start(bf16[2,2,80,512]{3,2,1,0:T(8,128)(2,1)S(1)} %dynamic-slice_bitcast_fusion.11), channel_id=1, source_target_pairs={{0,16},{1,17},{2,18},{3,19},{4,20},{5,21},{6,22},{7,23},{8,24},{9,... | collective-permute-start | bytes 983048 | tf_op jit(solution)/shard_map/ppermute | solution.py:804
  409.0 10.0 %collective-permute-start.30 = (bf16[2,2,80,512]{3,2,1,0:T(8,128)(2,1)S(1)}, bf16[2,2,80,512]{3,2,1,0:T(8,128)(2,1)S(1)}, u32[]{:S(2)}, u32[]{:S(2)}) collective-permute-start(bf16[2,2,80,512]{3,2,1,0:T(8,128)(2,1)S(1)} %dynamic-slice_bitcast_fusion.12), channel_id=1, source_target_pairs={{0,8},{1,9},{2,10},{3,11},{4,12},{5,13},{6,14},{7,15},{8,0},{9,1},... | collective-permute-start | bytes 983048 | tf_op jit(solution)/shard_map/ppermute | solution.py:804
  416.6 15.6 %copy-start.16 = (bf16[4,8,16,512]{3,2,1,0:T(8,128)(2,1)S(1)}, bf16[4,8,16,512]{3,2,1,0:T(8,128)(2,1)}, u32[]{:S(2)}) copy-start(bf16[4,8,16,512]{3,2,1,0:T(8,128)(2,1)} %copy-done.15) | copy-start | bytes 1572868
  416.7 15.6 %copy-start.18 = (bf16[32,48,512]{2,1,0:T(8,128)(2,1)S(1)}, bf16[32,48,512]{2,1,0:T(8,128)(2,1)}, u32[]{:S(2)}) copy-start(bf16[32,48,512]{2,1,0:T(8,128)(2,1)} %get-tuple-element.119) | copy-start | bytes 4718596
  416.7 7.0 %collective-permute-start.34 = (bf16[2,80,512]{2,1,0:T(8,128)(2,1)S(1)}, bf16[2,80,512]{2,1,0:T(8,128)(2,1)S(1)}, u32[]{:S(2)}, u32[]{:S(2)}) collective-permute-start(bf16[2,80,512]{2,1,0:T(8,128)(2,1)S(1)} %dynamic-slice_bitcast_fusion.17), channel_id=1, source_target_pairs={{0,2},{1,3},{2,0},{3,1},{4,6},{5,7},{6,4},{7,5},{8,10},{9,11},{10,... | collective-permute-start | bytes 491528 | tf_op jit(solution)/shard_map/ppermute | solution.py:804
  419.1 7.8 %collective-permute-start.31 = (bf16[2,80,512]{2,1,0:T(8,128)(2,1)S(1)}, bf16[2,80,512]{2,1,0:T(8,128)(2,1)S(1)}, u32[]{:S(2)}, u32[]{:S(2)}) collective-permute-start(bf16[2,80,512]{2,1,0:T(8,128)(2,1)S(1)} %dynamic-slice_bitcast_fusion.18), channel_id=1, source_target_pairs={{0,2},{1,3},{2,0},{3,1},{4,6},{5,7},{6,4},{7,5},{8,10},{9,11},{10,... | collective-permute-start | bytes 491528 | tf_op jit(solution)/shard_map/ppermute | solution.py:804
  423.7 8.7 %copy-start.11 = (bf16[32,64,512]{2,1,0:T(8,128)(2,1)S(1)}, bf16[32,64,512]{2,1,0:T(8,128)(2,1)}, u32[]{:S(2)}) copy-start(bf16[32,64,512]{2,1,0:T(8,128)(2,1)} %get-tuple-element.120) | copy-start | bytes 6291460
  423.8 8.5 %collective-permute-start.35 = (bf16[80,512]{1,0:T(8,128)(2,1)S(1)}, bf16[80,512]{1,0:T(8,128)(2,1)S(1)}, u32[]{:S(2)}, u32[]{:S(2)}) collective-permute-start(bf16[80,512]{1,0:T(8,128)(2,1)S(1)} %dynamic-slice_bitcast_fusion.21), channel_id=1, source_target_pairs={{0,4},{1,5},{2,6},{3,7},{4,0},{5,1},{6,2},{7,3},{8,12},{9,13},{10,... | collective-permute-start | bytes 245768 | tf_op jit(solution)/shard_map/ppermute | solution.py:804
  426.9 5.5 %copy-start.10 = (bf16[32,64,512]{2,1,0:T(8,128)(2,1)S(1)}, bf16[32,64,512]{2,1,0:T(8,128)(2,1)}, u32[]{:S(2)}) copy-start(bf16[32,64,512]{2,1,0:T(8,128)(2,1)} %get-tuple-element.118) | copy-start | bytes 6291460
  426.9 6.2 %collective-permute-start.32 = (bf16[80,512]{1,0:T(8,128)(2,1)S(1)}, bf16[80,512]{1,0:T(8,128)(2,1)S(1)}, u32[]{:S(2)}, u32[]{:S(2)}) collective-permute-start(bf16[80,512]{1,0:T(8,128)(2,1)S(1)} %dynamic-slice_bitcast_fusion.22), channel_id=1, source_target_pairs={{0,4},{1,5},{2,6},{3,7},{4,0},{5,1},{6,2},{7,3},{8,12},{9,13},{10,... | collective-permute-start | bytes 245768 | tf_op jit(solution)/shard_map/ppermute | solution.py:804
  433.0 13.6 %collective-permute-start.26 = (bf16[2,2,2,96,512]{4,3,2,1,0:T(8,128)(2,1)S(1)}, bf16[2,2,2,96,512]{4,3,2,1,0:T(8,128)(2,1)S(1)}, u32[]{:S(2)}, u32[]{:S(2)}) collective-permute-start(bf16[2,2,2,96,512]{4,3,2,1,0:T(8,128)(2,1)S(1)} %dynamic-slice_bitcast_fusion.3), channel_id=1, source_target_pairs={{0,8},{1,9},{2,10},{3,11},{4,12},{5,13},{6,14},{7,15},{8,0},{9,1},... | collective-permute-start | bytes 2359304 | tf_op jit(solution)/shard_map/ppermute | solution.py:804
  433.2 20.5 %collective-permute-start.22 = (bf16[2,2,2,96,512]{4,3,2,1,0:T(8,128)(2,1)S(1)}, bf16[2,2,2,96,512]{4,3,2,1,0:T(8,128)(2,1)S(1)}, u32[]{:S(2)}, u32[]{:S(2)}) collective-permute-start(bf16[2,2,2,96,512]{4,3,2,1,0:T(8,128)(2,1)S(1)} %dynamic-slice_bitcast_fusion.4), channel_id=1, source_target_pairs={{0,16},{1,17},{2,18},{3,19},{4,20},{5,21},{6,22},{7,23},{8,24},{9,... | collective-permute-start | bytes 2359304 | tf_op jit(solution)/shard_map/ppermute | solution.py:804
  446.8 13.6 %collective-permute-start.27 = (bf16[2,2,96,512]{3,2,1,0:T(8,128)(2,1)S(1)}, bf16[2,2,96,512]{3,2,1,0:T(8,128)(2,1)S(1)}, u32[]{:S(2)}, u32[]{:S(2)}) collective-permute-start(bf16[2,2,96,512]{3,2,1,0:T(8,128)(2,1)S(1)} %dynamic-slice_bitcast_fusion.9), channel_id=1, source_target_pairs={{0,16},{1,17},{2,18},{3,19},{4,20},{5,21},{6,22},{7,23},{8,24},{9,... | collective-permute-start | bytes 1179656 | tf_op jit(solution)/shard_map/ppermute | solution.py:804
  453.8 7.8 %collective-permute-start.23 = (bf16[2,2,96,512]{3,2,1,0:T(8,128)(2,1)S(1)}, bf16[2,2,96,512]{3,2,1,0:T(8,128)(2,1)S(1)}, u32[]{:S(2)}, u32[]{:S(2)}) collective-permute-start(bf16[2,2,96,512]{3,2,1,0:T(8,128)(2,1)S(1)} %dynamic-slice_bitcast_fusion.10), channel_id=1, source_target_pairs={{0,8},{1,9},{2,10},{3,11},{4,12},{5,13},{6,14},{7,15},{8,0},{9,1},... | collective-permute-start | bytes 1179656 | tf_op jit(solution)/shard_map/ppermute | solution.py:804
  460.5 8.4 %collective-permute-start.28 = (bf16[2,96,512]{2,1,0:T(8,128)(2,1)S(1)}, bf16[2,96,512]{2,1,0:T(8,128)(2,1)S(1)}, u32[]{:S(2)}, u32[]{:S(2)}) collective-permute-start(bf16[2,96,512]{2,1,0:T(8,128)(2,1)S(1)} %dynamic-slice_bitcast_fusion.15), channel_id=1, source_target_pairs={{0,2},{1,3},{2,0},{3,1},{4,6},{5,7},{6,4},{7,5},{8,10},{9,11},{10,... | collective-permute-start | bytes 589832 | tf_op jit(solution)/shard_map/ppermute | solution.py:804
  461.7 9.3 %collective-permute-start.24 = (bf16[2,96,512]{2,1,0:T(8,128)(2,1)S(1)}, bf16[2,96,512]{2,1,0:T(8,128)(2,1)S(1)}, u32[]{:S(2)}, u32[]{:S(2)}) collective-permute-start(bf16[2,96,512]{2,1,0:T(8,128)(2,1)S(1)} %dynamic-slice_bitcast_fusion.16), channel_id=1, source_target_pairs={{0,2},{1,3},{2,0},{3,1},{4,6},{5,7},{6,4},{7,5},{8,10},{9,11},{10,... | collective-permute-start | bytes 589832 | tf_op jit(solution)/shard_map/ppermute | solution.py:804
  468.9 6.4 %collective-permute-start.29 = (bf16[96,512]{1,0:T(8,128)(2,1)S(1)}, bf16[96,512]{1,0:T(8,128)(2,1)S(1)}, u32[]{:S(2)}, u32[]{:S(2)}) collective-permute-start(bf16[96,512]{1,0:T(8,128)(2,1)S(1)} %dynamic-slice_bitcast_fusion.19), channel_id=1, source_target_pairs={{0,4},{1,5},{2,6},{3,7},{4,0},{5,1},{6,2},{7,3},{8,12},{9,13},{10,... | collective-permute-start | bytes 294920 | tf_op jit(solution)/shard_map/ppermute | solution.py:804
  471.0 6.5 %collective-permute-start.25 = (bf16[96,512]{1,0:T(8,128)(2,1)S(1)}, bf16[96,512]{1,0:T(8,128)(2,1)S(1)}, u32[]{:S(2)}, u32[]{:S(2)}) collective-permute-start(bf16[96,512]{1,0:T(8,128)(2,1)S(1)} %dynamic-slice_bitcast_fusion.20), channel_id=1, source_target_pairs={{0,4},{1,5},{2,6},{3,7},{4,0},{5,1},{6,2},{7,3},{8,12},{9,13},{10,... | collective-permute-start | bytes 294920 | tf_op jit(solution)/shard_map/ppermute | solution.py:804
  (17 other events, 21.6 us)
Sparse Core Ops, SparseCore 0:
  11.6 89.3 all-gather.4
  118.6 72.1 all-gather.6
  228.8 120.6 reduce-scatter.1
